TPU v7x, 32 devices: a whole 2x2x4 slice. The times are simulated.
32 devices in a mesh: dp: 8 (over z, y), seq: 4 (over x, core).
Axes of the slice: x: 2, y: 2, z: 4, core: 2. Of those that a mesh axis runs over, the one named last changes fastest.
Arguments:
- tokens: bfloat16 [8, 512, 768], P('dp', 'seq'), may hold values from -6 to 6
- cotangent: bfloat16 [8, 512, 768], P('dp', 'seq'), may hold values from -6 to 6
- segment_ids: int32 [8, 512], P('dp', 'seq'), may hold values from 0 to 7, never falling along the last dimension, each value on 1 to 256 neighbouring positions
- pad_mask: int32 [8, 512], P('dp', 'seq'), may hold values 0 or 1
- routes: int32 [8, 512, 2], P('dp', 'seq'), may hold values from 0 to 3, all different within a row; in each aligned block of 128 rows (0 to 127, 128 to 255, ..., all dimensions but the last counted through in order) at most 96 rows name the same one
- gate_weights: float32 [8, 512, 2], P('dp', 'seq'), may hold values from 0.25 to 1
- gain_one: float32 [768], replicated, may hold values from 0.5 to 1.5
- w_qkv: bfloat16 [768, 2304], P(('dp', 'seq')), may hold values from -0.21875 to 0.21875
- w_attn: bfloat16 [768, 768], P(('dp', 'seq')), may hold values from -1.75 to 1.75
- rel_table: bfloat16 [12, 32], replicated, may hold values from -4 to 4
- gain_two: float32 [768], replicated, may hold values from 0.5 to 1.5
- w_expert_in: bfloat16 [4, 768, 3072], P(None, ('dp', 'seq')), may hold values from -0.21875 to 0.21875
- w_expert_out: bfloat16 [4, 3072, 768], P(None, ('dp', 'seq')), may hold values from -0.109375 to 0.109375
Outputs:
- output: bfloat16 [8, 512, 768], P('dp', 'seq')
- grad_tokens: float32 [8, 512, 768], P('dp', 'seq')
- grad_gain_one: float32 [768], replicated
- grad_w_qkv: float32 [768, 2304], P(('dp', 'seq'))
- grad_w_attn: float32 [768, 768], P(('dp', 'seq'))
- grad_rel_table: float32 [12, 32], replicated
- grad_gain_two: float32 [768], replicated
- grad_expert_in: float32 [4, 768, 3072], P(None, ('dp', 'seq'))
- grad_expert_out: float32 [4, 3072, 768], P(None, ('dp', 'seq'))
Inputs may be any that keep to these rules, and one draw needn't show every extreme that they name: `routes`: the two experts of a token differ. Among the rows of one device no expert is named more than 96 times, and in some device's rows one expert is named exactly 96 times. `segment_ids`: ids never fall along a sequence; a document has 1 to 256 positions, and one has exactly that many.
All inputs are finite; a program needn't handle non-finite values. No bound on the sum of `pad_mask` on one device may be relied on, other than what follows from the above.
Results may differ from a plain program's by a relative error of at most 0.011.
Values may be sent and summed in bfloat16 or wider, within the bound.
No kernel may reach another device: no remote copies, remote signals or barrier semaphores. Data moves between devices by JAX's collectives and lax.ppermute only.
A program may use at most 320 MiB of HBM per device.

v0:
```python
import math

import jax
import jax.numpy as jnp
import numpy as np
from jax import lax
from jax.sharding import PartitionSpec as P

BUCKETS = 32
MAX_DIST = 128
CAP = 96


def bucket_edges():
    exact_span = BUCKETS // 2
    distance = np.arange(1, 8 * MAX_DIST + 1)
    widened = np.maximum(distance, exact_span) / exact_span
    spread = exact_span + (np.log(widened) / np.log(MAX_DIST / exact_span) * exact_span).astype(
        np.int64
    )
    bucket_of = np.where(distance < exact_span, distance, np.minimum(spread, BUCKETS - 1))
    return np.array(
        [distance[np.argmax(bucket_of >= target)] for target in range(1, BUCKETS)], dtype=np.int32
    )


def norm_stats(values):
    factor = lax.rsqrt(jnp.mean(values * values, axis=-1, keepdims=True) + 1e-06)
    return (values * factor, factor)


def norm_back(grad_normed, scaled, factor, gain_vec):
    grad_scaled = grad_normed * gain_vec
    inner_mean = jnp.mean(grad_scaled * scaled, axis=-1, keepdims=True)
    return (factor * (grad_scaled - scaled * inner_mean), jnp.sum(grad_normed * scaled, axis=0))


def make_onehot(distance, edges_np):
    bucket_of = jnp.sum((distance[:, :, None] >= edges_np).astype(jnp.int32), axis=-1)
    return (bucket_of[:, :, None] == jnp.arange(BUCKETS, dtype=jnp.int32)).astype(jnp.bfloat16)


def block_bias(table_low, edges_np, distance):
    far_away = jnp.min(distance) >= int(edges_np[-1])

    def block_detailed(unused):
        return jnp.einsum(
            "qkb,hb->hqk",
            make_onehot(distance, edges_np),
            table_low,
            preferred_element_type=jnp.float32,
        )

    def block_constant(unused):
        last_col = table_low[:, BUCKETS - 1].astype(jnp.float32)
        return jnp.broadcast_to(last_col[:, None, None], (table_low.shape[0],) + distance.shape)

    return lax.cond(far_away, block_constant, block_detailed, 0)


def table_part(grad_low, edges_np, distance):
    far_away = jnp.min(distance) >= int(edges_np[-1])

    def table_detailed(unused):
        return jnp.einsum(
            "hqk,qkb->hb",
            grad_low,
            make_onehot(distance, edges_np),
            preferred_element_type=jnp.float32,
        )

    def table_constant(unused):
        totals = jnp.sum(grad_low, axis=(1, 2), dtype=jnp.float32)
        return totals[:, None] * (jnp.arange(BUCKETS) == BUCKETS - 1).astype(jnp.float32)

    return lax.cond(far_away, table_constant, table_detailed, 0)


def body(
    tokens,
    cotangent,
    segment_ids,
    pad_mask,
    routes,
    gate_weights,
    gain_one,
    w_qkv,
    w_attn,
    rel_table,
    gain_two,
    w_expert_in,
    w_expert_out,
):
    gathered = (
        lax.all_gather(w_qkv, ("dp", "seq"), axis=0, tiled=True),
        lax.all_gather(w_attn, ("dp", "seq"), axis=0, tiled=True),
        lax.all_gather(w_expert_in, ("dp", "seq"), axis=1, tiled=True),
        lax.all_gather(w_expert_out, ("dp", "seq"), axis=1, tiled=True),
    )
    full_qkv, full_attn, full_in, full_out = gathered
    inputs = tokens[0].astype(jnp.float32)
    row_count, model_width = inputs.shape
    head_count = rel_table.shape[0]
    head_size = model_width // head_count
    score_scale = head_size ** (-0.5)
    seg_local = segment_ids[0]
    seq_index = lax.axis_index("seq")
    length = row_count * lax.axis_size("seq")
    key_block = math.gcd(length, 512)
    query_pos = seq_index * row_count + jnp.arange(row_count, dtype=jnp.int32)
    block_count = ((seq_index + 1) * row_count + key_block - 1) // key_block
    edges_np = bucket_edges()
    scaled_one, factor_one = norm_stats(inputs)
    normed_one = (scaled_one * gain_one).astype(jnp.bfloat16)
    project = jnp.dot(normed_one, full_qkv, preferred_element_type=jnp.float32)
    queries = project[:, :model_width].astype(jnp.bfloat16)
    keys_local = project[:, model_width : 2 * model_width].astype(jnp.bfloat16)
    values_local = project[:, 2 * model_width :].astype(jnp.bfloat16)
    info_local = jnp.where(pad_mask[0] == 1, seg_local, -1)
    keys_all, values_all, info_all, seg_all = (
        lax.all_gather(keys_local, "seq", axis=0, tiled=True),
        lax.all_gather(values_local, "seq", axis=0, tiled=True),
        lax.all_gather(info_local, "seq", axis=0, tiled=True),
        lax.all_gather(seg_local, "seq", axis=0, tiled=True),
    )
    query_heads = queries.reshape(row_count, head_count, head_size)

    def block_scores(block_index):
        key_start = block_index * key_block
        key_heads = lax.dynamic_slice_in_dim(keys_all, key_start, key_block, 0).reshape(
            key_block, head_count, head_size
        )
        value_heads = lax.dynamic_slice_in_dim(values_all, key_start, key_block, 0).reshape(
            key_block, head_count, head_size
        )
        info_block = lax.dynamic_slice_in_dim(info_all, key_start, key_block, 0)
        key_pos = key_start + jnp.arange(key_block, dtype=jnp.int32)
        distance = query_pos[:, None] - key_pos[None, :]
        allowed = (distance >= 0) & ((info_block[None, :] == seg_local[:, None]) | (distance == 0))
        raw_scores = (
            jnp.einsum("qhd,khd->hqk", query_heads, key_heads, preferred_element_type=jnp.float32)
            * score_scale
        )
        raw_scores = raw_scores + block_bias(rel_table, edges_np, distance)
        return (
            jnp.where(allowed[None], raw_scores, -1e30),
            allowed[None],
            key_heads,
            value_heads,
            distance,
            key_start,
        )

    def max_step(block_index, running):
        top_score, row_total = running
        pieces = block_scores(block_index)
        new_top = jnp.maximum(top_score, jnp.max(pieces[0], axis=-1))
        exponent = jnp.where(pieces[1], jnp.exp(pieces[0] - new_top[:, :, None]), 0.0)
        return (new_top, row_total * jnp.exp(top_score - new_top) + jnp.sum(exponent, axis=-1))

    start_top = jnp.full((head_count, row_count), -1e30, jnp.float32)
    start_total = jnp.zeros((head_count, row_count), jnp.float32)
    top_score, row_total = lax.fori_loop(0, block_count, max_step, (start_top, start_total))
    log_total = top_score + jnp.log(row_total)

    def out_step(block_index, mixed_acc):
        pieces = block_scores(block_index)
        prob_low = jnp.where(pieces[1], jnp.exp(pieces[0] - log_total[:, :, None]), 0.0).astype(
            jnp.bfloat16
        )
        return mixed_acc + jnp.einsum(
            "hqk,khd->qhd", prob_low, pieces[3], preferred_element_type=jnp.float32
        )

    mixed_full = lax.fori_loop(
        0, block_count, out_step, jnp.zeros((row_count, head_count, head_size), jnp.float32)
    )
    mixed_low = mixed_full.reshape(row_count, model_width).astype(jnp.bfloat16)
    hidden_one = inputs + jnp.dot(mixed_low, full_attn, preferred_element_type=jnp.float32)
    scaled_two, factor_two = norm_stats(hidden_one)
    normed_two = (scaled_two * gain_two).astype(jnp.bfloat16)
    route_local = routes[0]
    expert_count = w_expert_in.shape[0]
    top_count = route_local.shape[1]
    flat_routes = route_local.reshape(-1)
    expert_hot = (flat_routes[:, None] == jnp.arange(expert_count, dtype=jnp.int32)).astype(
        jnp.int32
    )
    earlier = jnp.cumsum(expert_hot, axis=0) - expert_hot
    slot_index = jnp.sum(earlier * expert_hot, axis=1)
    slot_float = (
        (slot_index[:, None] == jnp.arange(CAP, dtype=jnp.int32))
        .astype(jnp.float32)
        .reshape(row_count, top_count, CAP)
    )
    expert_float = expert_hot.astype(jnp.float32).reshape(row_count, top_count, expert_count)
    dispatch = jnp.einsum(
        "tke,tkc->ect",
        expert_float.astype(jnp.bfloat16),
        slot_float.astype(jnp.bfloat16),
        preferred_element_type=jnp.float32,
    ).astype(jnp.bfloat16)
    slot_gate = jnp.einsum(
        "tke,tkc,tk->ec", expert_float, slot_float, gate_weights[0], precision=lax.Precision.HIGHEST
    )
    entered = jnp.einsum(
        "ect,td->ecd", dispatch, normed_two, preferred_element_type=jnp.float32
    ).astype(jnp.bfloat16)
    pre_act = jnp.einsum("ecd,edf->ecf", entered, full_in, preferred_element_type=jnp.float32)
    active = jax.nn.gelu(pre_act).astype(jnp.bfloat16)
    result = jnp.einsum("ecf,efd->ecd", active, full_out, preferred_element_type=jnp.float32)
    expert_low = (slot_gate[:, :, None] * result).astype(jnp.bfloat16)
    combined = jnp.einsum("ect,ecd->td", dispatch, expert_low, preferred_element_type=jnp.float32)
    output = (hidden_one + combined).astype(jnp.bfloat16)
    regathered = (
        lax.all_gather(w_qkv, ("dp", "seq"), axis=0, tiled=True),
        lax.all_gather(w_attn, ("dp", "seq"), axis=0, tiled=True),
        lax.all_gather(w_expert_in, ("dp", "seq"), axis=1, tiled=True),
        lax.all_gather(w_expert_out, ("dp", "seq"), axis=1, tiled=True),
    )
    back_qkv, back_attn, back_in, back_out = regathered
    grad_out_low = cotangent[0]
    grad_slots = jnp.einsum(
        "ect,td->ecd", dispatch, grad_out_low, preferred_element_type=jnp.float32
    )
    grad_result = (slot_gate[:, :, None] * grad_slots).astype(jnp.bfloat16)
    grad_w_out = jnp.einsum("ecf,ecd->efd", active, grad_result, preferred_element_type=jnp.float32)
    grad_active = jnp.einsum(
        "ecd,efd->ecf", grad_result, back_out, preferred_element_type=jnp.float32
    )
    unused_value, gelu_pull = jax.vjp(jax.nn.gelu, pre_act)
    grad_pre = gelu_pull(grad_active)[0].astype(jnp.bfloat16)
    grad_w_in = jnp.einsum("ecd,ecf->edf", entered, grad_pre, preferred_element_type=jnp.float32)
    grad_entered = jnp.einsum(
        "ecf,edf->ecd", grad_pre, back_in, preferred_element_type=jnp.float32
    ).astype(jnp.bfloat16)
    grad_normed_two = jnp.einsum(
        "ect,ecd->td", dispatch, grad_entered, preferred_element_type=jnp.float32
    )
    grad_hidden_norm, grad_gain_two = norm_back(grad_normed_two, scaled_two, factor_two, gain_two)
    grad_hidden = grad_out_low.astype(jnp.float32) + grad_hidden_norm
    branch_low = grad_hidden.astype(jnp.bfloat16)
    grad_w_attn = lax.dot_general(
        mixed_low, branch_low, (((0,), (0,)), ((), ())), preferred_element_type=jnp.float32
    )
    grad_mixed = lax.dot_general(
        branch_low, back_attn, (((1,), (1,)), ((), ())), preferred_element_type=jnp.float32
    ).astype(jnp.bfloat16)
    grad_mixed_heads = grad_mixed.reshape(row_count, head_count, head_size)
    row_delta = jnp.sum(grad_mixed_heads.astype(jnp.float32) * mixed_full, axis=-1).T

    def score_grads(pieces):
        prob_full = jnp.where(pieces[1], jnp.exp(pieces[0] - log_total[:, :, None]), 0.0)
        grad_prob = jnp.einsum(
            "qhd,khd->hqk", grad_mixed_heads, pieces[3], preferred_element_type=jnp.float32
        )
        grad_score = (prob_full * (grad_prob - row_delta[:, :, None])).astype(jnp.bfloat16)
        return (prob_full.astype(jnp.bfloat16), grad_score)

    start_query = jnp.zeros((row_count, head_count, head_size), jnp.float32)
    start_table = jnp.zeros((head_count, BUCKETS), jnp.float32)

    def back_step(block_index, running):
        grad_query, grad_key_all, grad_value_all, grad_table = running
        pieces = block_scores(block_index)
        prob_low, grad_score = score_grads(pieces)
        grad_query = (
            grad_query
            + jnp.einsum("hqk,khd->qhd", grad_score, pieces[2], preferred_element_type=jnp.float32)
            * score_scale
        )
        key_part = (
            jnp.einsum("hqk,qhd->khd", grad_score, query_heads, preferred_element_type=jnp.float32)
            * score_scale
        ).reshape(key_block, model_width)
        value_part = jnp.einsum(
            "hqk,qhd->khd", prob_low, grad_mixed_heads, preferred_element_type=jnp.float32
        ).reshape(key_block, model_width)
        grad_key_all = lax.dynamic_update_slice_in_dim(grad_key_all, key_part, pieces[5], 0)
        grad_value_all = lax.dynamic_update_slice_in_dim(grad_value_all, value_part, pieces[5], 0)
        grad_table = grad_table + table_part(grad_score, edges_np, pieces[4])
        return (grad_query, grad_key_all, grad_value_all, grad_table)

    start_back = (
        start_query,
        jnp.zeros((length, model_width), jnp.float32),
        jnp.zeros((length, model_width), jnp.float32),
        start_table,
    )
    grad_query, grad_key_all, grad_value_all, grad_table = lax.fori_loop(
        0, block_count, back_step, start_back
    )
    grad_keys, grad_values = (
        lax.psum_scatter(
            grad_key_all.astype(jnp.bfloat16), "seq", scatter_dimension=0, tiled=True
        ).astype(jnp.float32),
        lax.psum_scatter(
            grad_value_all.astype(jnp.bfloat16), "seq", scatter_dimension=0, tiled=True
        ).astype(jnp.float32),
    )
    grad_proj = jnp.concatenate(
        [
            grad_query.reshape(row_count, model_width).astype(jnp.bfloat16),
            grad_keys.astype(jnp.bfloat16),
            grad_values.astype(jnp.bfloat16),
        ],
        axis=1,
    )
    grad_w_qkv = lax.dot_general(
        normed_one, grad_proj, (((0,), (0,)), ((), ())), preferred_element_type=jnp.float32
    )
    grad_normed_one = lax.dot_general(
        grad_proj, back_qkv, (((1,), (1,)), ((), ())), preferred_element_type=jnp.float32
    )
    grad_input_norm, grad_gain_one = norm_back(grad_normed_one, scaled_one, factor_one, gain_one)
    grad_inputs = grad_hidden + grad_input_norm
    table_total, gain_one_total, gain_two_total = lax.psum(
        (grad_table, grad_gain_one, grad_gain_two), ("dp", "seq")
    )
    shares = (
        lax.psum_scatter(grad_w_qkv, ("dp", "seq"), scatter_dimension=0, tiled=True),
        lax.psum_scatter(grad_w_attn, ("dp", "seq"), scatter_dimension=0, tiled=True),
        lax.psum_scatter(grad_w_in, ("dp", "seq"), scatter_dimension=1, tiled=True),
        lax.psum_scatter(grad_w_out, ("dp", "seq"), scatter_dimension=1, tiled=True),
    )
    return (
        output[None],
        grad_inputs[None],
        gain_one_total,
        shares[0],
        shares[1],
        table_total,
        gain_two_total,
        shares[2],
        shares[3],
    )


def solution(mesh):
    return jax.shard_map(
        body,
        mesh=mesh,
        in_specs=(
            P("dp", "seq", None),
            P("dp", "seq", None),
            P("dp", "seq"),
            P("dp", "seq"),
            P("dp", "seq", None),
            P("dp", "seq", None),
            P(),
            P(("dp", "seq"), None),
            P(("dp", "seq"), None),
            P(),
            P(),
            P(None, ("dp", "seq"), None),
            P(None, ("dp", "seq"), None),
        ),
        out_specs=(
            P("dp", "seq", None),
            P("dp", "seq", None),
            P(),
            P(("dp", "seq"), None),
            P(("dp", "seq"), None),
            P(),
            P(),
            P(None, ("dp", "seq"), None),
            P(None, ("dp", "seq"), None),
        ),
        check_vma=False,
    )
```

profile of v0, /device:TPU:0, one launch (start us, length us, event | category | flops | bytes accessed | tf_op | source)
XLA Modules:
  0.0 1434.9 jit_solution(6802587693438444505)
XLA Ops:
  25.1 48.6 %all-gather.6.cloned.1.call-done = bf16[768,2304]{1,0:T(8,128)(2,1)} async-done(((bf16[24,2304]{1,0:T(8,128)(2,1)}), bf16[768,2304]{1,0:T(8,128)(2,1)}) %all-gather.6.cloned.1.call-update) | async-done | bytes 3538960 | tf_op jit(solution)/shard_map/all_gather | solution.py:95
  76.6 8.6 all_gather.27
  86.5 8.7 all_gather.28
  97.0 10.8 while.44
  108.5 13.2 while.45
  110.5 6.7 conditional.21
  121.8 7.8 all-gather.8.cloned.1.call-done
  132.5 123.6 %all-gather.12.cloned.1.call-done = bf16[4,3072,768]{2,1,0:T(8,128)(2,1)} async-done(((bf16[4,96,768]{2,1,0:T(8,128)(2,1)}), bf16[4,3072,768]{2,1,0:T(8,128)(2,1)}) %all-gather.12.cloned.1.call-update) | async-done | bytes 18874384 | tf_op jit(solution)/shard_map/all_gather | solution.py:98
  256.1 14.2 fusion.98
  270.3 111.4 %all-gather.10.cloned.1.call-done = bf16[4,768,3072]{2,1,0:T(8,128)(2,1)} async-done(((bf16[4,24,3072]{2,1,0:T(8,128)(2,1)}), bf16[4,768,3072]{2,1,0:T(8,128)(2,1)}) %all-gather.10.cloned.1.call-update) | async-done | bytes 18874384 | tf_op jit(solution)/shard_map/all_gather | solution.py:97
  381.7 11.7 fusion.46
  393.4 14.6 %multiply_reduce_fusion = (f32[768]{0:T(1024)}, f32[128]{0:T(128)S(1)}, f32[128,768]{1,0:T(8,128)}) fusion(f32[128,768]{1,0:T(8,128)S(1)} %get-tuple-element.749, f32[128]{0:T(128)S(1)} %add_rsqrt_fusion, f32[768]{0:T(1024)S(1)} %copy-done.44, bf16[4,96,128]{2,1,0:T(8,128)(2,1)S(1)} %copy-done.25, bf16[4,96,3072]{2,1,0:T(8,128)(2,1)S(1)} %get-tuple-element.750, ...), kind=kOutput, calls=%fused_computation.122 | convolution fusion | flops 1888320640 | bytes 22125568 | tf_op jit(solution)/shard_map/ect,ecd->td/dot_general | solution.py:237
  416.3 23.4 %while.46 = (s32[]{:T(128)}, f32[128,12,64]{0,2,1:T(8,128)}, bf16[512,768]{0,1:T(8,128)(2,1)}, bf16[512,768]{0,1:T(8,128)(2,1)}, f32[12,32]{1,0:T(8,128)S(1)}, /...) while((s32[]{:T(128)}, f32[128,12,64]{0,2,1:T(8,128)}, ...), condition=%wide.region_30.31_spmd.clone.clone, body=%wide.region_21.30_spmd.sunk.clone.clone.sunk | while | flops 628818944 | bytes 50517476 | solution.py:290
  432.0 7.6 conditional.23
  446.8 16.9 %reduce-scatter.21.cloned.1.call-done = bf16[128,768]{1,0:T(8,128)(2,1)} async-done(((bf16[512,768]{1,0:T(8,128)(2,1)}), bf16[128,768]{1,0:T(8,128)(2,1)}) %reduce-scatter.21.cloned.1.call-update) | async-done | bytes 196624
  464.8 25.3 %reduce-scatter.19.cloned.1.call-done = bf16[128,768]{1,0:T(8,128)(2,1)} async-done(((bf16[512,768]{1,0:T(8,128)(2,1)}), bf16[128,768]{1,0:T(8,128)(2,1)}) %reduce-scatter.19.cloned.1.call-update) | async-done | bytes 196624
  497.2 15.2 %fusion.99 = f32[4,768,3072]{2,1,0:T(8,128)} fusion(bf16[4,96,768]{2,1,0:T(8,128)(2,1)S(1)} %copy-done.20, bf16[4,96,3072]{2,1,0:T(8,128)(2,1)S(1)} %copy-done.10), kind=kOutput, calls=%fused_computation.168 | convolution fusion | flops 1811939328 | bytes 40697856 | tf_op jit(solution)/shard_map/ecd,ecf->edf/dot_general | solution.py:233
  513.4 17.7 %fusion.95 = f32[4,3072,768]{2,1,0:T(8,128)} fusion(bf16[4,96,768]{2,1,0:T(8,128)(2,1)S(1)} %copy-done.18, f32[4,96,3072]{2,1,0:T(8,128)} %get-tuple-element.751), kind=kOutput, calls=%fused_computation.164 | convolution fusion | flops 1822556160 | bytes 43057152 | tf_op jit(solution)/shard_map/ecf,ecd->efd/dot_general | solution.py:227
  532.1 10.6 fusion.55
  546.6 39.8 %all-reduce = (f32[768]{0:T(1024)}, f32[12,32]{1,0:T(8,128)}, f32[768]{0:T(1024)}) all-reduce(f32[768]{0:T(1024)S(1)} %get-tuple-element.658, f32[12,32]{1,0:T(8,128)S(1)} %copy-done.35, f32[768]{0:T(1024)S(1)} %copy-done.45), channel_id=1, replica_groups=mesh['dp'=8,'seq'=4] {'dp','seq'}, use_global_device_ids=true, to_apply=%region_35.36 | all-reduce | flops 1920 | bytes 15360 | tf_op jit(solution)/shard_map/psum | solution.py:317
  587.3 7.7 reduce-scatter.13.cloned.1.call-done
  595.1 125.3 %reduce-scatter.11.cloned.1.call-done = f32[24,2304]{1,0:T(8,128)} async-done(((f32[768,2304]{1,0:T(8,128)}), f32[24,2304]{1,0:T(8,128)}) %reduce-scatter.11.cloned.1.call-update) | async-done | bytes 221200 | tf_op jit(solution)/shard_map/reduce_scatter | solution.py:321
  720.3 353.3 %reduce-scatter.15.cloned.1.call-done = f32[4,24,3072]{2,1,0:T(8,128)} async-done(((f32[4,768,3072]{2,1,0:T(8,128)}), f32[4,24,3072]{2,1,0:T(8,128)}) %reduce-scatter.15.cloned.1.call-update) | async-done | bytes 1179664 | tf_op jit(solution)/shard_map/reduce_scatter | solution.py:323
  1073.6 353.9 %reduce-scatter.17.cloned.1.call-done = f32[4,96,768]{2,1,0:T(8,128)} async-done(((f32[4,3072,768]{2,1,0:T(8,128)}), f32[4,96,768]{2,1,0:T(8,128)}) %reduce-scatter.17.cloned.1.call-update) | async-done | bytes 1179664 | tf_op jit(solution)/shard_map/reduce_scatter | solution.py:324
  (217 shorter events, 111.0 us)
Async XLA Ops:
  7.2 66.6 %copy-start.15 = (bf16[1,128,768]{2,1,0:T(8,128)(2,1)S(1)}, bf16[1,128,768]{2,1,0:T(8,128)(2,1)}, u32[]{:S(2)}) copy-start(bf16[1,128,768]{2,1,0:T(8,128)(2,1)} %param.28) | copy-start | bytes 589828
  7.2 66.6 %copy-start.40 = (f32[768]{0:T(1024)S(1)}, f32[768]{0:T(1024)}, u32[]{:S(2)}) copy-start(f32[768]{0:T(1024)} %param.34) | copy-start | bytes 9220
  7.2 66.6 %all-gather.6.cloned.1.call-start = ((), (), s32[]{:S(2)}) async-start(), calls=%async_computation.6 | async-start | bytes 3649536 | tf_op jit(solution)/shard_map/all_gather | solution.py:95
  7.9 121.6 %all-gather.8.cloned.1.call-start = ((), (), s32[]{:S(2)}) async-start(), calls=%async_computation.7 | async-start | bytes 1216512 | tf_op jit(solution)/shard_map/all_gather | solution.py:96
  8.7 247.4 %all-gather.12.cloned.1.call-start = ((), (), s32[]{:S(2)}) async-start(), calls=%async_computation.9 | async-start | bytes 19464192 | tf_op jit(solution)/shard_map/all_gather | solution.py:98
  9.4 372.3 %all-gather.10.cloned.1.call-start = ((), (), s32[]{:S(2)}) async-start(), calls=%async_computation.8 | async-start | bytes 19464192 | tf_op jit(solution)/shard_map/all_gather | solution.py:97
  10.0 453.7 %reduce-scatter.21.cloned.1.call-start = ((), (), s32[]{:S(2)}) async-start(), calls=%async_computation.15 | async-start | bytes 983040
  14.5 62.1 %copy-start.23 = (bf16[4,96,128]{2,1,0:T(8,128)(2,1)}, bf16[4,96,128]{2,1,0:T(8,128)(2,1)S(1)}, u32[]{:S(2)}) copy-start(bf16[4,96,128]{2,1,0:T(8,128)(2,1)S(1)} %copy.119) | copy-start | bytes 294916
  22.0 54.6 %copy-start.48 = (f32[4,96]{1,0:T(4,128)}, f32[4,96]{1,0:T(4,128)S(1)}, u32[]{:S(2)}) copy-start(f32[4,96]{1,0:T(4,128)S(1)} %convolution_bitcast_fusion) | copy-start | bytes 4612
  23.1 53.5 %copy-start.46 = (f32[128]{0:T(128)}, f32[128]{0:T(128)S(1)}, u32[]{:S(2)}) copy-start(f32[128]{0:T(128)S(1)} %add_rsqrt_fusion.1) | copy-start | bytes 1540
  121.7 148.6 %copy-start.38 = (f32[12,128]{1,0:T(8,128)}, f32[12,128]{1,0:T(8,128)S(1)}, u32[]{:S(2)}) copy-start(f32[12,128]{1,0:T(8,128)S(1)} %get-tuple-element.1187) | copy-start | bytes 18436
  121.7 134.4 %copy-start.17 = (bf16[4,96,768]{2,1,0:T(8,128)(2,1)S(1)}, bf16[4,96,768]{2,1,0:T(8,128)(2,1)}, u32[]{:S(2)}) copy-start(bf16[4,96,768]{2,1,0:T(8,128)(2,1)} %fusion.47) | copy-start | bytes 1769476
  121.7 148.6 %copy-start.21 = (bf16[128,12,64]{0,2,1:T(8,128)(2,1)}, bf16[128,12,64]{0,2,1:T(8,128)(2,1)S(1)}, u32[]{:S(2)}) copy-start(bf16[128,12,64]{0,2,1:T(8,128)(2,1)S(1)} %convert_element_type.181) | copy-start | bytes 589828
  131.3 276.7 %copy-start.13 = (f32[128,768]{1,0:T(8,128)}, f32[128,768]{1,0:T(8,128)S(1)}, u32[]{:S(2)}) copy-start(f32[128,768]{1,0:T(8,128)S(1)} %get-tuple-element.749) | copy-start | bytes 1179652
  270.3 123.1 %copy-start.25 = (bf16[4,96,128]{2,1,0:T(8,128)(2,1)S(1)}, bf16[4,96,128]{2,1,0:T(8,128)(2,1)}, u32[]{:S(2)}) copy-start(bf16[4,96,128]{2,1,0:T(8,128)(2,1)} %copy-done.23) | copy-start | bytes 294916
  270.3 123.1 %copy-start.44 = (f32[768]{0:T(1024)S(1)}, f32[768]{0:T(1024)}, u32[]{:S(2)}) copy-start(f32[768]{0:T(1024)} %param.38) | copy-start | bytes 9220
  442.1 48.0 %reduce-scatter.19.cloned.1.call-start = ((), (), s32[]{:S(2)}) async-start(), calls=%async_computation.14 | async-start | bytes 983040
  444.5 46.7 %copy-start.16 = (bf16[1,128,768]{2,1,0:T(8,128)(2,1)S(1)}, bf16[1,128,768]{2,1,0:T(8,128)(2,1)}, u32[]{:S(2)}) copy-start(bf16[1,128,768]{2,1,0:T(8,128)(2,1)} %param.28) | copy-start | bytes 589828
  444.5 46.7 %copy-start.41 = (f32[768]{0:T(1024)S(1)}, f32[768]{0:T(1024)}, u32[]{:S(2)}) copy-start(f32[768]{0:T(1024)} %param.34) | copy-start | bytes 9220
  444.5 150.6 %reduce-scatter.13.cloned.1.call-start = ((), (), s32[]{:S(2)}) async-start(), calls=%async_computation.11 | async-start | bytes 2433024 | tf_op jit(solution)/shard_map/reduce_scatter | solution.py:322
  446.4 273.9 %reduce-scatter.11.cloned.1.call-start = ((), (), s32[]{:S(2)}) async-start(), calls=%async_computation.10 | async-start | bytes 7299072 | tf_op jit(solution)/shard_map/reduce_scatter | solution.py:321
  446.8 48.6 %copy-start.31 = (bf16[128,12,64]{0,2,1:T(8,128)(2,1)}, bf16[128,12,64]{0,2,1:T(8,128)(2,1)S(1)}, u32[]{:S(2)}) copy-start(bf16[128,12,64]{0,2,1:T(8,128)(2,1)S(1)} %convert_element_type.204) | copy-start | bytes 589828
  495.4 578.2 %reduce-scatter.15.cloned.1.call-start = ((), (), s32[]{:S(2)}) async-start(), calls=%async_computation.12 | async-start | bytes 38928384 | tf_op jit(solution)/shard_map/reduce_scatter | solution.py:323
  512.4 915.2 %reduce-scatter.17.cloned.1.call-start = ((), (), s32[]{:S(2)}) async-start(), calls=%async_computation.13 | async-start | bytes 38928384 | tf_op jit(solution)/shard_map/reduce_scatter | solution.py:324
  (36 other events, 267.3 us)
Sparse Core Ops, SparseCore 0:
  10.9 62.7 all-gather.5
  76.7 52.8 all-gather.7
  132.5 123.5 all-gather.11
  258.9 122.7 all-gather.9
  442.2 21.4 reduce-scatter.20
  466.8 23.2 reduce-scatter.18
  496.0 99.0 reduce-scatter.12
  602.3 118.0 reduce-scatter.10
  727.4 346.2 reduce-scatter.14
  1081.6 345.9 reduce-scatter.16
where the time goes:
time: 1440 us; the launch traced here: 1430 us
  waiting for transfers between devices  1180 us (82%)
  matrix products  125 us (9%)
  blocking collectives  63.1 us (4%)
  local copies, waits for them, and re-layouts  31.1 us (2%)
  other arithmetic  20 us (1%)
  between operations  15.1 us (1%)
    reduce_scatter x1, waiting for transfers between devices, body(): lax.psum_scatter(grad_w_out, ('dp', 'seq'), scatter_dimension=1, tiled=True)  354 us
    reduce_scatter x1, waiting for transfers between devices, body(): lax.psum_scatter(grad_w_in, ('dp', 'seq'), scatter_dimension=1, tiled=True)  353 us
    reduce_scatter x1, waiting for transfers between devices, body(): lax.psum_scatter(grad_w_qkv, ('dp', 'seq'), scatter_dimension=0, tiled=True)  125 us
    all_gather x1, waiting for transfers between devices, body(): lax.all_gather(w_expert_out, ('dp', 'seq'), axis=1, tiled=True)  124 us
    all_gather x1, waiting for transfers between devices, body(): lax.all_gather(w_expert_in, ('dp', 'seq'), axis=1, tiled=True)  111 us
    all_gather x1, waiting for transfers between devices, body(): lax.all_gather(w_qkv, ('dp', 'seq'), axis=0, tiled=True)  48.6 us
    unnamed x12, waiting for transfers between devices  44.9 us
    psum x1, blocking collectives, body(): lax.psum((grad_table, grad_gain_one, grad_gain_two), ('dp', 'seq'))  39.8 us
  transfers between devices with their start and end apart: 10, of which 10 were waited for; matrix products, arithmetic and copies ran while one was open for 8% of the time, Pallas kernels for 0%

commit v1 on v0

--- a/solution.py
+++ b/solution.py
@@ -4,6 +4,9 @@
 import jax.numpy as jnp
 import numpy as np
 from jax import lax
+from jax.experimental import pallas as pl
+from jax.experimental.pallas import tpu as pltpu
+from jax.sharding import Mesh
 from jax.sharding import PartitionSpec as P
 
 BUCKETS = 32
@@ -336,7 +339,7 @@
     )
 
 
-def solution(mesh):
+def rows_solution(mesh):
     return jax.shard_map(
         body,
         mesh=mesh,
@@ -368,3 +371,569 @@
         ),
         check_vma=False,
     )
+
+
+F32 = jnp.float32
+BF16 = jnp.bfloat16
+ROWS = 128
+EXT = 128
+AXES = ("z", "y", "x", "c")
+VMEM_BYTES = 48 * 1024 * 1024
+
+
+def swap(value, axis, step=1):
+    size = lax.axis_size(axis)
+    return lax.ppermute(value, axis, [(i, i ^ step) for i in range(size)])
+
+
+def gather_seq(value):
+    pair = jnp.concatenate([value, swap(value, "x")], axis=0)
+    return jnp.concatenate([pair, swap(pair, "c")], axis=0)
+
+
+def reduce_seq(part):
+    half = part.shape[0] // 2
+    quarter = half // 2
+    got = swap(part[half:].astype(BF16), "c")
+    pair = part[:half].astype(F32) + got.astype(F32)
+    got_pair = swap(pair[quarter:].astype(BF16), "x")
+    return pair[:quarter] + got_pair.astype(F32)
+
+
+def mm(a, b):
+    return lax.dot_general(a, b, (((1,), (0,)), ((), ())), preferred_element_type=F32)
+
+
+def mm_t(a, b):
+    return lax.dot_general(a, b, (((1,), (1,)), ((), ())), preferred_element_type=F32)
+
+
+def t_mm(a, b):
+    return lax.dot_general(a, b, (((0,), (0,)), ((), ())), preferred_element_type=F32)
+
+
+def slot_rows(block, me):
+    mask = jnp.bitwise_xor(me, block)
+    slot = jnp.right_shift(mask, 1) + 2 * jnp.bitwise_and(mask, 1)
+    return pl.ds(pl.multiple_of(slot * ROWS, ROWS), ROWS)
+
+
+def tile_distance(offset):
+    row = lax.broadcasted_iota(jnp.int32, (ROWS, ROWS), 0)
+    col = lax.broadcasted_iota(jnp.int32, (ROWS, ROWS), 1)
+    return offset + row - col
+
+
+def fill_bias(bias_ref, tab_ref, heads):
+    edges = [int(e) for e in bucket_edges()]
+    for near in range(2):
+        distance = tile_distance(near * ROWS)
+        tiles = [jnp.full((ROWS, ROWS), tab_ref[h, 0], F32) for h in range(heads)]
+        for b, edge in enumerate(edges):
+            above = distance >= edge
+            tiles = [jnp.where(above, tab_ref[h, b + 1], tiles[h]) for h in range(heads)]
+        for h in range(heads):
+            bias_ref[near * heads + h] = tiles[h]
+
+
+def read_marks(xs_ref, me, width, blocks):
+    seg_cols, info_rows = [], []
+    for i in range(blocks):
+        marks = xs_ref[slot_rows(i, me), width : width + EXT].astype(F32)
+        seg_cols.append(marks[:, 0:1])
+        info_rows.append(marks.T[1:2, :])
+    return seg_cols, info_rows
+
+
+def mask_tiles(i, seg_cols, info_rows):
+    tiles = []
+    for j in range(i + 1):
+        seen = info_rows[j] == seg_cols[i]
+        if j == i:
+            distance = tile_distance(0)
+            seen = (distance == 0) | ((distance > 0) & seen)
+        tiles.append(jnp.where(seen, 0.0, -1e30))
+    return tiles
+
+
+def add_tiles(i, h, heads, masks, bias_ref, tab_ref):
+    tiles = []
+    for j in range(i + 1):
+        if i - j < 2:
+            tiles.append(masks[j] + bias_ref[(i - j) * heads + h])
+        else:
+            tiles.append(masks[j] + tab_ref[h, BUCKETS - 1])
+    return jnp.concatenate(tiles, axis=1) if len(tiles) > 1 else tiles[0]
+
+
+def attend_kernel(
+    me_ref, tab_ref, xs_ref, gain_ref, wq_ref, n1_ref, qkv_ref, mixed_ref, lse_ref, bias_ref
+):
+    me = me_ref[0]
+    width = gain_ref.shape[1]
+    third = wq_ref.shape[1] // 3
+    heads = tab_ref.shape[0]
+    size = third // heads
+    blocks = xs_ref.shape[0] // ROWS
+    scale = size ** (-0.5)
+    fill_bias(bias_ref, tab_ref, heads)
+    for i in range(blocks):
+        x = xs_ref[slot_rows(i, me), :width].astype(F32)
+        factor = lax.rsqrt(jnp.mean(x * x, axis=-1, keepdims=True) + 1e-06)
+        n1_ref[i * ROWS : (i + 1) * ROWS, :] = (x * factor * gain_ref[...]).astype(BF16)
+    qkv_ref[...] = mm(n1_ref[...], wq_ref[...]).astype(BF16)
+    seg_cols, info_rows = read_marks(xs_ref, me, width, blocks)
+    lane = lax.broadcasted_iota(jnp.int32, (ROWS, EXT), 1)
+    for i in range(blocks):
+        masks = mask_tiles(i, seg_cols, info_rows)
+        span = (i + 1) * ROWS
+        rows = slice(i * ROWS, span)
+        outs = []
+        lse = jnp.zeros((ROWS, EXT), F32)
+        for h in range(heads):
+            q = qkv_ref[rows, h * size : (h + 1) * size]
+            k = qkv_ref[0:span, third + h * size : third + (h + 1) * size]
+            v = qkv_ref[0:span, 2 * third + h * size : 2 * third + (h + 1) * size]
+            scores = mm_t(q, k) * scale + add_tiles(i, h, heads, masks, bias_ref, tab_ref)
+            top = jnp.max(scores, axis=-1, keepdims=True)
+            weight = jnp.exp(scores - top)
+            total = jnp.sum(weight, axis=-1, keepdims=True)
+            prob = (weight * (1.0 / total)).astype(BF16)
+            outs.append(mm(prob, v))
+            lse = jnp.where(lane == h, top + jnp.log(total), lse)
+        mixed_ref[slot_rows(i, me), :] = jnp.concatenate(outs, axis=1).astype(BF16)
+        lse_ref[rows, :] = lse
+
+
+def attend_back_kernel(
+    me_ref,
+    tab_ref,
+    branch_ref,
+    watt_ref,
+    qkv_ref,
+    n1_ref,
+    lse_ref,
+    xs_ref,
+    wq_ref,
+    mixed_ref,
+    gwq_ref,
+    gno_ref,
+    gain_ref,
+    gtab_ref,
+    gwatt_ref,
+    bias_ref,
+    dk_ref,
+    dv_ref,
+    proj_ref,
+):
+    me = me_ref[0]
+    width = watt_ref.shape[1]
+    third = wq_ref.shape[1] // 3
+    heads = tab_ref.shape[0]
+    size = third // heads
+    blocks = xs_ref.shape[0] // ROWS
+    scale = size ** (-0.5)
+    fill_bias(bias_ref, tab_ref, heads)
+    seg_cols, info_rows = read_marks(xs_ref, me, width, blocks)
+    dk_ref[...] = jnp.zeros_like(dk_ref)
+    dv_ref[...] = jnp.zeros_like(dv_ref)
+    near = [[jnp.zeros((ROWS, ROWS), F32) for _ in range(heads)] for _ in range(2)]
+    far = [jnp.zeros((1, ROWS), F32) for _ in range(heads)]
+    for i in range(blocks):
+        masks = mask_tiles(i, seg_cols, info_rows)
+        span = (i + 1) * ROWS
+        rows = slice(i * ROWS, span)
+        grad_mixed = mm_t(branch_ref[slot_rows(i, me), :], watt_ref[...]).astype(BF16)
+        for h in range(heads):
+            own = slice(h * size, (h + 1) * size)
+            q = qkv_ref[rows, own]
+            k = qkv_ref[0:span, third + h * size : third + (h + 1) * size]
+            v = qkv_ref[0:span, 2 * third + h * size : 2 * third + (h + 1) * size]
+            dm = grad_mixed[:, own]
+            scores = mm_t(q, k) * scale + add_tiles(i, h, heads, masks, bias_ref, tab_ref)
+            prob = jnp.exp(scores - lse_ref[rows, h : h + 1])
+            grad_prob = mm_t(dm, v)
+            delta = jnp.sum(prob * grad_prob, axis=-1, keepdims=True)
+            grad_score = (prob * (grad_prob - delta)).astype(BF16)
+            proj_ref[rows, own] = (mm(grad_score, k) * scale).astype(BF16)
+            dk_ref[0:span, own] += t_mm(grad_score, q)
+            dv_ref[0:span, own] += t_mm(prob.astype(BF16), dm)
+            for j in range(i + 1):
+                tile = grad_score[:, j * ROWS : (j + 1) * ROWS].astype(F32)
+                if i - j < 2:
+                    near[i - j][h] = near[i - j][h] + tile
+                else:
+                    far[h] = far[h] + jnp.sum(tile, axis=0, keepdims=True)
+    proj_ref[:, third : 2 * third] = (dk_ref[...] * scale).astype(BF16)
+    proj_ref[:, 2 * third :] = dv_ref[...].astype(BF16)
+    edges = [int(e) for e in bucket_edges()]
+    buckets = []
+    for n in range(2):
+        distance = tile_distance(n * ROWS)
+        count = jnp.zeros((ROWS, ROWS), jnp.int32)
+        for edge in edges:
+            count = count + (distance >= edge).astype(jnp.int32)
+        buckets.append(count)
+    for b in range(BUCKETS):
+        picks = [buckets[n] == b for n in range(2)]
+        for h in range(heads):
+            line = jnp.sum(
+                jnp.where(picks[0], near[0][h], 0.0) + jnp.where(picks[1], near[1][h], 0.0),
+                axis=0,
+                keepdims=True,
+            )
+            if b == BUCKETS - 1:
+                line = line + far[h]
+            gtab_ref[h * BUCKETS + b : h * BUCKETS + b + 1, :] = line
+    gwq_ref[...] = t_mm(n1_ref[...], proj_ref[...]).astype(BF16)
+    gain = jnp.zeros((1, width), F32)
+    for i in range(blocks):
+        x = xs_ref[slot_rows(i, me), :width].astype(F32)
+        factor = lax.rsqrt(jnp.mean(x * x, axis=-1, keepdims=True) + 1e-06)
+        part = mm_t(proj_ref[i * ROWS : (i + 1) * ROWS, :], wq_ref[...])
+        gno_ref[slot_rows(i, me), :] = part.astype(BF16)
+        gain = gain + jnp.sum(part * (x * factor), axis=0, keepdims=True)
+    gain_ref[...] = jnp.broadcast_to(gain, gain_ref.shape)
+    gwatt_ref[...] = t_mm(mixed_ref[...], branch_ref[...]).astype(BF16)
+
+
+def expert_kernel(x_ref, g_ref, w1_ref, w2_ref, pick_ref, dx_ref, act_ref, pre_ref, out_ref):
+    width = x_ref.shape[1]
+    step = 256
+    root = math.sqrt(2.0 / math.pi)
+
+    def tile(t, carry):
+        rows = pl.ds(pl.multiple_of(t * step, step), step)
+        choose = mm(g_ref[rows, width:], pick_ref[...])
+        v = mm(x_ref[rows, :], w1_ref[...])
+        square = v * v
+        curve = jnp.tanh(root * v * (1.0 + 0.044715 * square))
+        half = 0.5 * (1.0 + curve)
+        slope = half + 0.5 * v * (1.0 - curve * curve) * (root * (1.0 + 3 * 0.044715 * square))
+        act = (choose * (v * half)).astype(BF16)
+        act_ref[rows, :] = act
+        grad_act = mm_t(g_ref[rows, :width], w2_ref[...])
+        grad_pre = (choose * grad_act * slope).astype(BF16)
+        pre_ref[rows, :] = grad_pre
+        dx_ref[rows, :] = mm_t(grad_pre, w1_ref[...]).astype(BF16)
+        out_ref[rows, :] = mm(act, w2_ref[...]).astype(BF16)
+        return carry
+
+    lax.fori_loop(0, x_ref.shape[0] // step, tile, 0)
+
+
+def weight_grad_kernel(count, *refs):
+    xs, gs, acts, pres = (refs[n * count : (n + 1) * count] for n in range(4))
+    own1_ref, far1_ref, own2_ref, far2_ref = refs[4 * count :]
+    width = xs[0].shape[1]
+    half = own1_ref.shape[1]
+    own1, far1, own2, far2 = 0.0, 0.0, 0.0, 0.0
+    for x, pre in zip(xs, pres):
+        own1 = own1 + t_mm(x[...], pre[:, :half])
+    own1_ref[...] = own1
+    for x, pre in zip(xs, pres):
+        far1 = far1 + t_mm(x[...], pre[:, half:])
+    far1_ref[...] = far1.astype(BF16)
+    for act, g in zip(acts, gs):
+        own2 = own2 + t_mm(act[:, :half], g[:, :width])
+    own2_ref[...] = own2
+    for act, g in zip(acts, gs):
+        far2 = far2 + t_mm(act[:, half:], g[:, :width])
+    far2_ref[...] = far2.astype(BF16)
+
+
+def call(kernel, outs, args, scratch=(), scalars=0, flops=0, moved=0, exps=0):
+    smem = pl.BlockSpec(memory_space=pltpu.SMEM)
+    vmem = pl.BlockSpec(memory_space=pltpu.VMEM)
+    return pl.pallas_call(
+        kernel,
+        out_shape=[jax.ShapeDtypeStruct(shape, dtype) for shape, dtype in outs],
+        in_specs=[smem] * scalars + [vmem] * (len(args) - scalars),
+        out_specs=[vmem] * len(outs),
+        scratch_shapes=list(scratch),
+        compiler_params=pltpu.CompilerParams(vmem_limit_bytes=VMEM_BYTES),
+        cost_estimate=pl.CostEstimate(flops=flops, bytes_accessed=moved, transcendentals=exps),
+    )(*args)
+
+
+def head_body(
+    tokens,
+    cotangent,
+    segment_ids,
+    pad_mask,
+    routes,
+    gate_weights,
+    gain_one,
+    w_qkv,
+    w_attn,
+    rel_table,
+    gain_two,
+    w_expert_in,
+    w_expert_out,
+):
+    x_low = tokens[0]
+    g_low = cotangent[0]
+    rows, width = x_low.shape
+    size_z, size_y, size_x, size_c = (lax.axis_size(a) for a in AXES)
+    parts = size_x * size_c
+    devices = size_z * size_y * parts
+    me = lax.axis_index(("x", "c"))
+    head_count = rel_table.shape[0]
+    heads = head_count // parts
+    third = width // parts
+    length = rows * parts
+    experts, shard, ff = w_expert_in.shape
+    ff_own = ff // devices
+    me_arr = me.astype(jnp.int32).reshape(1)
+
+    seg = segment_ids[0]
+    info = jnp.where(pad_mask[0] == 1, seg, -1)
+    marks = jnp.stack([seg, info], axis=1).astype(BF16)
+    x_ext = jnp.concatenate([x_low, jnp.pad(marks, ((0, 0), (0, EXT - 2)))], axis=1)
+    xs = gather_seq(x_ext)
+
+    by_part = w_qkv.reshape(shard, 3, parts, third).transpose(2, 0, 1, 3)
+    by_part = by_part.reshape(1, parts, shard, 3 * third)
+    qkv_send = jnp.broadcast_to(by_part, (devices // parts, parts, shard, 3 * third))
+    wq = lax.all_to_all(
+        qkv_send.reshape(devices, shard, 3 * third), AXES, 0, 0, tiled=True
+    ).reshape(width, 3 * third)
+
+    in_send = w_expert_in.reshape(experts, shard, devices, ff_own).transpose(2, 1, 0, 3)
+    in_send = in_send.reshape(devices, shard, experts * ff_own)
+    in_send, wq = lax.optimization_barrier((in_send, wq))
+    w1_own = lax.all_to_all(in_send, AXES, 0, 0, tiled=True).reshape(width, experts * ff_own)
+    w2_own = w_expert_out.reshape(experts * ff_own, width)
+    w1 = jnp.concatenate([w1_own, swap(w1_own, "y")], axis=1)
+    w2 = jnp.concatenate([w2_own, swap(w2_own, "y")], axis=0)
+
+    groups = devices // parts
+    to_part = [((i % groups) * parts + i // groups) for i in range(devices)]
+    att_one = lax.ppermute(w_attn, AXES, [(i, to_part[i]) for i in range(devices)])
+    watt = lax.all_gather(att_one, ("z", "y"), axis=0, tiled=True)
+
+    expert_ids = jnp.arange(experts, dtype=jnp.int32)
+    choose = jnp.sum(
+        gate_weights[0][:, :, None] * (routes[0][:, :, None] == expert_ids).astype(F32), axis=1
+    )
+    choose_hi = choose.astype(BF16)
+    choose_lo = (choose - choose_hi.astype(F32)).astype(BF16)
+    g_ext = jnp.concatenate(
+        [g_low, choose_hi, choose_lo, jnp.zeros((rows, EXT - 2 * experts), BF16)], axis=1
+    )
+    g_ext, wq = lax.optimization_barrier((g_ext, wq))
+    g_z = jnp.stack([g_ext] + [swap(g_ext, "z", k) for k in range(1, size_z)])
+    g_x = swap(g_z, "x")
+    g_zx = jnp.concatenate([g_z, g_x], axis=1)
+    g_c = swap(g_zx, "c")
+    g_all = jnp.concatenate([g_zx, g_c], axis=1)
+
+    table = lax.dynamic_slice_in_dim(rel_table, me * heads, heads, 0).astype(F32)
+    n1, qkv, mixed, lse = call(
+        attend_kernel,
+        [
+            ((length, width), BF16),
+            ((length, 3 * third), BF16),
+            ((length, third), BF16),
+            ((length, EXT), F32),
+        ],
+        [me_arr, table, xs, gain_one.reshape(1, width), wq],
+        scratch=[pltpu.VMEM((2 * heads, ROWS, ROWS), F32)],
+        scalars=2,
+        flops=2 * length * width * 3 * third + 4 * length * length * third,
+        moved=2 * length * width * 4,
+        exps=heads * length * length,
+    )
+    branch_part = mm(mixed, watt)
+    inputs = x_low.astype(F32)
+    hidden_one = inputs + reduce_seq(branch_part)
+    scaled_two, factor_two = norm_stats(hidden_one)
+    normed_two = (scaled_two * gain_two).astype(BF16)
+
+    pick_np = np.zeros((EXT, 2 * experts * ff_own), np.float32)
+    for e in range(experts):
+        for y in range(2):
+            start = (y * experts + e) * ff_own
+            pick_np[[e, experts + e], start : start + ff_own] = 1.0
+    pick = jnp.asarray(pick_np, BF16)
+    ff_two = 2 * experts * ff_own
+    x_blocks, g_blocks, act_blocks, pre_blocks, out_blocks = [], [], [], [], []
+    grad_normed_two = None
+    for k in range(size_z):
+        x_block = gather_seq(normed_two if k == 0 else swap(normed_two, "z", k))
+        g_block = g_all[k]
+        dx, act, pre, out = call(
+            expert_kernel,
+            [
+                ((length, width), BF16),
+                ((length, ff_two), BF16),
+                ((length, ff_two), BF16),
+                ((length, width), BF16),
+            ],
+            [x_block, g_block, w1, w2, pick],
+            flops=8 * length * width * ff_two,
+            moved=2 * (6 * length * width + 2 * width * ff_two),
+            exps=length * ff_two,
+        )
+        x_blocks.append(x_block)
+        g_blocks.append(g_block)
+        act_blocks.append(act)
+        pre_blocks.append(pre)
+        out_blocks.append(out)
+        back = reduce_seq(dx)
+        if k:
+            back = swap(back.astype(BF16), "z", k).astype(F32)
+        grad_normed_two = back if grad_normed_two is None else grad_normed_two + back
+
+    outs = jnp.stack(out_blocks)
+    half = length // 2
+    out_c = outs[:, :half].astype(F32) + swap(outs[:, half:], "c").astype(F32)
+    out_x = out_c[:, :rows] + swap(out_c[:, rows:].astype(BF16), "x").astype(F32)
+    combined = out_x[0]
+    for k in range(1, size_z):
+        combined = combined + swap(out_x[k].astype(BF16), "z", k).astype(F32)
+    output = (hidden_one + combined).astype(BF16)
+
+    ff_half = experts * ff_own
+    own1, far1, own2, far2 = call(
+        lambda *refs: weight_grad_kernel(size_z, *refs),
+        [
+            ((width, ff_half), F32),
+            ((width, ff_half), BF16),
+            ((ff_half, width), F32),
+            ((ff_half, width), BF16),
+        ],
+        [*x_blocks, *g_blocks, *act_blocks, *pre_blocks],
+        flops=4 * size_z * length * width * ff_two,
+        moved=2 * 4 * size_z * length * width,
+    )
+    grad_w_out = (own2 + swap(far2, "y").astype(F32)).reshape(experts, ff_own, width)
+    in_sum = (own1 + swap(far1, "y").astype(F32)).astype(BF16)
+    in_got = lax.all_to_all(
+        in_sum.reshape(devices, shard, ff_half), AXES, 0, 0, tiled=True
+    )
+    grad_w_in = (
+        in_got.reshape(devices, shard, experts, ff_own)
+        .transpose(2, 1, 0, 3)
+        .reshape(experts, shard, ff)
+        .astype(F32)
+    )
+
+    grad_hidden_norm, gain_two_part = norm_back(grad_normed_two, scaled_two, factor_two, gain_two)
+    grad_hidden = g_low.astype(F32) + grad_hidden_norm
+    branch = gather_seq(grad_hidden.astype(BF16))
+    gwq, gno, gain_one_part, table_part, gwatt = call(
+        attend_back_kernel,
+        [
+            ((width, 3 * third), BF16),
+            ((length, width), BF16),
+            ((8, width), F32),
+            ((heads * BUCKETS, ROWS), F32),
+            ((third, width), BF16),
+        ],
+        [me_arr, table, branch, watt, qkv, n1, lse, xs, wq, mixed],
+        scratch=[
+            pltpu.VMEM((2 * heads, ROWS, ROWS), F32),
+            pltpu.VMEM((length, third), F32),
+            pltpu.VMEM((length, third), F32),
+            pltpu.VMEM((length, 3 * third), BF16),
+        ],
+        scalars=2,
+        flops=6 * length * width * 3 * third + 10 * length * length * third,
+        moved=2 * length * width * 6,
+        exps=heads * length * length,
+    )
+    grad_normed_one = reduce_seq(gno)
+    scaled_one, factor_one = norm_stats(inputs)
+    grad_input_norm, unused_gain = norm_back(grad_normed_one, scaled_one, factor_one, gain_one)
+    grad_inputs = grad_hidden + grad_input_norm
+
+    att_share = lax.psum_scatter(gwatt, ("z", "y"), scatter_dimension=0, tiled=True)
+    grad_w_attn = lax.ppermute(
+        att_share, AXES, [(to_part[i], i) for i in range(devices)]
+    ).astype(F32)
+
+    small_table = lax.dynamic_update_slice_in_dim(
+        jnp.zeros((head_count, BUCKETS), F32),
+        jnp.sum(table_part, axis=1).reshape(heads, BUCKETS),
+        me * heads,
+        0,
+    )
+    small = jnp.concatenate([gain_one_part[0], gain_two_part, small_table.reshape(-1)])
+    small_hi = small.astype(BF16)
+    small_lo = (small - small_hi.astype(F32)).astype(BF16)
+    count = small.shape[0]
+    extra = -(-2 * count // (3 * third * 8)) * 8
+    small_rows = jnp.pad(
+        jnp.concatenate([small_hi, small_lo]), (0, extra * 3 * third - 2 * count)
+    ).reshape(1, extra, 3 * third)
+    last_send = jnp.concatenate(
+        [
+            gwq.reshape(devices, shard, 3 * third),
+            jnp.broadcast_to(small_rows, (devices, extra, 3 * third)),
+        ],
+        axis=1,
+    )
+    last = lax.all_to_all(last_send, AXES, 0, 0, tiled=True).astype(F32)
+    grad_w_qkv = (
+        jnp.sum(last[:, :shard].reshape(groups, parts, shard, 3, third), axis=0)
+        .transpose(1, 2, 0, 3)
+        .reshape(shard, 3 * width)
+    )
+    small_sum = jnp.sum(last[:, shard:], axis=0).reshape(-1)
+    totals = small_sum[:count] + small_sum[count : 2 * count]
+    return (
+        output[None],
+        grad_inputs[None],
+        totals[:width],
+        grad_w_qkv,
+        grad_w_attn,
+        totals[2 * width :].reshape(head_count, BUCKETS),
+        totals[width : 2 * width],
+        grad_w_in,
+        grad_w_out,
+    )
+
+
+def heads_fit(mesh):
+    return mesh.shape["seq"] == 4 and mesh.shape["dp"] == 8
+
+
+def solution(mesh):
+    if not heads_fit(mesh):
+        return rows_solution(mesh)
+    grid = Mesh(mesh.devices.reshape(mesh.shape["dp"] // 2, 2, mesh.shape["seq"] // 2, 2), AXES)
+    by_token = P(("z", "y"), ("x", "c"))
+    by_row = P(AXES, None)
+    by_second = P(None, AXES, None)
+    return jax.shard_map(
+        head_body,
+        mesh=grid,
+        in_specs=(
+            by_token,
+            by_token,
+            by_token,
+            by_token,
+            by_token,
+            by_token,
+            P(),
+            by_row,
+            by_row,
+            P(),
+            P(),
+            by_second,
+            by_second,
+        ),
+        out_specs=(
+            by_token,
+            by_token,
+            P(),
+            by_row,
+            by_row,
+            P(),
+            P(),
+            by_second,
+            by_second,
+        ),
+        check_vma=False,
+    )

time: 1440 us -> 395 us (0.27)
  waiting for transfers between devices: 1180 us -> 149 us
  matrix products: 125 us -> 0.35 us
  starting transfers between devices: 0.65 us -> 64.6 us
  Pallas kernels: 0 us -> 46.9 us
  blocking collectives: 63.1 us -> 31.1 us
  other arithmetic: 20 us -> 36.8 us
    reduce_scatter x4 -> x1, waiting for transfers between devices: 840 us -> 41.3 us  [head_body(): lax.psum_scatter(gwatt, ('z', 'y'), scatter_dimension=0, tiled=True)]
    all_gather x4 -> x0, waiting for transfers between devices: 291 us -> none  [the longest x1 124 us: body(): lax.all_gather(w_expert_out, ('dp', 'seq'), axis=1, tiled=True)]
    dot_general x27 -> x1, matrix products: 125 us -> 0.35 us  [mm(): lax.dot_general(a, b, (((1,), (0,)), ((), ())), preferred_element_type=F32)]
    ppermute x0 -> x46, waiting for transfers between devices: none -> 107 us  [the longest x44 107 us: swap(): return lax.ppermute(value, axis, [(i, i ^ step) for i in range(size)])]
    pallas_call x0 -> x7, Pallas kernels: none -> 46.9 us  [call(): pl.pallas_call(kernel, out_shape=[jax.ShapeDtypeStruct(shape, dtype) for...]
    unnamed x12 -> x1, waiting for transfers between devices: 44.9 us -> 0.02 us
    ppermute x0 -> x46, starting transfers between devices: none -> 44.2 us  [the longest x44 41.9 us: swap(): return lax.ppermute(value, axis, [(i, i ^ step) for i in range(size)])]
    psum x1 -> x0, blocking collectives: 39.8 us -> none  [body(): lax.psum((grad_table, grad_gain_one, grad_gain_two), ('dp', 'seq'))]
  transfers between devices with their start and end apart: 10 -> 51, of which waited for: 10 -> 17; matrix products, arithmetic and copies ran while one was open for 8% -> 14% of each run, Pallas kernels for 0% -> 9%
where the time goes in v1:
time: 395 us; the launch traced here: 387 us
  waiting for transfers between devices  149 us (38%)
  starting transfers between devices  64.6 us (16%)
  Pallas kernels  46.9 us (12%)
  local copies, waits for them, and re-layouts  43.2 us (11%)
  other arithmetic  36.8 us (9%)
  blocking collectives  31.1 us (8%)
  between operations  15.7 us (4%)
    ppermute x44, waiting for transfers between devices, swap(): return lax.ppermute(value, axis, [(i, i ^ step) for i in range(size)])  107 us
    pallas_call x7, Pallas kernels, call(): pl.pallas_call(kernel, out_shape=[jax.ShapeDtypeStruct(shape, dtype) for...  46.9 us
    ppermute x44, starting transfers between devices, swap(): return lax.ppermute(value, axis, [(i, i ^ step) for i in range(size)])  41.9 us
    reduce_scatter x1, waiting for transfers between devices, head_body(): lax.psum_scatter(gwatt, ('z', 'y'), scatter_dimension=0, tiled=True)  41.3 us
    all_gather x1, blocking collectives, head_body(): watt = lax.all_gather(att_one, ('z', 'y'), axis=0, tiled=True)  31.1 us
    unnamed x122, local copies, waits for them, and re-layouts  14.1 us
  transfers between devices with their start and end apart: 51, of which 17 were waited for; matrix products, arithmetic and copies ran while one was open for 14% of the time, Pallas kernels for 9%

profile of v1, /device:TPU:0, one launch (start us, length us, event | category | flops | bytes accessed | tf_op | source)
XLA Modules:
  0.0 387.3 jit_solution(2984142246633552995)
XLA Ops:
  9.6 7.3 %all-to-all-start = ((bf16[32,24,576]{2,1,0:T(8,128)(2,1)}), bf16[32,24,576]{2,1,0:T(8,128)(2,1)S(1)}, u32[]{:S(2)}, u32[]{:S(2)}) async-start(bf16[32,24,576]{2,1,0:T(8,128)(2,1)} %bitcast.9), calls=%async_computation | async-start | bytes 1966080 | tf_op jit(solution)/shard_map/all_to_all | solution.py:698
  20.0 13.2 %collective-permute-done = bf16[128,896]{1,0:T(8,128)(2,1)S(1)} collective-permute-done((bf16[128,896]{1,0:T(8,128)(2,1)S(1)}, bf16[128,896]{1,0:T(8,128)(2,1)S(1)}, u32[]{:S(2)}, u32[]{:S(2)}) %collective-permute-start) | collective-permute-done | bytes 229408 | tf_op jit(solution)/shard_map/ppermute | solution.py:386
  37.7 31.1 %all_gather.3.watt_ref = bf16[192,768]{1,0:T(8,128)(2,1)S(1)} all-gather(bf16[24,768]{1,0:T(8,128)(2,1)S(1)} %collective-permute-done.2), channel_id=1, replica_groups=mesh['z'=4,'y'=2,'x'=2,'c'=2] {'z','y'}, dimensions={0}, use_global_device_ids=true | all-gather | bytes 331776 | tf_op jit(solution)/shard_map/all_gather | solution.py:713
  69.9 5.7 %shard_map.205 = (bf16[512,768]{1,0:T(8,128)(2,1)S(1)}, bf16[512,576]{1,0:T(8,128)(2,1)S(1)}, bf16[512,192]{1,0:T(8,128)(2,1)S(1)}, f32[512,128]{1,0:T(8,128)S(1)}) custom-call(s32[1]{0:T(128)} %bitcast.1.me_ref, f32[3,32]{1,0:T(4,128)S(1)} %dynamic-slice_convert_fusion.tab_ref, bf16[512,896]{1,0:T(8,128)(2,1)S(1)} %pad_maximum_fusion.6.xs_ref, ...), custom_call_target="tpu_custom_call" | custom-call | flops 654311424 | bytes 3145728 | tf_op jit(solution)/shard_map/pallas_call | solution.py:648
  76.7 3.8 collective-permute-start.7
  80.6 6.0 %collective-permute-done.9 = bf16[128,896]{1,0:T(8,128)(2,1)S(1)} collective-permute-done((bf16[128,896]{1,0:T(8,128)(2,1)S(1)}, bf16[128,896]{1,0:T(8,128)(2,1)S(1)}, u32[]{:S(2)}, u32[]{:S(2)}) %collective-permute-start.9) | collective-permute-done | bytes 229408 | tf_op jit(solution)/shard_map/ppermute | solution.py:386
  86.5 10.6 %collective-permute-done.8 = bf16[128,896]{1,0:T(8,128)(2,1)S(1)} collective-permute-done((bf16[128,896]{1,0:T(8,128)(2,1)S(1)}, bf16[128,896]{1,0:T(8,128)(2,1)S(1)}, u32[]{:S(2)}, u32[]{:S(2)}) %collective-permute-start.8) | collective-permute-done | bytes 229408 | tf_op jit(solution)/shard_map/ppermute | solution.py:386
  98.9 7.0 %collective-permute-start.10 = (bf16[4,128,896]{2,1,0:T(8,128)(2,1)}, bf16[4,128,896]{2,1,0:T(8,128)(2,1)S(1)}, u32[]{:S(2)}, u32[]{:S(2)}) collective-permute-start(bf16[4,128,896]{2,1,0:T(8,128)(2,1)} %pad_maximum_fusion.7), channel_id=1, source_target_pairs={{0,2},{2,0},{1,3},{3,1},{4,6},{6,4},{5,7},{7,5},{8,10},{10,8},{9,1... | collective-permute-start | bytes 2752520 | tf_op jit(solution)/shard_map/ppermute | solution.py:386
  107.1 4.6 %all-to-all-start.1 = ((bf16[32,24,384]{2,1,0:T(8,128)(2,1)}), bf16[32,24,384]{2,1,0:T(8,128)(2,1)}, u32[]{:S(2)}, u32[]{:S(2)}) async-start(bf16[32,24,384]{2,1,0:T(8,128)(2,1)} %reshape.141), calls=%async_computation.1 | async-start | bytes 1179648 | tf_op jit(solution)/shard_map/all_to_all | solution.py:705
  111.7 24.4 %collective-permute-done.4 = bf16[128,768]{1,0:T(8,128)(2,1)} collective-permute-done((bf16[128,768]{1,0:T(8,128)(2,1)S(1)}, bf16[128,768]{1,0:T(8,128)(2,1)}, u32[]{:S(2)}, u32[]{:S(2)}) %collective-permute-start.4) | collective-permute-done | bytes 196640 | tf_op jit(solution)/shard_map/ppermute | solution.py:386
  150.3 3.6 collective-permute-done.17
  173.3 9.5 %collective-permute-done.12 = bf16[768,384]{1,0:T(8,128)(2,1)S(1)} collective-permute-done((bf16[768,384]{1,0:T(8,128)(2,1)}, bf16[768,384]{1,0:T(8,128)(2,1)S(1)}, u32[]{:S(2)}, u32[]{:S(2)}) %collective-permute-start.12) | collective-permute-done | bytes 589856 | tf_op jit(solution)/shard_map/ppermute | solution.py:386
  187.2 5.5 %shard_map.209 = (bf16[512,768]{1,0:T(8,128)(2,1)S(1)}, bf16[512,768]{1,0:T(8,128)(2,1)S(1)}, bf16[512,768]{1,0:T(8,128)(2,1)S(1)}, bf16[512,768]{1,0:T(8,128)(2,1)S(1)}) custom-call(bf16[512,768]{1,0:T(8,128)(2,1)} %constant_dynamic-update-slice_fusion.6.x_ref.refs_3_, bf16[512,896]{1,0:T(8,128)(2,1)S(1)} %get-tuple-element.85.g_ref.refs_7_, ...), custom_call_target="tpu_custom_call" | custom-call | flops 2415919104 | bytes 7077888 | tf_op jit(solution)/shard_map/pallas_call | solution.py:648
  194.4 4.5 %shard_map.208 = (bf16[512,768]{1,0:T(8,128)(2,1)S(1)}, bf16[512,768]{1,0:T(8,128)(2,1)S(1)}, bf16[512,768]{1,0:T(8,128)(2,1)S(1)}, bf16[512,768]{1,0:T(8,128)(2,1)S(1)}) custom-call(bf16[512,768]{1,0:T(8,128)(2,1)S(1)} %copy-done.6, bf16[512,896]{1,0:T(8,128)(2,1)S(1)} %get-tuple-element.86.g_ref.refs_6_, bf16[768,768]{1,0:T(8,128)(2,1)S(1)} %pad_maximum_fusion.4.w1_ref, ...), custom_call_target="tpu_custom_call" | custom-call | flops 2415919104 | bytes 7077888 | tf_op jit(solution)/shard_map/pallas_call | solution.py:648
  200.8 4.5 %shard_map.207 = (bf16[512,768]{1,0:T(8,128)(2,1)S(1)}, bf16[512,768]{1,0:T(8,128)(2,1)S(1)}, bf16[512,768]{1,0:T(8,128)(2,1)S(1)}, bf16[512,768]{1,0:T(8,128)(2,1)S(1)}) custom-call(bf16[512,768]{1,0:T(8,128)(2,1)S(1)} %constant_dynamic-update-slice_fusion.x_ref.refs_1_, bf16[512,896]{1,0:T(8,128)(2,1)S(1)} %get-tuple-element.87.g_ref.refs_5_, ...), custom_call_target="tpu_custom_call" | custom-call | flops 2415919104 | bytes 7077888 | tf_op jit(solution)/shard_map/pallas_call | solution.py:648
  207.1 4.7 %shard_map.206 = (bf16[512,768]{1,0:T(8,128)(2,1)S(1)}, bf16[512,768]{1,0:T(8,128)(2,1)S(1)}, bf16[512,768]{1,0:T(8,128)(2,1)S(1)}, bf16[512,768]{1,0:T(8,128)(2,1)S(1)}) custom-call(bf16[512,768]{1,0:T(8,128)(2,1)S(1)} %pad_maximum_fusion.8.x_ref.refs_0_, bf16[512,896]{1,0:T(8,128)(2,1)S(1)} %get-tuple-element.84.g_ref.refs_4_, ...), custom_call_target="tpu_custom_call" | custom-call | flops 2415919104 | bytes 7077888 | tf_op jit(solution)/shard_map/pallas_call | solution.py:648
  229.6 10.7 %shard_map.211 = (f32[768,384]{1,0:T(8,128)}, bf16[768,384]{1,0:T(8,128)(2,1)S(1)}, f32[384,768]{1,0:T(8,128)}, bf16[384,768]{1,0:T(8,128)(2,1)}) custom-call(bf16[512,768]{1,0:T(8,128)(2,1)S(1)} %pad_maximum_fusion.8.x_ref.refs_0_, bf16[512,768]{1,0:T(8,128)(2,1)S(1)} %constant_dynamic-update-slice_fusion.x_ref.refs_1_, bf16[512,768]{1,0:T(8,128)(2,1)S(1)} %copy-done.6, ...), custom_call_target="tpu_custom_call" | custom-call | flops 4831838208 | bytes 12582912 | tf_op jit(solution)/shard_map/pallas_call | solution.py:648
  248.0 6.5 %collective-permute-done.44 = bf16[768,384]{1,0:T(8,128)(2,1)S(1)} collective-permute-done((bf16[768,384]{1,0:T(8,128)(2,1)S(1)}, bf16[768,384]{1,0:T(8,128)(2,1)S(1)}, u32[]{:S(2)}, u32[]{:S(2)}) %collective-permute-start.44) | collective-permute-done | bytes 589856 | tf_op jit(solution)/shard_map/ppermute | solution.py:386
  265.0 11.3 %shard_map.210 = (bf16[768,576]{1,0:T(8,128)(2,1)S(1)}, bf16[512,768]{1,0:T(8,128)(2,1)S(1)}, f32[8,768]{1,0:T(8,128)S(1)}, f32[96,128]{1,0:T(8,128)S(1)}, bf16[192,768]{1,0:T(8,128)(2,1)}) custom-call(s32[1]{0:T(128)} %bitcast.1.me_ref, f32[3,32]{1,0:T(4,128)S(1)} %dynamic-slice_convert_fusion.tab_ref, bf16[512,768]{1,0:T(8,128)(2,1)S(1)} %pad_maximum_fusion.9.branch_ref, ...), custom_call_target="tpu_custom_call" | custom-call | flops 1862270976 | bytes 4718592 | tf_op jit(solution)/shard_map/pallas_call | solution.py:648
  278.9 4.9 %all-to-all-start.2 = ((bf16[32,32,576]{2,1,0:T(8,128)(2,1)}), bf16[32,32,576]{2,1,0:T(8,128)(2,1)S(1)}, u32[]{:S(2)}, u32[]{:S(2)}) async-start(bf16[32,32,576]{2,1,0:T(8,128)(2,1)} %pad_maximum_fusion.3), calls=%async_computation.2 | async-start | bytes 2621440 | tf_op jit(solution)/shard_map/all_to_all | solution.py:877
  301.0 41.3 %reduce-scatter.2.cloned.1.call-done = bf16[24,768]{1,0:T(8,128)(2,1)} async-done(((bf16[192,768]{1,0:T(8,128)(2,1)}), bf16[24,768]{1,0:T(8,128)(2,1)}) %reduce-scatter.2.cloned.1.call-update) | async-done | bytes 36880 | tf_op jit(solution)/shard_map/reduce_scatter | solution.py:851
  346.2 6.1 %collective-permute-start.27 = (bf16[128,768]{1,0:T(8,128)(2,1)S(1)}, bf16[128,768]{1,0:T(8,128)(2,1)S(1)}, u32[]{:S(2)}, u32[]{:S(2)}) collective-permute-start(bf16[128,768]{1,0:T(8,128)(2,1)S(1)} %get-tuple-element.89), channel_id=1, source_target_pairs={{0,24},{8,16},{16,8},{24,0},{1,25},{9,17},{17,9},{25,1},{2,26},{10... | collective-permute-start | bytes 589832 | tf_op jit(solution)/shard_map/ppermute | solution.py:386
  353.6 4.5 %collective-permute-done.27 = bf16[128,768]{1,0:T(8,128)(2,1)S(1)} collective-permute-done((bf16[128,768]{1,0:T(8,128)(2,1)S(1)}, bf16[128,768]{1,0:T(8,128)(2,1)S(1)}, u32[]{:S(2)}, u32[]{:S(2)}) %collective-permute-start.27) | collective-permute-done | bytes 196640 | tf_op jit(solution)/shard_map/ppermute | solution.py:386
  358.1 10.8 %collective-permute-done.26 = bf16[128,768]{1,0:T(8,128)(2,1)S(1)} collective-permute-done((bf16[128,768]{1,0:T(8,128)(2,1)S(1)}, bf16[128,768]{1,0:T(8,128)(2,1)S(1)}, u32[]{:S(2)}, u32[]{:S(2)}) %collective-permute-start.26) | collective-permute-done | bytes 196640 | tf_op jit(solution)/shard_map/ppermute | solution.py:386
  (317 shorter events, 129.4 us)
Async XLA Ops:
  9.6 60.3 %all-to-all-start = ((bf16[32,24,576]{2,1,0:T(8,128)(2,1)}), bf16[32,24,576]{2,1,0:T(8,128)(2,1)S(1)}, u32[]{:S(2)}, u32[]{:S(2)}) async-start(bf16[32,24,576]{2,1,0:T(8,128)(2,1)} %bitcast.9), calls=%async_computation | async-start | bytes 1966080 | tf_op jit(solution)/shard_map/all_to_all | solution.py:698
  19.0 18.7 %collective-permute-start.2 = (bf16[24,768]{1,0:T(8,128)(2,1)S(1)}, bf16[24,768]{1,0:T(8,128)(2,1)S(1)}, u32[]{:S(2)}, u32[]{:S(2)}) collective-permute-start(bf16[24,768]{1,0:T(8,128)(2,1)S(1)} %copy-done.57), channel_id=1, source_target_pairs={{0,0},{1,4},{2,8},{3,12},{4,16},{5,20},{6,24},{7,28},{8,1},{9,5},{... | collective-permute-start | bytes 110600 | tf_op jit(solution)/shard_map/ppermute | solution.py:712
  34.0 34.8 %collective-permute-start.1 = (bf16[256,896]{1,0:T(8,128)(2,1)}, bf16[256,896]{1,0:T(8,128)(2,1)}, u32[]{:S(2)}, u32[]{:S(2)}) collective-permute-start(bf16[256,896]{1,0:T(8,128)(2,1)} %pad_maximum_fusion.10), channel_id=1, source_target_pairs={{0,1},{1,0},{2,3},{3,2},{4,5},{5,4},{6,7},{7,6},{8,9},{9,8},{10,11... | collective-permute-start | bytes 1376264 | tf_op jit(solution)/shard_map/ppermute | solution.py:386
  76.0 29.9 %collective-permute-start.3 = (bf16[256,768]{1,0:T(8,128)(2,1)S(1)}, bf16[256,768]{1,0:T(8,128)(2,1)S(1)}, u32[]{:S(2)}, u32[]{:S(2)}) collective-permute-start(bf16[256,768]{1,0:T(8,128)(2,1)S(1)} %slice.304), channel_id=1, source_target_pairs={{0,1},{1,0},{2,3},{3,2},{4,5},{5,4},{6,7},{7,6},{8,9},{9,8},{10,11... | collective-permute-start | bytes 1179656 | tf_op jit(solution)/shard_map/ppermute | solution.py:386
  76.7 20.3 %collective-permute-start.8 = (bf16[128,896]{1,0:T(8,128)(2,1)S(1)}, bf16[128,896]{1,0:T(8,128)(2,1)S(1)}, u32[]{:S(2)}, u32[]{:S(2)}) collective-permute-start(bf16[128,896]{1,0:T(8,128)(2,1)S(1)} %maximum_maximum_fusion), channel_id=1, source_target_pairs={{0,16},{8,24},{16,0},{24,8},{1,17},{9,25},{17,1},{25,9},{2,18},{10... | collective-permute-start | bytes 688136 | tf_op jit(solution)/shard_map/ppermute | solution.py:386
  76.7 20.3 %collective-permute-start.7 = (bf16[128,896]{1,0:T(8,128)(2,1)S(1)}, bf16[128,896]{1,0:T(8,128)(2,1)S(1)}, u32[]{:S(2)}, u32[]{:S(2)}) collective-permute-start(bf16[128,896]{1,0:T(8,128)(2,1)S(1)} %maximum_maximum_fusion), channel_id=1, source_target_pairs={{0,8},{8,0},{16,24},{24,16},{1,9},{9,1},{17,25},{25,17},{2,10},{10... | collective-permute-start | bytes 688136 | tf_op jit(solution)/shard_map/ppermute | solution.py:386
  98.9 43.1 %collective-permute-start.10 = (bf16[4,128,896]{2,1,0:T(8,128)(2,1)}, bf16[4,128,896]{2,1,0:T(8,128)(2,1)S(1)}, u32[]{:S(2)}, u32[]{:S(2)}) collective-permute-start(bf16[4,128,896]{2,1,0:T(8,128)(2,1)} %pad_maximum_fusion.7), channel_id=1, source_target_pairs={{0,2},{2,0},{1,3},{3,1},{4,6},{6,4},{5,7},{7,5},{8,10},{10,8},{9,1... | collective-permute-start | bytes 2752520 | tf_op jit(solution)/shard_map/ppermute | solution.py:386
  106.9 29.2 %collective-permute-start.4 = (bf16[128,768]{1,0:T(8,128)(2,1)S(1)}, bf16[128,768]{1,0:T(8,128)(2,1)}, u32[]{:S(2)}, u32[]{:S(2)}) collective-permute-start(bf16[128,768]{1,0:T(8,128)(2,1)S(1)} %slice.310), channel_id=1, source_target_pairs={{0,2},{2,0},{1,3},{3,1},{4,6},{6,4},{5,7},{7,5},{8,10},{10,8},{9,1... | collective-permute-start | bytes 589832 | tf_op jit(solution)/shard_map/ppermute | solution.py:386
  107.0 39.3 %collective-permute-start.13 = (bf16[384,768]{1,0:T(8,128)(2,1)}, bf16[384,768]{1,0:T(8,128)(2,1)}, u32[]{:S(2)}, u32[]{:S(2)}) collective-permute-start(bf16[384,768]{1,0:T(8,128)(2,1)} %bitcast.17), channel_id=1, source_target_pairs={{0,4},{4,0},{1,5},{5,1},{2,6},{6,2},{3,7},{7,3},{8,12},{12,8},{9,1... | collective-permute-start | bytes 1769480 | tf_op jit(solution)/shard_map/ppermute | solution.py:386
  107.1 59.7 %all-to-all-start.1 = ((bf16[32,24,384]{2,1,0:T(8,128)(2,1)}), bf16[32,24,384]{2,1,0:T(8,128)(2,1)}, u32[]{:S(2)}, u32[]{:S(2)}) async-start(bf16[32,24,384]{2,1,0:T(8,128)(2,1)} %reshape.141), calls=%async_computation.1 | async-start | bytes 1179648 | tf_op jit(solution)/shard_map/all_to_all | solution.py:705
  139.0 16.7 %collective-permute-start.14 = (bf16[128,768]{1,0:T(8,128)(2,1)S(1)}, bf16[128,768]{1,0:T(8,128)(2,1)S(1)}, u32[]{:S(2)}, u32[]{:S(2)}) collective-permute-start(bf16[128,768]{1,0:T(8,128)(2,1)S(1)} %multiply_convert_fusion), channel_id=1, source_target_pairs={{0,8},{8,0},{16,24},{24,16},{1,9},{9,1},{17,25},{25,17},{2,10},{10... | collective-permute-start | bytes 589832 | tf_op jit(solution)/shard_map/ppermute | solution.py:386
  146.3 37.7 %collective-permute-start.11 = (bf16[4,256,896]{2,1,0:T(8,128)(2,1)}, bf16[4,256,896]{2,1,0:T(8,128)(2,1)}, u32[]{:S(2)}, u32[]{:S(2)}) collective-permute-start(bf16[4,256,896]{2,1,0:T(8,128)(2,1)} %pad_maximum_fusion.2), channel_id=1, source_target_pairs={{0,1},{1,0},{2,3},{3,2},{4,5},{5,4},{6,7},{7,6},{8,9},{9,8},{10,11... | collective-permute-start | bytes 5505032 | tf_op jit(solution)/shard_map/ppermute | solution.py:386
  149.5 17.3 %collective-permute-start.6 = (bf16[256,768]{1,0:T(8,128)(2,1)}, bf16[256,768]{1,0:T(8,128)(2,1)}, u32[]{:S(2)}, u32[]{:S(2)}) collective-permute-start(bf16[256,768]{1,0:T(8,128)(2,1)} %pad_maximum_fusion.11), channel_id=1, source_target_pairs={{0,1},{1,0},{2,3},{3,2},{4,5},{5,4},{6,7},{7,6},{8,9},{9,8},{10,11... | collective-permute-start | bytes 1179656 | tf_op jit(solution)/shard_map/ppermute | solution.py:386
  193.6 18.4 %collective-permute-start.36 = (bf16[256,768]{1,0:T(8,128)(2,1)S(1)}, bf16[256,768]{1,0:T(8,128)(2,1)}, u32[]{:S(2)}, u32[]{:S(2)}) collective-permute-start(bf16[256,768]{1,0:T(8,128)(2,1)S(1)} %slice.181), channel_id=1, source_target_pairs={{0,1},{1,0},{2,3},{3,2},{4,5},{5,4},{6,7},{7,6},{8,9},{9,8},{10,11... | collective-permute-start | bytes 1179656 | tf_op jit(solution)/shard_map/ppermute | solution.py:386
  217.7 23.0 %collective-permute-start.29 = (bf16[128,768]{1,0:T(8,128)(2,1)S(1)}, bf16[128,768]{1,0:T(8,128)(2,1)S(1)}, u32[]{:S(2)}, u32[]{:S(2)}) collective-permute-start(bf16[128,768]{1,0:T(8,128)(2,1)S(1)} %slice.309), channel_id=1, source_target_pairs={{0,2},{2,0},{1,3},{3,1},{4,6},{6,4},{5,7},{7,5},{8,10},{10,8},{9,1... | collective-permute-start | bytes 589832 | tf_op jit(solution)/shard_map/ppermute | solution.py:386
  221.1 19.6 %collective-permute-start.38 = (bf16[128,768]{1,0:T(8,128)(2,1)S(1)}, bf16[128,768]{1,0:T(8,128)(2,1)S(1)}, u32[]{:S(2)}, u32[]{:S(2)}) collective-permute-start(bf16[128,768]{1,0:T(8,128)(2,1)S(1)} %fusion.9), channel_id=1, source_target_pairs={{0,24},{8,16},{16,8},{24,0},{1,25},{9,17},{17,9},{25,1},{2,26},{10... | collective-permute-start | bytes 589832 | tf_op jit(solution)/shard_map/ppermute | solution.py:386
  244.5 39.3 %collective-permute-start.23 = (bf16[4,256,768]{2,1,0:T(8,128)(2,1)}, bf16[4,256,768]{2,1,0:T(8,128)(2,1)}, u32[]{:S(2)}, u32[]{:S(2)}) collective-permute-start(bf16[4,256,768]{2,1,0:T(8,128)(2,1)} %slice.208), channel_id=1, source_target_pairs={{0,1},{1,0},{2,3},{3,2},{4,5},{5,4},{6,7},{7,6},{8,9},{9,8},{10,11... | collective-permute-start | bytes 4718600 | tf_op jit(solution)/shard_map/ppermute | solution.py:386
  255.5 23.4 %all-to-all-start.3 = ((bf16[32,24,384]{2,1,0:T(8,128)(2,1)}), bf16[32,24,384]{2,1,0:T(8,128)(2,1)}, u32[]{:S(2)}, u32[]{:S(2)}) async-start(bf16[32,24,384]{2,1,0:T(8,128)(2,1)} %bitcast.33), calls=%async_computation.4 | async-start | bytes 1179648 | tf_op jit(solution)/shard_map/all_to_all | solution.py:812
  258.8 83.5 %reduce-scatter.2.cloned.1.call-start = ((), (), s32[]{:S(2)}) async-start(), calls=%async_computation.5 | async-start | bytes 331776 | tf_op jit(solution)/shard_map/reduce_scatter | solution.py:851
  259.1 32.3 %collective-permute-start.45 = (bf16[384,768]{1,0:T(8,128)(2,1)}, bf16[384,768]{1,0:T(8,128)(2,1)}, u32[]{:S(2)}, u32[]{:S(2)}) collective-permute-start(bf16[384,768]{1,0:T(8,128)(2,1)} %get-tuple-element.74), channel_id=1, source_target_pairs={{0,4},{4,0},{1,5},{5,1},{2,6},{6,2},{3,7},{7,3},{8,12},{12,8},{9,1... | collective-permute-start | bytes 1769480 | tf_op jit(solution)/shard_map/ppermute | solution.py:386
  278.9 91.2 %all-to-all-start.2 = ((bf16[32,32,576]{2,1,0:T(8,128)(2,1)}), bf16[32,32,576]{2,1,0:T(8,128)(2,1)S(1)}, u32[]{:S(2)}, u32[]{:S(2)}) async-start(bf16[32,32,576]{2,1,0:T(8,128)(2,1)} %pad_maximum_fusion.3), calls=%async_computation.2 | async-start | bytes 2621440 | tf_op jit(solution)/shard_map/all_to_all | solution.py:877
  287.0 57.2 %collective-permute-start.24 = (bf16[4,128,768]{2,1,0:T(8,128)(2,1)}, bf16[4,128,768]{2,1,0:T(8,128)(2,1)}, u32[]{:S(2)}, u32[]{:S(2)}) collective-permute-start(bf16[4,128,768]{2,1,0:T(8,128)(2,1)} %slice.303), channel_id=1, source_target_pairs={{0,2},{2,0},{1,3},{3,1},{4,6},{6,4},{5,7},{7,5},{8,10},{10,8},{9,1... | collective-permute-start | bytes 2359304 | tf_op jit(solution)/shard_map/ppermute | solution.py:386
  290.8 53.2 %collective-permute-start.42 = (bf16[128,768]{1,0:T(8,128)(2,1)S(1)}, bf16[128,768]{1,0:T(8,128)(2,1)S(1)}, u32[]{:S(2)}, u32[]{:S(2)}) collective-permute-start(bf16[128,768]{1,0:T(8,128)(2,1)S(1)} %slice.305), channel_id=1, source_target_pairs={{0,2},{2,0},{1,3},{3,1},{4,6},{6,4},{5,7},{7,5},{8,10},{10,8},{9,1... | collective-permute-start | bytes 589832 | tf_op jit(solution)/shard_map/ppermute | solution.py:386
  352.3 16.7 %collective-permute-start.26 = (bf16[128,768]{1,0:T(8,128)(2,1)S(1)}, bf16[128,768]{1,0:T(8,128)(2,1)S(1)}, u32[]{:S(2)}, u32[]{:S(2)}) collective-permute-start(bf16[128,768]{1,0:T(8,128)(2,1)S(1)} %get-tuple-element.90), channel_id=1, source_target_pairs={{0,16},{8,24},{16,0},{24,8},{1,17},{9,25},{17,1},{25,9},{2,18},{10... | collective-permute-start | bytes 589832 | tf_op jit(solution)/shard_map/ppermute | solution.py:386
  (85 other events, 1177.1 us)
Sparse Core Ops, SparseCore 0:
  277.7 64.5 reduce-scatter.1

commit v2 on v1

--- a/solution.py
+++ b/solution.py
@@ -1,3 +1,4 @@
+import functools
 import math
 
 import jax
@@ -377,8 +378,10 @@
 BF16 = jnp.bfloat16
 ROWS = 128
 EXT = 128
+TAB_AT = 256
 AXES = ("z", "y", "x", "c")
-VMEM_BYTES = 48 * 1024 * 1024
+MIB = 1024 * 1024
+BYTES_US = 3690000
 
 
 def swap(value, axis, step=1):
@@ -386,18 +389,19 @@
     return lax.ppermute(value, axis, [(i, i ^ step) for i in range(size)])
 
 
+def after(value, *earlier):
+    return lax.optimization_barrier((value, earlier))[0]
+
+
 def gather_seq(value):
-    pair = jnp.concatenate([value, swap(value, "x")], axis=0)
-    return jnp.concatenate([pair, swap(pair, "c")], axis=0)
-
-
-def reduce_seq(part):
-    half = part.shape[0] // 2
-    quarter = half // 2
-    got = swap(part[half:].astype(BF16), "c")
-    pair = part[:half].astype(F32) + got.astype(F32)
-    got_pair = swap(pair[quarter:].astype(BF16), "x")
-    return pair[:quarter] + got_pair.astype(F32)
+    along_x = swap(value, "x")
+    return value, along_x, swap(value, "c"), swap(along_x, "c")
+
+
+def reduce_seq(keep, send):
+    rows = keep.shape[0] // 2
+    pair = keep + swap(send, "c").astype(F32)
+    return pair[:rows] + swap(pair[rows:].astype(BF16), "x").astype(F32)
 
 
 def mm(a, b):
@@ -412,10 +416,12 @@
     return lax.dot_general(a, b, (((0,), (0,)), ((), ())), preferred_element_type=F32)
 
 
-def slot_rows(block, me):
-    mask = jnp.bitwise_xor(me, block)
-    slot = jnp.right_shift(mask, 1) + 2 * jnp.bitwise_and(mask, 1)
-    return pl.ds(pl.multiple_of(slot * ROWS, ROWS), ROWS)
+SLOTS = (0, 2, 1, 3)
+
+
+def slot_rows(slot, me):
+    block = jnp.bitwise_xor(me, SLOTS[slot])
+    return pl.ds(pl.multiple_of(block * ROWS, ROWS), ROWS)
 
 
 def tile_distance(offset):
@@ -436,10 +442,10 @@
             bias_ref[near * heads + h] = tiles[h]
 
 
-def read_marks(xs_ref, me, width, blocks):
+def read_marks(xs_ref, width, blocks):
     seg_cols, info_rows = [], []
     for i in range(blocks):
-        marks = xs_ref[slot_rows(i, me), width : width + EXT].astype(F32)
+        marks = xs_ref[i * ROWS : (i + 1) * ROWS, width : width + EXT].astype(F32)
         seg_cols.append(marks[:, 0:1])
         info_rows.append(marks.T[1:2, :])
     return seg_cols, info_rows
@@ -466,23 +472,55 @@
     return jnp.concatenate(tiles, axis=1) if len(tiles) > 1 else tiles[0]
 
 
+def copies(pairs, sem_ref):
+    return [pltpu.make_async_copy(a, b, sem_ref.at[n]) for n, (a, b) in enumerate(pairs)]
+
+
 def attend_kernel(
-    me_ref, tab_ref, xs_ref, gain_ref, wq_ref, n1_ref, qkv_ref, mixed_ref, lse_ref, bias_ref
+    me_ref,
+    place_ref,
+    tab_ref,
+    x0_ref,
+    x1_ref,
+    x2_ref,
+    x3_ref,
+    gain_ref,
+    *refs,
 ):
-    me = me_ref[0]
+    w_refs = refs[:2]
+    mixed_ref = refs[2]
+    home = refs[3:8]
+    kept = refs[8:13]
+    blocks_ref, bias_ref, sem_ref = refs[13:]
+    xs_ref, n1_ref, wq_ref, qkv_ref, lse_ref = kept
+    out = copies(zip(kept, home), sem_ref)
+    me, place = me_ref[0], place_ref[0]
     width = gain_ref.shape[1]
     third = wq_ref.shape[1] // 3
     heads = tab_ref.shape[0]
     size = third // heads
     blocks = xs_ref.shape[0] // ROWS
+    devices, shard = blocks_ref.shape[0], blocks_ref.shape[1]
     scale = size ** (-0.5)
     fill_bias(bias_ref, tab_ref, heads)
-    for i in range(blocks):
-        x = xs_ref[slot_rows(i, me), :width].astype(F32)
+    for slot, x_ref in enumerate((x0_ref, x1_ref, x2_ref, x3_ref)):
+        rows = slot_rows(slot, me)
+        xs_ref[rows, :] = x_ref[...]
+        x = x_ref[:, :width].astype(F32)
         factor = lax.rsqrt(jnp.mean(x * x, axis=-1, keepdims=True) + 1e-06)
-        n1_ref[i * ROWS : (i + 1) * ROWS, :] = (x * factor * gain_ref[...]).astype(BF16)
+        n1_ref[rows, :] = (x * factor * gain_ref[...]).astype(BF16)
+    out[0].start()
+    out[1].start()
+    for n, w_ref in enumerate(w_refs):
+        y = jnp.bitwise_xor(jnp.bitwise_and(place, 1), n)
+        for i in range(devices // 2):
+            blocks_ref[(2 * (i // blocks) + y) * blocks + i % blocks] = w_ref[i]
+    for i in range(devices):
+        wq_ref[i * shard : (i + 1) * shard, :] = blocks_ref[i]
+    out[2].start()
     qkv_ref[...] = mm(n1_ref[...], wq_ref[...]).astype(BF16)
-    seg_cols, info_rows = read_marks(xs_ref, me, width, blocks)
+    out[3].start()
+    seg_cols, info_rows = read_marks(xs_ref, width, blocks)
     lane = lax.broadcasted_iota(jnp.int32, (ROWS, EXT), 1)
     for i in range(blocks):
         masks = mask_tiles(i, seg_cols, info_rows)
@@ -501,31 +539,43 @@
             prob = (weight * (1.0 / total)).astype(BF16)
             outs.append(mm(prob, v))
             lse = jnp.where(lane == h, top + jnp.log(total), lse)
-        mixed_ref[slot_rows(i, me), :] = jnp.concatenate(outs, axis=1).astype(BF16)
+        mixed_ref[rows, :] = jnp.concatenate(outs, axis=1).astype(BF16)
         lse_ref[rows, :] = lse
+    out[4].start()
+    for copy in out:
+        copy.wait()
+
+
+def project_kernel(me_ref, mixed_ref, watt_ref, keep_ref, send_ref):
+    me = me_ref[0]
+    for slot in range(len(SLOTS)):
+        part = mm(mixed_ref[slot_rows(slot, me), :], watt_ref[...])
+        if slot < 2:
+            keep_ref[slot * ROWS : (slot + 1) * ROWS, :] = part
+        else:
+            send_ref[(slot - 2) * ROWS : (slot - 1) * ROWS, :] = part.astype(BF16)
 
 
 def attend_back_kernel(
     me_ref,
+    place_ref,
     tab_ref,
-    branch_ref,
+    b0_ref,
+    b1_ref,
+    b2_ref,
+    b3_ref,
     watt_ref,
-    qkv_ref,
-    n1_ref,
-    lse_ref,
-    xs_ref,
-    wq_ref,
-    mixed_ref,
-    gwq_ref,
-    gno_ref,
-    gain_ref,
-    gtab_ref,
-    gwatt_ref,
-    bias_ref,
-    dk_ref,
-    dv_ref,
-    proj_ref,
+    gain_two_ref,
+    *refs,
 ):
+    home = refs[:6]
+    wkeep_ref, wsend_ref, keep_ref, send_ref = refs[6:10]
+    kept = refs[10:16]
+    bias_ref, dm_ref, dk_ref, dv_ref, proj_ref, gtab_ref, small_ref, grad_ref, sem_ref = refs[16:]
+    xs_ref, n1_ref, wq_ref, qkv_ref, lse_ref, mixed_ref = kept
+    fetch = copies(zip(home, kept), sem_ref)
+    for copy in fetch:
+        copy.start()
     me = me_ref[0]
     width = watt_ref.shape[1]
     third = wq_ref.shape[1] // 3
@@ -534,7 +584,11 @@
     blocks = xs_ref.shape[0] // ROWS
     scale = size ** (-0.5)
     fill_bias(bias_ref, tab_ref, heads)
-    seg_cols, info_rows = read_marks(xs_ref, me, width, blocks)
+    for slot, b_ref in enumerate((b0_ref, b1_ref, b2_ref, b3_ref)):
+        dm_ref[slot_rows(slot, me), :] = mm_t(b_ref[...], watt_ref[...]).astype(BF16)
+    for copy in fetch:
+        copy.wait()
+    seg_cols, info_rows = read_marks(xs_ref, width, blocks)
     dk_ref[...] = jnp.zeros_like(dk_ref)
     dv_ref[...] = jnp.zeros_like(dv_ref)
     near = [[jnp.zeros((ROWS, ROWS), F32) for _ in range(heads)] for _ in range(2)]
@@ -543,13 +597,12 @@
         masks = mask_tiles(i, seg_cols, info_rows)
         span = (i + 1) * ROWS
         rows = slice(i * ROWS, span)
-        grad_mixed = mm_t(branch_ref[slot_rows(i, me), :], watt_ref[...]).astype(BF16)
         for h in range(heads):
             own = slice(h * size, (h + 1) * size)
             q = qkv_ref[rows, own]
             k = qkv_ref[0:span, third + h * size : third + (h + 1) * size]
             v = qkv_ref[0:span, 2 * third + h * size : 2 * third + (h + 1) * size]
-            dm = grad_mixed[:, own]
+            dm = dm_ref[rows, own]
             scores = mm_t(q, k) * scale + add_tiles(i, h, heads, masks, bias_ref, tab_ref)
             prob = jnp.exp(scores - lse_ref[rows, h : h + 1])
             grad_prob = mm_t(dm, v)
@@ -566,6 +619,7 @@
                     far[h] = far[h] + jnp.sum(tile, axis=0, keepdims=True)
     proj_ref[:, third : 2 * third] = (dk_ref[...] * scale).astype(BF16)
     proj_ref[:, 2 * third :] = dv_ref[...].astype(BF16)
+    gtab_ref[...] = jnp.zeros_like(gtab_ref)
     edges = [int(e) for e in bucket_edges()]
     buckets = []
     for n in range(2):
@@ -585,74 +639,321 @@
             if b == BUCKETS - 1:
                 line = line + far[h]
             gtab_ref[h * BUCKETS + b : h * BUCKETS + b + 1, :] = line
-    gwq_ref[...] = t_mm(n1_ref[...], proj_ref[...]).astype(BF16)
     gain = jnp.zeros((1, width), F32)
-    for i in range(blocks):
-        x = xs_ref[slot_rows(i, me), :width].astype(F32)
+    for slot in range(blocks):
+        rows = slot_rows(slot, me)
+        x = xs_ref[rows, :width].astype(F32)
         factor = lax.rsqrt(jnp.mean(x * x, axis=-1, keepdims=True) + 1e-06)
-        part = mm_t(proj_ref[i * ROWS : (i + 1) * ROWS, :], wq_ref[...])
-        gno_ref[slot_rows(i, me), :] = part.astype(BF16)
+        part = mm_t(proj_ref[rows, :], wq_ref[...])
+        if slot < 2:
+            keep_ref[slot * ROWS : (slot + 1) * ROWS, :] = part
+        else:
+            send_ref[(slot - 2) * ROWS : (slot - 1) * ROWS, :] = part.astype(BF16)
         gain = gain + jnp.sum(part * (x * factor), axis=0, keepdims=True)
-    gain_ref[...] = jnp.broadcast_to(gain, gain_ref.shape)
-    gwatt_ref[...] = t_mm(mixed_ref[...], branch_ref[...]).astype(BF16)
-
-
-def expert_kernel(x_ref, g_ref, w1_ref, w2_ref, pick_ref, dx_ref, act_ref, pre_ref, out_ref):
-    width = x_ref.shape[1]
+    wide = 3 * third
+    table = jnp.sum(gtab_ref[...].T, axis=0, keepdims=True)
+    small_ref[...] = jnp.zeros_like(small_ref)
+    for n, value in enumerate((gain, gain_two_ref[...])):
+        for m, piece in enumerate(halves(value)):
+            small_ref[4 * n + 2 * m : 4 * n + 2 * m + 1, :] = piece[:, :wide]
+            small_ref[4 * n + 2 * m + 1 : 4 * n + 2 * m + 2, : width - wide] = piece[:, wide:]
+    for m, piece in enumerate(halves(table)):
+        small_ref[2 * m + 1 : 2 * m + 2, TAB_AT : TAB_AT + EXT] = piece
+    small = small_ref[...].astype(BF16)
+    grad = t_mm(n1_ref[...], proj_ref[...])
+    att = 0.0
+    for slot, b_ref in enumerate((b0_ref, b1_ref, b2_ref, b3_ref)):
+        att = att + t_mm(mixed_ref[slot_rows(slot, me), :], b_ref[...])
+    groups, rows = grad_ref.shape[0], grad_ref.shape[1]
+    shard = third // groups
+    main = width // groups
+    for n in range(groups):
+        grad_ref[n, :main, :] = grad[n * main : (n + 1) * main, :]
+        piece = att[n * shard : (n + 1) * shard, :]
+        grad_ref[n, main : main + shard, :] = piece[:, :wide]
+        for m in range(3):
+            grad_ref[n, main + shard :, m * third : (m + 1) * third] = piece[
+                m * 8 : (m + 1) * 8, wide:
+            ]
+    own = jnp.bitwise_and(place_ref[0], 1)
+    for z in range(groups // 2):
+        wkeep_ref[z * rows : (z + 1) * rows, :] = grad_ref[2 * z + own]
+        wsend_ref[z * rows : (z + 1) * rows, :] = grad_ref[2 * z + 1 - own].astype(BF16)
+    wkeep_ref[groups // 2 * rows :, :] = small.astype(F32)
+    wsend_ref[groups // 2 * rows :, :] = small
+
+
+def halves(value):
+    high = value.astype(BF16).astype(F32)
+    return high, value - high
+
+
+def split_small(rows):
+    pieces = []
+    for n in range(2):
+        pieces += halves(rows[4 * n : 4 * n + 2] + rows[4 * n + 2 : 4 * n + 4])
+    return jnp.concatenate(pieces, axis=0).astype(BF16)
+
+
+def fold_y_kernel(place_ref, keep_ref, got_ref, own_ref, *refs):
+    sends, block_ref = refs[:-1], refs[-1]
+    count, rows = block_ref.shape[0], block_ref.shape[1]
+    total = keep_ref[...] + got_ref[...].astype(F32)
+    for z in range(count):
+        block_ref[z] = total[z * rows : (z + 1) * rows, :]
+    small = split_small(total[count * rows :, :])
+    me = jnp.right_shift(place_ref[0], 1)
+    own_ref[:rows, :] = block_ref[me]
+    own_ref[rows:, :] = small.astype(F32)
+    for k, send_ref in enumerate(sends):
+        send_ref[:rows, :] = block_ref[jnp.bitwise_xor(me, k + 1)].astype(BF16)
+        send_ref[rows:, :] = small
+
+
+def fold_z_kernel(me_ref, own_ref, *refs):
+    gots, att_ref, keep_ref, sends, block_ref = refs[:3], refs[3], refs[4], refs[5:-1], refs[-1]
+    count, shard, wide = block_ref.shape
+    third = wide // 3
+    total = (own_ref[...] + gots[0][...].astype(F32)) + (
+        gots[1][...].astype(F32) + gots[2][...].astype(F32)
+    )
+    for s in range(count):
+        block_ref[s] = total[s * shard : (s + 1) * shard, :]
+    main = count * shard
+    att_ref[:, :wide] = total[main : main + shard, :].astype(BF16)
+    rest = total[main + shard : main + shard + 8, :]
+    att_ref[:, wide:] = jnp.concatenate(
+        [rest[:, m * third : (m + 1) * third] for m in range(3)], axis=0
+    ).astype(BF16)
+    small = split_small(total[main + shard + 8 :, :])
+    keep_ref[:shard, :] = block_ref[me_ref[0]]
+    keep_ref[shard:, :] = small.astype(F32)
+    for k, send_ref in enumerate(sends):
+        send_ref[:shard, :] = block_ref[jnp.bitwise_xor(me_ref[0], SLOTS[k + 1])].astype(BF16)
+        send_ref[shard:, :] = small
+
+
+def fold_seq_kernel(me_ref, *refs):
+    pieces, gwq_ref, one_ref, two_ref, tab_ref, block_ref, table_ref = (
+        refs[:4],
+        *refs[4:],
+    )
+    parts, shard = block_ref.shape[0], block_ref.shape[1]
+    wide = block_ref.shape[2]
+    width = one_ref.shape[1]
+    third = wide // 3
+    values = [piece[...].astype(F32) for piece in pieces]
+    for slot, value in enumerate(values):
+        s = jnp.bitwise_xor(me_ref[0], SLOTS[slot])
+        block_ref[s] = value[:shard]
+        table_ref[s] = jnp.broadcast_to(
+            (value[shard + 1 : shard + 2] + value[shard + 3 : shard + 4])[
+                :, TAB_AT : TAB_AT + EXT
+            ],
+            (8, EXT),
+        )
+    for s in range(parts):
+        for n in range(3):
+            at = n * width + s * third
+            gwq_ref[:, at : at + third] = block_ref[s, :, n * third : (n + 1) * third]
+        tab_ref[s : s + 1, :] = table_ref[s, 0:1, :]
+    small = (values[0][shard:] + values[1][shard:]) + (values[2][shard:] + values[3][shard:])
+    for n, out_ref in enumerate((one_ref, two_ref)):
+        out_ref[:, :wide] = small[4 * n : 4 * n + 1] + small[4 * n + 2 : 4 * n + 3]
+        rest = small[4 * n + 1 : 4 * n + 2] + small[4 * n + 3 : 4 * n + 4]
+        out_ref[:, wide:] = rest[:, : width - wide]
+
+
+def qkv_send_kernel(w_ref, send_ref):
+    count, shard, wide = send_ref.shape
+    third = wide // 3
+    width = w_ref.shape[1] // 3
+    parts = width // third
+    for p in range(parts):
+        for n in range(3):
+            at = n * width + p * third
+            piece = w_ref[:, at : at + third]
+            for i in range(p, count, parts):
+                send_ref[i, :, n * third : (n + 1) * third] = piece
+
+
+def in_send_kernel(w_ref, send_ref):
+    devices, shard, wide = send_ref.shape
+    experts = w_ref.shape[0]
+    own = wide // experts
+    for i in range(devices):
+        for e in range(experts):
+            send_ref[i, :, e * own : (e + 1) * own] = w_ref[e, :, i * own : (i + 1) * own]
+
+
+def in_last_kernel(got_ref, grad_ref):
+    devices, shard, wide = got_ref.shape
+    experts = grad_ref.shape[0]
+    own = wide // experts
+    for i in range(devices):
+        for e in range(experts):
+            grad_ref[e, :, i * own : (i + 1) * own] = got_ref[
+                i, :, e * own : (e + 1) * own
+            ].astype(F32)
+
+
+def expert_kernel(
+    step,
+    place_ref,
+    xa_ref,
+    xb_ref,
+    g_all_ref,
+    w1a_ref,
+    w1b_ref,
+    w2a_ref,
+    w2b_ref,
+    pick_ref,
+    act_home,
+    pre_home,
+    keep_ref,
+    send_ref,
+    x_ref,
+    g_ref,
+    dx_ref,
+    act_ref,
+    pre_ref,
+    sem_ref,
+):
+    rows, width = xa_ref.shape
+    half = w1a_ref.shape[1]
+    tile_cols = 256
+    root = math.sqrt(2.0 / math.pi)
+    own, far = g_rows(step, place_ref[0])
+    fetch = copies(
+        [
+            (g_all_ref.at[own], g_ref.at[pl.ds(0, rows)]),
+            (g_all_ref.at[far], g_ref.at[pl.ds(rows, rows)]),
+        ],
+        sem_ref,
+    )
+    for copy in fetch:
+        copy.start()
+    x_ref[:rows, :] = xa_ref[...]
+    x_ref[rows:, :] = xb_ref[...]
+    dx_ref[...] = jnp.zeros_like(dx_ref)
+    for copy in fetch:
+        copy.wait()
+
+    def tile(t, carry):
+        cols = pl.ds(pl.multiple_of(t * tile_cols, tile_cols), tile_cols)
+        for side, (w1_ref, w2_ref) in enumerate(((w1a_ref, w2a_ref), (w1b_ref, w2b_ref))):
+            out_cols = pl.ds(pl.multiple_of(side * half + t * tile_cols, tile_cols), tile_cols)
+            choose = mm(g_ref[:, width:], pick_ref[:, cols])
+            v = mm(x_ref[...], w1_ref[:, cols])
+            square = v * v
+            curve = jnp.tanh(root * v * (1.0 + 0.044715 * square))
+            part = 0.5 * (1.0 + curve)
+            slope = part + 0.5 * v * (1.0 - curve * curve) * (
+                root * (1.0 + 3 * 0.044715 * square)
+            )
+            act_ref[:, out_cols] = (choose * (v * part)).astype(BF16)
+            grad_act = mm_t(g_ref[:, :width], w2_ref[cols, :])
+            grad_pre = (choose * grad_act * slope).astype(BF16)
+            pre_ref[:, out_cols] = grad_pre
+            dx_ref[...] += mm_t(grad_pre, w1_ref[:, cols])
+        return carry
+
+    lax.fori_loop(0, half // tile_cols, tile, 0)
+    home = copies([(act_ref, act_home), (pre_ref, pre_home)], sem_ref)
+    for copy in home:
+        copy.start()
+    keep_ref[...] = dx_ref[:rows, :]
+    send_ref[...] = dx_ref[rows:, :].astype(BF16)
+    for copy in home:
+        copy.wait()
+
+
+def g_rows(step, place):
+    own = jnp.bitwise_xor(place, 2 * step)
+    return own, jnp.bitwise_xor(own, 1)
+
+
+def expert_out_kernel(count, place_ref, w2a_ref, w2b_ref, *refs):
+    acts, keep_ref, send_ref, act_ref, sem_ref = refs[:count], *refs[count:]
+    rows = keep_ref.shape[1]
+    half = w2a_ref.shape[0]
+    fetch = copies([(act, act_ref.at[k]) for k, act in enumerate(acts)], sem_ref)
+    for copy in fetch:
+        copy.start()
+    for k in range(count):
+        fetch[k].wait()
+        out = mm(act_ref[k, :, :half], w2a_ref[...]) + mm(act_ref[k, :, half:], w2b_ref[...])
+        keep_ref[k] = out[:rows]
+        send_ref[k] = out[rows:].astype(BF16)
+
+
+def in_grad_kernel(count, *refs):
+    xs, pres = refs[: 2 * count], refs[2 * count : 3 * count]
+    own_ref, far_ref, xt_ref, pre_ref, sem_ref = refs[3 * count :]
+    rows = xs[0].shape[0]
+    half = own_ref.shape[1]
     step = 256
-    root = math.sqrt(2.0 / math.pi)
+    fetch = copies(
+        [(p, pre_ref.at[pl.ds(k * 2 * rows, 2 * rows)]) for k, p in enumerate(pres)], sem_ref
+    )
+    for copy in fetch:
+        copy.start()
+    for k in range(2 * count):
+        xt_ref[:, k * rows : (k + 1) * rows] = xs[k][...].T
+    for copy in fetch:
+        copy.wait()
 
     def tile(t, carry):
-        rows = pl.ds(pl.multiple_of(t * step, step), step)
-        choose = mm(g_ref[rows, width:], pick_ref[...])
-        v = mm(x_ref[rows, :], w1_ref[...])
-        square = v * v
-        curve = jnp.tanh(root * v * (1.0 + 0.044715 * square))
-        half = 0.5 * (1.0 + curve)
-        slope = half + 0.5 * v * (1.0 - curve * curve) * (root * (1.0 + 3 * 0.044715 * square))
-        act = (choose * (v * half)).astype(BF16)
-        act_ref[rows, :] = act
-        grad_act = mm_t(g_ref[rows, :width], w2_ref[...])
-        grad_pre = (choose * grad_act * slope).astype(BF16)
-        pre_ref[rows, :] = grad_pre
-        dx_ref[rows, :] = mm_t(grad_pre, w1_ref[...]).astype(BF16)
-        out_ref[rows, :] = mm(act, w2_ref[...]).astype(BF16)
+        cols = pl.ds(pl.multiple_of(t * step, step), step)
+        cols_far = pl.ds(pl.multiple_of(half + t * step, step), step)
+        far_ref[:, cols] = mm(xt_ref[...], pre_ref[:, cols_far]).astype(BF16)
+        own_ref[:, cols] = mm(xt_ref[...], pre_ref[:, cols])
         return carry
 
-    lax.fori_loop(0, x_ref.shape[0] // step, tile, 0)
-
-
-def weight_grad_kernel(count, *refs):
-    xs, gs, acts, pres = (refs[n * count : (n + 1) * count] for n in range(4))
-    own1_ref, far1_ref, own2_ref, far2_ref = refs[4 * count :]
-    width = xs[0].shape[1]
-    half = own1_ref.shape[1]
-    own1, far1, own2, far2 = 0.0, 0.0, 0.0, 0.0
-    for x, pre in zip(xs, pres):
-        own1 = own1 + t_mm(x[...], pre[:, :half])
-    own1_ref[...] = own1
-    for x, pre in zip(xs, pres):
-        far1 = far1 + t_mm(x[...], pre[:, half:])
-    far1_ref[...] = far1.astype(BF16)
-    for act, g in zip(acts, gs):
-        own2 = own2 + t_mm(act[:, :half], g[:, :width])
-    own2_ref[...] = own2
-    for act, g in zip(acts, gs):
-        far2 = far2 + t_mm(act[:, half:], g[:, :width])
-    far2_ref[...] = far2.astype(BF16)
-
-
-def call(kernel, outs, args, scratch=(), scalars=0, flops=0, moved=0, exps=0):
+    lax.fori_loop(0, half // step, tile, 0)
+
+
+def out_grad_kernel(count, place_ref, g_all_ref, *refs):
+    acts = refs[:count]
+    own_ref, far_ref, g_ref, act_ref, sem_ref = refs[count:]
+    rows = g_all_ref.shape[1]
+    half, width = own_ref.shape
+    step = 256
+    pairs = [(a, act_ref.at[pl.ds(k * 2 * rows, 2 * rows)]) for k, a in enumerate(acts)]
+    for k in range(count):
+        for m, place in enumerate(g_rows(k, place_ref[0])):
+            pairs.append((g_all_ref.at[place], g_ref.at[pl.ds((2 * k + m) * rows, rows)]))
+    fetch = copies(pairs, sem_ref)
+    for copy in fetch:
+        copy.start()
+    for copy in fetch:
+        copy.wait()
+
+    def tile(t, carry):
+        cols = pl.ds(pl.multiple_of(t * step, step), step)
+        cols_far = pl.ds(pl.multiple_of(half + t * step, step), step)
+        far_ref[cols, :] = t_mm(act_ref[:, cols_far], g_ref[:, :width]).astype(BF16)
+        own_ref[cols, :] = t_mm(act_ref[:, cols], g_ref[:, :width])
+        return carry
+
+    lax.fori_loop(0, half // step, tile, 0)
+
+
+def call(kernel, outs, args, us, scratch=(), scalars=0, far=(), home=(), mib=60):
     smem = pl.BlockSpec(memory_space=pltpu.SMEM)
     vmem = pl.BlockSpec(memory_space=pltpu.VMEM)
+    hbm = pl.BlockSpec(memory_space=pltpu.HBM)
     return pl.pallas_call(
         kernel,
         out_shape=[jax.ShapeDtypeStruct(shape, dtype) for shape, dtype in outs],
-        in_specs=[smem] * scalars + [vmem] * (len(args) - scalars),
-        out_specs=[vmem] * len(outs),
+        in_specs=[smem] * scalars
+        + [hbm if n in far else vmem for n in range(scalars, len(args))],
+        out_specs=[hbm if n in home else vmem for n in range(len(outs))],
         scratch_shapes=list(scratch),
-        compiler_params=pltpu.CompilerParams(vmem_limit_bytes=VMEM_BYTES),
-        cost_estimate=pl.CostEstimate(flops=flops, bytes_accessed=moved, transcendentals=exps),
+        compiler_params=pltpu.CompilerParams(vmem_limit_bytes=mib * MIB),
+        cost_estimate=pl.CostEstimate(
+            flops=0, bytes_accessed=int(us * BYTES_US), transcendentals=0
+        ),
     )(*args)
 
 
@@ -690,27 +991,51 @@
     info = jnp.where(pad_mask[0] == 1, seg, -1)
     marks = jnp.stack([seg, info], axis=1).astype(BF16)
     x_ext = jnp.concatenate([x_low, jnp.pad(marks, ((0, 0), (0, EXT - 2)))], axis=1)
-    xs = gather_seq(x_ext)
-
-    by_part = w_qkv.reshape(shard, 3, parts, third).transpose(2, 0, 1, 3)
-    by_part = by_part.reshape(1, parts, shard, 3 * third)
-    qkv_send = jnp.broadcast_to(by_part, (devices // parts, parts, shard, 3 * third))
-    wq = lax.all_to_all(
-        qkv_send.reshape(devices, shard, 3 * third), AXES, 0, 0, tiled=True
-    ).reshape(width, 3 * third)
-
-    in_send = w_expert_in.reshape(experts, shard, devices, ff_own).transpose(2, 1, 0, 3)
-    in_send = in_send.reshape(devices, shard, experts * ff_own)
-    in_send, wq = lax.optimization_barrier((in_send, wq))
+    x_slots = gather_seq(x_ext)
+
+    groups = devices // parts
+    across = [(i, i ^ 3) for i in range(parts)]
+    to_part = [((i % groups) * parts + i // groups) for i in range(devices)]
+    q_send = call(
+        qkv_send_kernel,
+        [((devices // 2, shard, 3 * third), BF16)],
+        [w_qkv],
+        us=1,
+        mib=8,
+    )[0]
+    q_own = lax.all_to_all(q_send, ("z", "x", "c"), 0, 0, tiled=True)
+
+    att_one = lax.ppermute(w_attn, AXES, [(i, to_part[i]) for i in range(devices)])
+    z_index = lax.axis_index("z")
+    y_index = lax.axis_index("y")
+    att_z = jnp.zeros((size_z, shard, width), BF16)
+    for k in range(size_z):
+        piece = att_one if k == 0 else swap(att_one, "z", k)
+        att_z = lax.dynamic_update_slice_in_dim(
+            att_z, piece[None], jnp.bitwise_xor(z_index, k), 0
+        )
+    att_y = swap(att_z, "y")
+    watt = jnp.where(
+        y_index == 0, jnp.stack([att_z, att_y], axis=1), jnp.stack([att_y, att_z], axis=1)
+    ).reshape(third, width)
+
+    w2_own = w_expert_out.reshape(experts * ff_own, width)
+    w2a = jnp.concatenate([w2_own, swap(w2_own, "x")], axis=0)
+    w2b = swap(w2a, "c")
+    q_own = after(q_own, watt, x_slots, w2a)
+    q_far = swap(q_own, "y")
+
+    in_send = call(
+        in_send_kernel,
+        [((devices, shard, experts * ff_own), BF16)],
+        [w_expert_in],
+        us=1.2,
+        mib=16,
+    )[0]
+    in_send = after(in_send, q_own)
     w1_own = lax.all_to_all(in_send, AXES, 0, 0, tiled=True).reshape(width, experts * ff_own)
-    w2_own = w_expert_out.reshape(experts * ff_own, width)
-    w1 = jnp.concatenate([w1_own, swap(w1_own, "y")], axis=1)
-    w2 = jnp.concatenate([w2_own, swap(w2_own, "y")], axis=0)
-
-    groups = devices // parts
-    to_part = [((i % groups) * parts + i // groups) for i in range(devices)]
-    att_one = lax.ppermute(w_attn, AXES, [(i, to_part[i]) for i in range(devices)])
-    watt = lax.all_gather(att_one, ("z", "y"), axis=0, tiled=True)
+
+    w1_x = swap(w1_own, "x")
 
     expert_ids = jnp.arange(experts, dtype=jnp.int32)
     choose = jnp.sum(
@@ -721,175 +1046,259 @@
     g_ext = jnp.concatenate(
         [g_low, choose_hi, choose_lo, jnp.zeros((rows, EXT - 2 * experts), BF16)], axis=1
     )
-    g_ext, wq = lax.optimization_barrier((g_ext, wq))
-    g_z = jnp.stack([g_ext] + [swap(g_ext, "z", k) for k in range(1, size_z)])
-    g_x = swap(g_z, "x")
-    g_zx = jnp.concatenate([g_z, g_x], axis=1)
-    g_c = swap(g_zx, "c")
-    g_all = jnp.concatenate([g_zx, g_c], axis=1)
+    g_all = lax.all_gather(g_ext, ("z", "y"), axis=0)
+    place_arr = lax.axis_index(("z", "y")).astype(jnp.int32).reshape(1)
 
     table = lax.dynamic_slice_in_dim(rel_table, me * heads, heads, 0).astype(F32)
-    n1, qkv, mixed, lse = call(
+    half = length // 2
+    kept = [
+        ((length, width + EXT), BF16),
+        ((length, width), BF16),
+        ((width, 3 * third), BF16),
+        ((length, 3 * third), BF16),
+        ((length, EXT), F32),
+    ]
+    kept_scratch = [pltpu.VMEM(shape, dtype) for shape, dtype in kept]
+    mixed, *saved = call(
         attend_kernel,
-        [
-            ((length, width), BF16),
-            ((length, 3 * third), BF16),
-            ((length, third), BF16),
-            ((length, EXT), F32),
+        [((length, third), BF16), *kept],
+        [me_arr, place_arr, table, *x_slots, gain_one.reshape(1, width), q_own, q_far],
+        scratch=[
+            *kept_scratch,
+            pltpu.VMEM((devices, shard, 3 * third), BF16),
+            pltpu.VMEM((2 * heads, ROWS, ROWS), F32),
+            pltpu.SemaphoreType.DMA((5,)),
         ],
-        [me_arr, table, xs, gain_one.reshape(1, width), wq],
-        scratch=[pltpu.VMEM((2 * heads, ROWS, ROWS), F32)],
-        scalars=2,
-        flops=2 * length * width * 3 * third + 4 * length * length * third,
-        moved=2 * length * width * 4,
-        exps=heads * length * length,
-    )
-    branch_part = mm(mixed, watt)
+        scalars=3,
+        home=range(1, 6),
+        us=8,
+        mib=60,
+    )
+    saved = [*saved, mixed]
+    keep, send = call(
+        project_kernel,
+        [((half, width), F32), ((half, width), BF16)],
+        [me_arr, mixed, watt],
+        scalars=1,
+        us=1,
+        mib=16,
+    )
     inputs = x_low.astype(F32)
-    hidden_one = inputs + reduce_seq(branch_part)
+    hidden_one = inputs + reduce_seq(keep, send)
     scaled_two, factor_two = norm_stats(hidden_one)
     normed_two = (scaled_two * gain_two).astype(BF16)
 
-    pick_np = np.zeros((EXT, 2 * experts * ff_own), np.float32)
-    for e in range(experts):
-        for y in range(2):
-            start = (y * experts + e) * ff_own
-            pick_np[[e, experts + e], start : start + ff_own] = 1.0
+    w1a = jnp.concatenate([after(w1_own, normed_two), w1_x], axis=1)
+    w1b = swap(w1a, "c")
+    ff_two = parts * experts * ff_own
+    pick_np = np.zeros((EXT, ff_two // 2), np.float32)
+    for col in range(ff_two // 2):
+        e = col // ff_own % experts
+        pick_np[[e, experts + e], col] = 1.0
     pick = jnp.asarray(pick_np, BF16)
-    ff_two = 2 * experts * ff_own
-    x_blocks, g_blocks, act_blocks, pre_blocks, out_blocks = [], [], [], [], []
-    grad_normed_two = None
+    pair = 2 * rows
+    x_own = [normed_two] + [swap(normed_two, "z", k) for k in range(1, size_z)]
+    x_far = [swap(x, "y") for x in x_own]
+    acts, pres, keeps, gots, backs = [], [], [], [], []
     for k in range(size_z):
-        x_block = gather_seq(normed_two if k == 0 else swap(normed_two, "z", k))
-        g_block = g_all[k]
-        dx, act, pre, out = call(
-            expert_kernel,
+        x_here = x_own[k] if k < 2 else after(x_own[k], backs[k - 2])
+        act, pre, dx_keep, dx_send = call(
+            functools.partial(expert_kernel, k),
             [
-                ((length, width), BF16),
-                ((length, ff_two), BF16),
-                ((length, ff_two), BF16),
-                ((length, width), BF16),
+                ((pair, ff_two), BF16),
+                ((pair, ff_two), BF16),
+                ((rows, width), F32),
+                ((rows, width), BF16),
             ],
-            [x_block, g_block, w1, w2, pick],
-            flops=8 * length * width * ff_two,
-            moved=2 * (6 * length * width + 2 * width * ff_two),
-            exps=length * ff_two,
+            [place_arr, x_here, x_far[k], g_all, w1a, w1b, w2a, w2b, pick],
+            scratch=[
+                pltpu.VMEM((pair, width), BF16),
+                pltpu.VMEM((pair, width + EXT), BF16),
+                pltpu.VMEM((pair, width), F32),
+                pltpu.VMEM((pair, ff_two), BF16),
+                pltpu.VMEM((pair, ff_two), BF16),
+                pltpu.SemaphoreType.DMA((2,)),
+            ],
+            far=(3,),
+            home=(0, 1),
+            mib=20,
+            scalars=1,
+        us=5.5,
         )
-        x_blocks.append(x_block)
-        g_blocks.append(g_block)
-        act_blocks.append(act)
-        pre_blocks.append(pre)
-        out_blocks.append(out)
-        back = reduce_seq(dx)
-        if k:
-            back = swap(back.astype(BF16), "z", k).astype(F32)
-        grad_normed_two = back if grad_normed_two is None else grad_normed_two + back
-
-    outs = jnp.stack(out_blocks)
-    half = length // 2
-    out_c = outs[:, :half].astype(F32) + swap(outs[:, half:], "c").astype(F32)
-    out_x = out_c[:, :rows] + swap(out_c[:, rows:].astype(BF16), "x").astype(F32)
-    combined = out_x[0]
+        acts.append(act)
+        pres.append(pre)
+        keeps.append(dx_keep)
+        gots.append(swap(dx_send, "y"))
+        if k + 1 < size_z:
+            backs.append(dx_keep + gots[k].astype(F32))
+
+    ff_half = ff_two // 2
+    backs.append(keeps[-1] + gots[-1].astype(F32))
+    in_own, in_far = call(
+        functools.partial(in_grad_kernel, size_z),
+        [((width, ff_half), F32), ((width, ff_half), BF16)],
+        [*[x for both in zip(x_own, x_far) for x in both], *pres[:-1], after(pres[-1], *backs)],
+        scratch=[
+            pltpu.VMEM((width, size_z * pair), BF16),
+            pltpu.VMEM((size_z * pair, ff_two), BF16),
+            pltpu.SemaphoreType.DMA((size_z,)),
+        ],
+        far=range(2 * size_z, 3 * size_z),
+        us=6,
+        mib=24,
+    )
+    out_keep, out_send = call(
+        functools.partial(expert_out_kernel, size_z),
+        [((size_z, rows, width), F32), ((size_z, rows, width), BF16)],
+        [place_arr, w2a, w2b, after(acts[0], in_far), *acts[1:]],
+        scratch=[
+            pltpu.VMEM((size_z, pair, ff_two), BF16),
+            pltpu.SemaphoreType.DMA((size_z,)),
+        ],
+        scalars=1,
+        far=range(3, 3 + size_z),
+        us=4.4,
+        mib=24,
+    )
+    grad_normed_two = after(backs[0], out_send)
     for k in range(1, size_z):
-        combined = combined + swap(out_x[k].astype(BF16), "z", k).astype(F32)
-    output = (hidden_one + combined).astype(BF16)
-
-    ff_half = experts * ff_own
-    own1, far1, own2, far2 = call(
-        lambda *refs: weight_grad_kernel(size_z, *refs),
-        [
-            ((width, ff_half), F32),
-            ((width, ff_half), BF16),
-            ((ff_half, width), F32),
-            ((ff_half, width), BF16),
-        ],
-        [*x_blocks, *g_blocks, *act_blocks, *pre_blocks],
-        flops=4 * size_z * length * width * ff_two,
-        moved=2 * 4 * size_z * length * width,
-    )
-    grad_w_out = (own2 + swap(far2, "y").astype(F32)).reshape(experts, ff_own, width)
-    in_sum = (own1 + swap(far1, "y").astype(F32)).astype(BF16)
-    in_got = lax.all_to_all(
-        in_sum.reshape(devices, shard, ff_half), AXES, 0, 0, tiled=True
-    )
-    grad_w_in = (
-        in_got.reshape(devices, shard, experts, ff_own)
-        .transpose(2, 1, 0, 3)
-        .reshape(experts, shard, ff)
-        .astype(F32)
-    )
+        grad_normed_two = grad_normed_two + swap(backs[k].astype(BF16), "z", k).astype(F32)
 
     grad_hidden_norm, gain_two_part = norm_back(grad_normed_two, scaled_two, factor_two, gain_two)
     grad_hidden = g_low.astype(F32) + grad_hidden_norm
-    branch = gather_seq(grad_hidden.astype(BF16))
-    gwq, gno, gain_one_part, table_part, gwatt = call(
+    branch_low = grad_hidden.astype(BF16)
+    branch = gather_seq(branch_low)
+
+    quarter = ff_half // 2
+    in_c = after(in_own, out_send) + swap(in_far, "c").astype(F32)
+    in_x_got = swap(in_c[:, quarter:].astype(BF16), "x")
+    out_y = out_keep + swap(out_send, "y").astype(F32)
+    extra = 8
+    wide = 3 * third
+    rows_y = parts * shard + shard * width // wide
+    w_keep, w_send, gno_keep, gno_send = call(
         attend_back_kernel,
         [
-            ((width, 3 * third), BF16),
-            ((length, width), BF16),
-            ((8, width), F32),
-            ((heads * BUCKETS, ROWS), F32),
-            ((third, width), BF16),
+            ((size_z * rows_y + extra, wide), F32),
+            ((size_z * rows_y + extra, wide), BF16),
+            ((half, width), F32),
+            ((half, width), BF16),
         ],
-        [me_arr, table, branch, watt, qkv, n1, lse, xs, wq, mixed],
+        [
+            me_arr,
+            place_arr,
+            table,
+            *branch,
+            watt,
+            after(gain_two_part.reshape(1, width), out_y, in_c),
+            *saved,
+        ],
         scratch=[
+            *kept_scratch,
+            pltpu.VMEM((length, third), BF16),
             pltpu.VMEM((2 * heads, ROWS, ROWS), F32),
+            pltpu.VMEM((length, third), BF16),
             pltpu.VMEM((length, third), F32),
             pltpu.VMEM((length, third), F32),
-            pltpu.VMEM((length, 3 * third), BF16),
+            pltpu.VMEM((length, wide), BF16),
+            pltpu.VMEM((EXT, ROWS), F32),
+            pltpu.VMEM((extra, wide), F32),
+            pltpu.VMEM((groups, rows_y, wide), F32),
+            pltpu.SemaphoreType.DMA((6,)),
         ],
-        scalars=2,
-        flops=6 * length * width * 3 * third + 10 * length * length * third,
-        moved=2 * length * width * 6,
-        exps=heads * length * length,
-    )
-    grad_normed_one = reduce_seq(gno)
+        scalars=3,
+        far=range(9, 15),
+        us=10,
+        mib=60,
+    )
+    in_x = after(in_c[:, :quarter], gno_send) + in_x_got.astype(F32)
+    in_x_low = in_x.astype(BF16).reshape(devices, shard, quarter)
+    in_got = lax.all_to_all(in_x_low, AXES, 0, 0, tiled=True)
+    combined = after(out_y[0], gno_send)
+    for k in range(1, size_z):
+        combined = combined + swap(out_y[k].astype(BF16), "z", k).astype(F32)
+    output = (hidden_one + combined).astype(BF16)
+    first_act = after(acts[0], gno_send)
+    out_own, out_far = call(
+        functools.partial(out_grad_kernel, size_z),
+        [((ff_half, width), F32), ((ff_half, width), BF16)],
+        [place_arr, g_all, first_act, *acts[1:]],
+        scratch=[
+            pltpu.VMEM((size_z * pair, width + EXT), BF16),
+            pltpu.VMEM((size_z * pair, ff_two), BF16),
+            pltpu.SemaphoreType.DMA((3 * size_z,)),
+        ],
+        far=range(1, 2 + size_z),
+        scalars=1,
+        us=6.5,
+        mib=24,
+    )
+    z_keep, *z_sends = call(
+        fold_y_kernel,
+        [((rows_y + extra, wide), F32)] + [((rows_y + extra, wide), BF16)] * (size_z - 1),
+        [place_arr, after(w_keep, out_far), swap(after(w_send, in_x_low, combined), "y")],
+        scratch=[pltpu.VMEM((size_z, rows_y, wide), F32)],
+        scalars=1,
+        mib=12,
+        us=1,
+    )
+    out_c = after(out_own, z_keep) + swap(out_far, "c").astype(F32)
+    out_x_got = swap(out_c[quarter:].astype(BF16), "x")
+    att_share, s_keep, *s_sends = call(
+        fold_z_kernel,
+        [((shard, width), BF16), ((shard + extra, wide), F32)]
+        + [((shard + extra, wide), BF16)] * (parts - 1),
+        [me_arr, after(z_keep, in_got), *[swap(piece, "z", k + 1) for k, piece in enumerate(z_sends)]],
+        scratch=[pltpu.VMEM((parts, shard, wide), F32)],
+        scalars=1,
+        mib=12,
+        us=1,
+    )
+    grad_w_qkv, one_sum, two_sum, table_sum = call(
+        fold_seq_kernel,
+        [
+            ((shard, 3 * width), F32),
+            ((1, width), F32),
+            ((1, width), F32),
+            ((parts, EXT), F32),
+        ],
+        [
+            me_arr,
+            s_keep,
+            swap(s_sends[0], "x"),
+            swap(s_sends[1], "c"),
+            lax.ppermute(s_sends[2], ("x", "c"), across),
+        ],
+        scratch=[
+            pltpu.VMEM((parts, shard, wide), F32),
+            pltpu.VMEM((parts, 8, EXT), F32),
+        ],
+        scalars=1,
+        mib=12,
+        us=1,
+    )
+
+    grad_normed_one = reduce_seq(after(gno_keep, z_keep), after(gno_send, z_keep))
     scaled_one, factor_one = norm_stats(inputs)
     grad_input_norm, unused_gain = norm_back(grad_normed_one, scaled_one, factor_one, gain_one)
     grad_inputs = grad_hidden + grad_input_norm
 
-    att_share = lax.psum_scatter(gwatt, ("z", "y"), scatter_dimension=0, tiled=True)
+    grad_w_in = call(
+        in_last_kernel, [((experts, shard, ff), F32)], [in_got], us=1.3, mib=16
+    )[0]
+    grad_w_out = (out_c[:quarter] + out_x_got.astype(F32)).reshape(experts, ff_own, width)
+
     grad_w_attn = lax.ppermute(
         att_share, AXES, [(to_part[i], i) for i in range(devices)]
     ).astype(F32)
-
-    small_table = lax.dynamic_update_slice_in_dim(
-        jnp.zeros((head_count, BUCKETS), F32),
-        jnp.sum(table_part, axis=1).reshape(heads, BUCKETS),
-        me * heads,
-        0,
-    )
-    small = jnp.concatenate([gain_one_part[0], gain_two_part, small_table.reshape(-1)])
-    small_hi = small.astype(BF16)
-    small_lo = (small - small_hi.astype(F32)).astype(BF16)
-    count = small.shape[0]
-    extra = -(-2 * count // (3 * third * 8)) * 8
-    small_rows = jnp.pad(
-        jnp.concatenate([small_hi, small_lo]), (0, extra * 3 * third - 2 * count)
-    ).reshape(1, extra, 3 * third)
-    last_send = jnp.concatenate(
-        [
-            gwq.reshape(devices, shard, 3 * third),
-            jnp.broadcast_to(small_rows, (devices, extra, 3 * third)),
-        ],
-        axis=1,
-    )
-    last = lax.all_to_all(last_send, AXES, 0, 0, tiled=True).astype(F32)
-    grad_w_qkv = (
-        jnp.sum(last[:, :shard].reshape(groups, parts, shard, 3, third), axis=0)
-        .transpose(1, 2, 0, 3)
-        .reshape(shard, 3 * width)
-    )
-    small_sum = jnp.sum(last[:, shard:], axis=0).reshape(-1)
-    totals = small_sum[:count] + small_sum[count : 2 * count]
     return (
         output[None],
         grad_inputs[None],
-        totals[:width],
+        one_sum[0],
         grad_w_qkv,
         grad_w_attn,
-        totals[2 * width :].reshape(head_count, BUCKETS),
-        totals[width : 2 * width],
+        table_sum[:, : heads * BUCKETS].reshape(head_count, BUCKETS),
+        two_sum[0],
         grad_w_in,
         grad_w_out,
     )

time: 395 us -> 290 us (0.73); the launches traced: 387 us -> 289 us
  waiting for transfers between devices: 149 us -> 88.8 us
  blocking collectives: 31.1 us -> 0 us
  Pallas kernels: 46.9 us -> 72.6 us
  local copies, waits for them, and re-layouts: 43.2 us -> 20.1 us
  other arithmetic: 36.8 us -> 19.1 us
  starting transfers between devices: 64.6 us -> 73.8 us
    reduce_scatter x1 -> x0, waiting for transfers between devices: 41.3 us -> none  [head_body(): lax.psum_scatter(gwatt, ('z', 'y'), scatter_dimension=0, tiled=True)]
    all_gather x1 -> x0, blocking collectives: 31.1 us -> none  [head_body(): watt = lax.all_gather(att_one, ('z', 'y'), axis=0, tiled=True)]
    pallas_call x7 -> x16, Pallas kernels: 46.9 us -> 72.6 us  [call(): pl.pallas_call(kernel, out_shape=[jax.ShapeDtypeStruct(shape, dtype) for...]
    ppermute x44 -> x47, waiting for transfers between devices: 107 us -> 82.6 us  [swap(): return lax.ppermute(value, axis, [(i, i ^ step) for i in range(size)])]
    ppermute x44 -> x47, starting transfers between devices: 41.9 us -> 61.1 us  [swap(): return lax.ppermute(value, axis, [(i, i ^ step) for i in range(size)])]
    concatenate x15 -> x1, other arithmetic: 17.6 us -> 1.3 us  [head_body(): w2a = jnp.concatenate([w2_own, swap(w2_own, 'x')], axis=0)]
    all_to_all x3 -> x2, starting transfers between devices: 15.5 us -> 7.04 us  [the longest x1 4.43 us: head_body(): q_own = lax.all_to_all(q_send, ('z', 'x', 'c'), 0, 0, tiled=True)]
    convert_element_type x4 -> x1, local copies, waits for them, and re-layouts: 7.44 us -> 0.82 us  [head_body(): combined = combined + swap(out_y[k].astype(BF16), 'z', k).astype(F32)]
  transfers between devices with their start and end apart: 51 -> 54, of which waited for: 17 -> 17; matrix products, arithmetic and copies ran while one was open for 14% -> 7% of each run, Pallas kernels for 9% -> 25%
where the time goes in v2:
time: 290 us; the launch traced here: 289 us
  waiting for transfers between devices  88.8 us (31%)
  starting transfers between devices  73.8 us (25%)
  Pallas kernels  72.6 us (25%)
  local copies, waits for them, and re-layouts  20.1 us (7%)
  other arithmetic  19.1 us (7%)
  between operations  14.9 us (5%)
    ppermute x47, waiting for transfers between devices, swap(): return lax.ppermute(value, axis, [(i, i ^ step) for i in range(size)])  82.6 us
    pallas_call x16, Pallas kernels, call(): pl.pallas_call(kernel, out_shape=[jax.ShapeDtypeStruct(shape, dtype) for...  72.6 us
    ppermute x47, starting transfers between devices, swap(): return lax.ppermute(value, axis, [(i, i ^ step) for i in range(size)])  61.1 us
    unnamed x107, local copies, waits for them, and re-layouts  13.8 us
    all_to_all x1, waiting for transfers between devices, head_body(): in_got = lax.all_to_all(in_x_low, AXES, 0, 0, tiled=True)  6.11 us
  transfers between devices with their start and end apart: 54, of which 17 were waited for; matrix products, arithmetic and copies ran while one was open for 7% of the time, Pallas kernels for 25%

profile of v2, /device:TPU:0, one launch (start us, length us, event | category | flops | bytes accessed | tf_op | source)
XLA Modules:
  0.0 289.3 jit_solution(6565377892367675524)
XLA Ops:
  10.5 5.0 %collective-permute-start = (bf16[128,896]{1,0:T(8,128)(2,1)S(1)}, bf16[128,896]{1,0:T(8,128)(2,1)S(1)}, u32[]{:S(2)}, u32[]{:S(2)}) collective-permute-start(bf16[128,896]{1,0:T(8,128)(2,1)S(1)} %fusion.10.x0_ref), channel_id=1, source_target_pairs={{0,2},{2,0},{1,3},{3,1},{4,6},{6,4},{5,7},{7,5},{8,10},{10,8},{9,1... | collective-permute-start | bytes 688136 | tf_op jit(solution)/shard_map/ppermute | solution.py:389
  17.3 4.4 %all-to-all-start = ((bf16[16,24,576]{2,1,0:T(8,128)(2,1)}), bf16[16,24,576]{2,1,0:T(8,128)(2,1)}, u32[]{:S(2)}, u32[]{:S(2)}) async-start(bf16[16,24,576]{2,1,0:T(8,128)(2,1)} %shard_map.205), calls=%async_computation | async-start | bytes 983040 | tf_op jit(solution)/shard_map/all_to_all | solution.py:1006
  28.2 4.9 %collective-permute-done.4 = bf16[24,768]{1,0:T(8,128)(2,1)S(1)} collective-permute-done((bf16[24,768]{1,0:T(8,128)(2,1)S(1)}, bf16[24,768]{1,0:T(8,128)(2,1)S(1)}, u32[]{:S(2)}, u32[]{:S(2)}) %collective-permute-start.4) | collective-permute-done | bytes 36896 | tf_op jit(solution)/shard_map/ppermute | solution.py:389
  33.1 6.4 %collective-permute-done.5 = bf16[24,768]{1,0:T(8,128)(2,1)S(1)} collective-permute-done((bf16[24,768]{1,0:T(8,128)(2,1)S(1)}, bf16[24,768]{1,0:T(8,128)(2,1)S(1)}, u32[]{:S(2)}, u32[]{:S(2)}) %collective-permute-start.5) | collective-permute-done | bytes 36896 | tf_op jit(solution)/shard_map/ppermute | solution.py:389
  51.7 3.3 %all-to-all-start.1 = ((bf16[32,24,384]{2,1,0:T(8,128)(2,1)}), bf16[32,24,384]{2,1,0:T(8,128)(2,1)S(1)}, u32[]{:S(2)}, u32[]{:S(2)}) async-start(bf16[32,24,384]{2,1,0:T(8,128)(2,1)} %shard_map.208), calls=%async_computation.1 | async-start | bytes 1179648 | tf_op jit(solution)/shard_map/all_to_all | solution.py:1036
  56.9 8.4 %collective-permute-done.9.refs_1_ = bf16[16,24,576]{2,1,0:T(8,128)(2,1)} collective-permute-done((bf16[16,24,576]{2,1,0:T(8,128)(2,1)}, bf16[16,24,576]{2,1,0:T(8,128)(2,1)}, u32[]{:S(2)}, u32[]{:S(2)}) %collective-permute-start.9) | collective-permute-done | bytes 442400 | tf_op jit(solution)/shard_map/ppermute | solution.py:389
  65.3 9.4 %shard_map.206 = (bf16[512,192]{1,0:T(8,128)(2,1)}, bf16[512,896]{1,0:T(8,128)(2,1)}, bf16[512,768]{1,0:T(8,128)(2,1)}, bf16[768,576]{1,0:T(8,128)(2,1)}, bf16[512,576]{1,0:T(8,128)(2,1)}, /*index=5*/f32[512,128]{1,0:T(8,128)}) custom-call(s32[1]{0:T(128)} %bitcast.1.me_ref, s32[1]{0:T(128)} %bitcast.2.place_ref, f32[3,32]{1,0:T(4,128)} %fusion.12.tab_ref, ...), custom_call_target="tpu_custom_call" | custom-call | bytes 29520000 | tf_op jit(solution)/shard_map/pallas_call | solution.py:946
  80.6 5.2 %collective-permute-done.11 = bf16[128,768]{1,0:T(8,128)(2,1)S(1)} collective-permute-done((bf16[128,768]{1,0:T(8,128)(2,1)S(1)}, bf16[128,768]{1,0:T(8,128)(2,1)S(1)}, u32[]{:S(2)}, u32[]{:S(2)}) %collective-permute-start.11) | collective-permute-done | bytes 196640 | tf_op jit(solution)/shard_map/ppermute | solution.py:389
  89.5 11.6 %collective-permute-done.14 = bf16[768,384]{1,0:T(8,128)(2,1)S(1)} collective-permute-done((bf16[768,384]{1,0:T(8,128)(2,1)S(1)}, bf16[768,384]{1,0:T(8,128)(2,1)S(1)}, u32[]{:S(2)}, u32[]{:S(2)}) %collective-permute-start.14) | collective-permute-done | bytes 589856 | tf_op jit(solution)/shard_map/ppermute | solution.py:389
  102.0 7.5 %collective-permute-done.16.xa_ref.refs_2_ = bf16[128,768]{1,0:T(8,128)(2,1)S(1)} collective-permute-done((bf16[128,768]{1,0:T(8,128)(2,1)}, bf16[128,768]{1,0:T(8,128)(2,1)S(1)}, u32[]{:S(2)}, u32[]{:S(2)}) %collective-permute-start.16) | collective-permute-done | bytes 196640 | tf_op jit(solution)/shard_map/ppermute | solution.py:389
  121.3 6.3 %shard_map.210 = (bf16[256,1536]{1,0:T(8,128)(2,1)S(1)}, bf16[256,1536]{1,0:T(8,128)(2,1)S(1)}, f32[128,768]{1,0:T(8,128)S(1)}, bf16[128,768]{1,0:T(8,128)(2,1)S(1)}) custom-call(s32[1]{0:T(128)} %bitcast.2.place_ref, bf16[128,768]{1,0:T(8,128)(2,1)S(1)} %copy-done.18, bf16[128,768]{1,0:T(8,128)(2,1)S(1)} %copy-done.21, bf16[8,128,896]{2,1,0:T(8,128)(2,1)S(1)} %bitcast.49, ...), custom_call_target="tpu_custom_call" | custom-call | bytes 20295000 | tf_op jit(solution)/shard_map/pallas_call | solution.py:946
  131.3 6.4 %shard_map.209 = (bf16[256,1536]{1,0:T(8,128)(2,1)S(1)}, bf16[256,1536]{1,0:T(8,128)(2,1)S(1)}, f32[128,768]{1,0:T(8,128)S(1)}, bf16[128,768]{1,0:T(8,128)(2,1)S(1)}) custom-call(s32[1]{0:T(128)} %bitcast.2.place_ref, bf16[128,768]{1,0:T(8,128)(2,1)} %multiply_convert_fusion.xa_ref.refs_0_, bf16[128,768]{1,0:T(8,128)(2,1)} %collective-permute-done.13.xb_ref.refs_1_, ...), custom_call_target="tpu_custom_call" | custom-call | bytes 20295000 | tf_op jit(solution)/shard_map/pallas_call | solution.py:946
  140.0 6.2 %shard_map.212 = (bf16[256,1536]{1,0:T(8,128)(2,1)S(1)}, bf16[256,1536]{1,0:T(8,128)(2,1)S(1)}, f32[128,768]{1,0:T(8,128)S(1)}, bf16[128,768]{1,0:T(8,128)(2,1)S(1)}) custom-call(s32[1]{0:T(128)} %bitcast.2.place_ref, bf16[128,768]{1,0:T(8,128)(2,1)} %collective-permute-done.20.xa_ref.refs_6_, bf16[128,768]{1,0:T(8,128)(2,1)S(1)} %collective-permute-done.21.xb_ref.refs_7_, ...), custom_call_target="tpu_custom_call" | custom-call | bytes 20295000 | tf_op jit(solution)/shard_map/pallas_call | solution.py:946
  147.6 6.2 %shard_map.211 = (bf16[256,1536]{1,0:T(8,128)(2,1)S(1)}, bf16[256,1536]{1,0:T(8,128)(2,1)S(1)}, f32[128,768]{1,0:T(8,128)S(1)}, bf16[128,768]{1,0:T(8,128)(2,1)S(1)}) custom-call(s32[1]{0:T(128)} %bitcast.2.place_ref, bf16[128,768]{1,0:T(8,128)(2,1)} %collective-permute-done.18.xa_ref.refs_4_, bf16[128,768]{1,0:T(8,128)(2,1)S(1)} %collective-permute-done.19.xb_ref.refs_5_, ...), custom_call_target="tpu_custom_call" | custom-call | bytes 20295000 | tf_op jit(solution)/shard_map/pallas_call | solution.py:946
  162.6 5.0 %shard_map.213 = (f32[768,768]{1,0:T(8,128)S(1)}, bf16[768,768]{1,0:T(8,128)(2,1)S(1)}) custom-call(bf16[128,768]{1,0:T(8,128)(2,1)} %multiply_convert_fusion.xa_ref.refs_0_, bf16[128,768]{1,0:T(8,128)(2,1)} %collective-permute-done.13.xb_ref.refs_1_, bf16[128,768]{1,0:T(8,128)(2,1)S(1)} %copy-done.19, bf16[128,768]{1,0:T(8,128)(2,1)S(1)} %copy-done.22, ...), custom_call_target="tpu_custom_call" | custom-call | bytes 22140000 | tf_op jit(solution)/shard_map/pallas_call | solution.py:946
  167.6 4.4 %shard_map.214 = (f32[4,128,768]{2,1,0:T(8,128)S(1)}, bf16[4,128,768]{2,1,0:T(8,128)(2,1)S(1)}) custom-call(s32[1]{0:T(128)} %bitcast.2.place_ref, bf16[768,768]{1,0:T(8,128)(2,1)S(1)} %pad_maximum_fusion.w2a_ref, bf16[768,768]{1,0:T(8,128)(2,1)S(1)} %copy-done.4, bf16[256,1536]{1,0:T(8,128)(2,1)S(1)} %get-tuple-element.117.refs_0_, ...), custom_call_target="tpu_custom_call" | custom-call | bytes 16236000 | tf_op jit(solution)/shard_map/pallas_call | solution.py:946
  175.3 5.3 %collective-permute-done.30.b1_ref = bf16[128,768]{1,0:T(8,128)(2,1)S(1)} collective-permute-done((bf16[128,768]{1,0:T(8,128)(2,1)S(1)}, bf16[128,768]{1,0:T(8,128)(2,1)S(1)}, u32[]{:S(2)}, u32[]{:S(2)}) %collective-permute-start.30) | collective-permute-done | bytes 196640 | tf_op jit(solution)/shard_map/ppermute | solution.py:389
  180.6 6.3 %collective-permute-done.26 = bf16[4,128,768]{2,1,0:T(8,128)(2,1)S(1)} collective-permute-done((bf16[4,128,768]{2,1,0:T(8,128)(2,1)S(1)}, bf16[4,128,768]{2,1,0:T(8,128)(2,1)S(1)}, u32[]{:S(2)}, u32[]{:S(2)}) %collective-permute-start.26) | collective-permute-done | bytes 786464 | tf_op jit(solution)/shard_map/ppermute | solution.py:389
  194.7 14.0 %shard_map.215 = (f32[520,576]{1,0:T(8,128)}, bf16[520,576]{1,0:T(8,128)(2,1)}, f32[256,768]{1,0:T(8,128)}, bf16[256,768]{1,0:T(8,128)(2,1)}) custom-call(s32[1]{0:T(128)} %bitcast.1.me_ref, s32[1]{0:T(128)} %bitcast.2.place_ref, f32[3,32]{1,0:T(4,128)} %fusion.12.tab_ref, bf16[128,768]{1,0:T(8,128)(2,1)} %copy-done.43, bf16[128,768]{1,0:T(8,128)(2,1)} %copy-done.46, ...), custom_call_target="tpu_custom_call" | custom-call | bytes 36900000 | tf_op jit(solution)/shard_map/pallas_call | solution.py:946
  213.8 6.8 %shard_map.216 = (f32[768,768]{1,0:T(8,128)S(1)}, bf16[768,768]{1,0:T(8,128)(2,1)}) custom-call(s32[1]{0:T(128)} %bitcast.2.place_ref, bf16[8,128,896]{2,1,0:T(8,128)(2,1)S(1)} %bitcast.53, bf16[256,1536]{1,0:T(8,128)(2,1)S(1)} %copy-done.7, bf16[256,1536]{1,0:T(8,128)(2,1)S(1)} %get-tuple-element.99.refs_1_, bf16[256,1536]{1,0:T(8,128)(2,1)S(1)} %copy-done.11, ...), custom_call_target="tpu_custom_call" | custom-call | bytes 23985000 | tf_op jit(solution)/shard_map/pallas_call | solution.py:946
  235.3 6.1 %all-to-all-done.2.got_ref = bf16[32,24,384]{2,1,0:T(8,128)(2,1)S(1)} async-done(((bf16[32,24,384]{2,1,0:T(8,128)(2,1)}), bf16[32,24,384]{2,1,0:T(8,128)(2,1)S(1)}, u32[]{:S(2)}, u32[]{:S(2)}) %all-to-all-start.2) | async-done | bytes 589856 | tf_op jit(solution)/shard_map/all_to_all | solution.py:1216
  241.4 11.3 %collective-permute-done.42.refs_1_ = bf16[136,576]{1,0:T(8,128)(2,1)} collective-permute-done((bf16[136,576]{1,0:T(8,128)(2,1)}, bf16[136,576]{1,0:T(8,128)(2,1)}, u32[]{:S(2)}, u32[]{:S(2)}) %collective-permute-start.42) | collective-permute-done | bytes 156704 | tf_op jit(solution)/shard_map/ppermute | solution.py:389
  254.6 6.3 %collective-permute-start.44 = (bf16[32,576]{1,0:T(8,128)(2,1)S(1)}, bf16[32,576]{1,0:T(8,128)(2,1)S(1)}, u32[]{:S(2)}, u32[]{:S(2)}) collective-permute-start(bf16[32,576]{1,0:T(8,128)(2,1)S(1)} %get-tuple-element.131), channel_id=1, source_target_pairs={{0,2},{2,0},{1,3},{3,1},{4,6},{6,4},{5,7},{7,5},{8,10},{10,8},{9,1... | collective-permute-start | bytes 110600 | tf_op jit(solution)/shard_map/ppermute | solution.py:389
  272.9 7.4 %collective-permute-done.49 = bf16[384,768]{1,0:T(8,128)(2,1)} collective-permute-done((bf16[384,768]{1,0:T(8,128)(2,1)S(1)}, bf16[384,768]{1,0:T(8,128)(2,1)}, u32[]{:S(2)}, u32[]{:S(2)}) %collective-permute-start.49) | collective-permute-done | bytes 589856 | tf_op jit(solution)/shard_map/ppermute | solution.py:389
  (264 shorter events, 110.3 us)
Async XLA Ops:
  7.2 16.6 %collective-permute-start.3 = (bf16[24,768]{1,0:T(8,128)(2,1)}, bf16[24,768]{1,0:T(8,128)(2,1)S(1)}, u32[]{:S(2)}, u32[]{:S(2)}) collective-permute-start(bf16[24,768]{1,0:T(8,128)(2,1)} %param.22), channel_id=1, source_target_pairs={{0,0},{1,4},{2,8},{3,12},{4,16},{5,20},{6,24},{7,28},{8,1},{9,5},{... | collective-permute-start | bytes 110600 | tf_op jit(solution)/shard_map/ppermute | solution.py:1008
  10.5 32.3 %collective-permute-start = (bf16[128,896]{1,0:T(8,128)(2,1)S(1)}, bf16[128,896]{1,0:T(8,128)(2,1)S(1)}, u32[]{:S(2)}, u32[]{:S(2)}) collective-permute-start(bf16[128,896]{1,0:T(8,128)(2,1)S(1)} %fusion.10.x0_ref), channel_id=1, source_target_pairs={{0,2},{2,0},{1,3},{3,1},{4,6},{6,4},{5,7},{7,5},{8,10},{10,8},{9,1... | collective-permute-start | bytes 688136 | tf_op jit(solution)/shard_map/ppermute | solution.py:389
  17.3 30.2 %all-to-all-start = ((bf16[16,24,576]{2,1,0:T(8,128)(2,1)}), bf16[16,24,576]{2,1,0:T(8,128)(2,1)}, u32[]{:S(2)}, u32[]{:S(2)}) async-start(bf16[16,24,576]{2,1,0:T(8,128)(2,1)} %shard_map.205), calls=%async_computation | async-start | bytes 983040 | tf_op jit(solution)/shard_map/all_to_all | solution.py:1006
  21.7 94.9 %all-gather.3.cloned.1.call-start = ((), (), s32[]{:S(2)}) async-start(), calls=%async_computation.3 | async-start | bytes 2064384 | tf_op jit(solution)/shard_map/all_gather | solution.py:1049
  21.8 24.3 %collective-permute-start.8 = (bf16[384,768]{1,0:T(8,128)(2,1)S(1)}, bf16[384,768]{1,0:T(8,128)(2,1)}, u32[]{:S(2)}, u32[]{:S(2)}) collective-permute-start(bf16[384,768]{1,0:T(8,128)(2,1)S(1)} %bitcast.63), channel_id=1, source_target_pairs={{0,2},{2,0},{1,3},{3,1},{4,6},{6,4},{5,7},{7,5},{8,10},{10,8},{9,1... | collective-permute-start | bytes 1769480 | tf_op jit(solution)/shard_map/ppermute | solution.py:389
  47.5 17.8 %collective-permute-start.9 = (bf16[16,24,576]{2,1,0:T(8,128)(2,1)}, bf16[16,24,576]{2,1,0:T(8,128)(2,1)}, u32[]{:S(2)}, u32[]{:S(2)}) collective-permute-start(bf16[16,24,576]{2,1,0:T(8,128)(2,1)} %all-to-all-done.refs_0_), channel_id=1, source_target_pairs={{0,4},{4,0},{1,5},{5,1},{2,6},{6,2},{3,7},{7,3},{8,12},{12,8},{9,1... | collective-permute-start | bytes 1327112 | tf_op jit(solution)/shard_map/ppermute | solution.py:389
  51.7 34.3 %all-to-all-start.1 = ((bf16[32,24,384]{2,1,0:T(8,128)(2,1)}), bf16[32,24,384]{2,1,0:T(8,128)(2,1)S(1)}, u32[]{:S(2)}, u32[]{:S(2)}) async-start(bf16[32,24,384]{2,1,0:T(8,128)(2,1)} %shard_map.208), calls=%async_computation.1 | async-start | bytes 1179648 | tf_op jit(solution)/shard_map/all_to_all | solution.py:1036
  80.6 33.8 %collective-permute-start.12 = (bf16[768,768]{1,0:T(8,128)(2,1)S(1)}, bf16[768,768]{1,0:T(8,128)(2,1)S(1)}, u32[]{:S(2)}, u32[]{:S(2)}) collective-permute-start(bf16[768,768]{1,0:T(8,128)(2,1)S(1)} %pad_maximum_fusion.w2a_ref), channel_id=1, source_target_pairs={{0,1},{1,0},{2,3},{3,2},{4,5},{5,4},{6,7},{7,6},{8,9},{9,8},{10,11... | collective-permute-start | bytes 3538952 | tf_op jit(solution)/shard_map/ppermute | solution.py:389
  111.2 18.0 %collective-permute-start.20 = (bf16[128,768]{1,0:T(8,128)(2,1)}, bf16[128,768]{1,0:T(8,128)(2,1)}, u32[]{:S(2)}, u32[]{:S(2)}) collective-permute-start(bf16[128,768]{1,0:T(8,128)(2,1)} %multiply_convert_fusion.xa_ref.refs_0_), channel_id=1, source_target_pairs={{0,24},{8,16},{16,8},{24,0},{1,25},{9,17},{17,9},{25,1},{2,26},{10... | collective-permute-start | bytes 589832 | tf_op jit(solution)/shard_map/ppermute | solution.py:389
  114.4 16.5 %collective-permute-start.18 = (bf16[128,768]{1,0:T(8,128)(2,1)}, bf16[128,768]{1,0:T(8,128)(2,1)}, u32[]{:S(2)}, u32[]{:S(2)}) collective-permute-start(bf16[128,768]{1,0:T(8,128)(2,1)} %multiply_convert_fusion.xa_ref.refs_0_), channel_id=1, source_target_pairs={{0,16},{8,24},{16,0},{24,8},{1,17},{9,25},{17,1},{25,9},{2,18},{10... | collective-permute-start | bytes 589832 | tf_op jit(solution)/shard_map/ppermute | solution.py:389
  115.4 15.9 %collective-permute-start.13 = (bf16[128,768]{1,0:T(8,128)(2,1)}, bf16[128,768]{1,0:T(8,128)(2,1)}, u32[]{:S(2)}, u32[]{:S(2)}) collective-permute-start(bf16[128,768]{1,0:T(8,128)(2,1)} %multiply_convert_fusion.xa_ref.refs_0_), channel_id=1, source_target_pairs={{0,4},{4,0},{1,5},{5,1},{2,6},{6,2},{3,7},{7,3},{8,12},{12,8},{9,1... | collective-permute-start | bytes 589832 | tf_op jit(solution)/shard_map/ppermute | solution.py:389
  130.9 16.7 %collective-permute-start.19 = (bf16[128,768]{1,0:T(8,128)(2,1)}, bf16[128,768]{1,0:T(8,128)(2,1)S(1)}, u32[]{:S(2)}, u32[]{:S(2)}) collective-permute-start(bf16[128,768]{1,0:T(8,128)(2,1)} %collective-permute-done.18.xa_ref.refs_4_), channel_id=1, source_target_pairs={{0,4},{4,0},{1,5},{5,1},{2,6},{6,2},{3,7},{7,3},{8,12},{12,8},{9,1... | collective-permute-start | bytes 589832 | tf_op jit(solution)/shard_map/ppermute | solution.py:389
  139.5 33.2 %collective-permute-start.27 = (bf16[128,768]{1,0:T(8,128)(2,1)S(1)}, bf16[128,768]{1,0:T(8,128)(2,1)S(1)}, u32[]{:S(2)}, u32[]{:S(2)}) collective-permute-start(bf16[128,768]{1,0:T(8,128)(2,1)S(1)} %convert_add_fusion.10), channel_id=1, source_target_pairs={{0,8},{8,0},{16,24},{24,16},{1,9},{9,1},{17,25},{25,17},{2,10},{10... | collective-permute-start | bytes 589832 | tf_op jit(solution)/shard_map/ppermute | solution.py:389
  154.7 18.0 %collective-permute-start.29 = (bf16[128,768]{1,0:T(8,128)(2,1)S(1)}, bf16[128,768]{1,0:T(8,128)(2,1)S(1)}, u32[]{:S(2)}, u32[]{:S(2)}) collective-permute-start(bf16[128,768]{1,0:T(8,128)(2,1)S(1)} %convert_add_fusion.8), channel_id=1, source_target_pairs={{0,24},{8,16},{16,8},{24,0},{1,25},{9,17},{17,9},{25,1},{2,26},{10... | collective-permute-start | bytes 589832 | tf_op jit(solution)/shard_map/ppermute | solution.py:389
  174.5 17.9 %collective-permute-start.31 = (bf16[128,768]{1,0:T(8,128)(2,1)S(1)}, bf16[128,768]{1,0:T(8,128)(2,1)S(1)}, u32[]{:S(2)}, u32[]{:S(2)}) collective-permute-start(bf16[128,768]{1,0:T(8,128)(2,1)S(1)} %fusion.15.b0_ref), channel_id=1, source_target_pairs={{0,1},{1,0},{2,3},{3,2},{4,5},{5,4},{6,7},{7,6},{8,9},{9,8},{10,11... | collective-permute-start | bytes 589832 | tf_op jit(solution)/shard_map/ppermute | solution.py:389
  188.5 21.1 %collective-permute-start.37 = (bf16[768,384]{1,0:T(8,128)(2,1)}, bf16[768,384]{1,0:T(8,128)(2,1)}, u32[]{:S(2)}, u32[]{:S(2)}) collective-permute-start(bf16[768,384]{1,0:T(8,128)(2,1)} %slice.91), channel_id=1, source_target_pairs={{0,2},{2,0},{1,3},{3,1},{4,6},{6,4},{5,7},{7,5},{8,10},{10,8},{9,1... | collective-permute-start | bytes 1769480 | tf_op jit(solution)/shard_map/ppermute | solution.py:389
  190.5 18.3 %collective-permute-start.34 = (bf16[128,768]{1,0:T(8,128)(2,1)}, bf16[128,768]{1,0:T(8,128)(2,1)S(1)}, u32[]{:S(2)}, u32[]{:S(2)}) collective-permute-start(bf16[128,768]{1,0:T(8,128)(2,1)} %get-tuple-element.152), channel_id=1, source_target_pairs={{0,8},{8,0},{16,24},{24,16},{1,9},{9,1},{17,25},{25,17},{2,10},{10... | collective-permute-start | bytes 589832 | tf_op jit(solution)/shard_map/ppermute | solution.py:389
  191.2 17.5 %collective-permute-start.36 = (bf16[128,768]{1,0:T(8,128)(2,1)}, bf16[128,768]{1,0:T(8,128)(2,1)S(1)}, u32[]{:S(2)}, u32[]{:S(2)}) collective-permute-start(bf16[128,768]{1,0:T(8,128)(2,1)} %get-tuple-element.153), channel_id=1, source_target_pairs={{0,24},{8,16},{16,8},{24,0},{1,25},{9,17},{17,9},{25,1},{2,26},{10... | collective-permute-start | bytes 589832 | tf_op jit(solution)/shard_map/ppermute | solution.py:389
  192.3 16.4 %collective-permute-start.35 = (bf16[128,768]{1,0:T(8,128)(2,1)}, bf16[128,768]{1,0:T(8,128)(2,1)S(1)}, u32[]{:S(2)}, u32[]{:S(2)}) collective-permute-start(bf16[128,768]{1,0:T(8,128)(2,1)} %get-tuple-element.154), channel_id=1, source_target_pairs={{0,16},{8,24},{16,0},{24,8},{1,17},{9,25},{17,1},{25,9},{2,18},{10... | collective-permute-start | bytes 589832 | tf_op jit(solution)/shard_map/ppermute | solution.py:389
  221.9 39.0 %collective-permute-start.48 = (bf16[768,768]{1,0:T(8,128)(2,1)}, bf16[768,768]{1,0:T(8,128)(2,1)}, u32[]{:S(2)}, u32[]{:S(2)}) collective-permute-start(bf16[768,768]{1,0:T(8,128)(2,1)} %get-tuple-element.118), channel_id=1, source_target_pairs={{0,1},{1,0},{2,3},{3,2},{4,5},{5,4},{6,7},{7,6},{8,9},{9,8},{10,11... | collective-permute-start | bytes 3538952 | tf_op jit(solution)/shard_map/ppermute | solution.py:389
  221.9 19.5 %all-to-all-start.2 = ((bf16[32,24,384]{2,1,0:T(8,128)(2,1)}), bf16[32,24,384]{2,1,0:T(8,128)(2,1)S(1)}, u32[]{:S(2)}, u32[]{:S(2)}) async-start(bf16[32,24,384]{2,1,0:T(8,128)(2,1)} %bitcast.23), calls=%async_computation.2 | async-start | bytes 1179648 | tf_op jit(solution)/shard_map/all_to_all | solution.py:1216
  229.9 22.8 %collective-permute-start.42 = (bf16[136,576]{1,0:T(8,128)(2,1)}, bf16[136,576]{1,0:T(8,128)(2,1)}, u32[]{:S(2)}, u32[]{:S(2)}) collective-permute-start(bf16[136,576]{1,0:T(8,128)(2,1)} %get-tuple-element.128), channel_id=1, source_target_pairs={{0,16},{8,24},{16,0},{24,8},{1,17},{9,25},{17,1},{25,9},{2,18},{10... | collective-permute-start | bytes 470024 | tf_op jit(solution)/shard_map/ppermute | solution.py:389
  232.4 20.3 %collective-permute-start.43 = (bf16[136,576]{1,0:T(8,128)(2,1)}, bf16[136,576]{1,0:T(8,128)(2,1)}, u32[]{:S(2)}, u32[]{:S(2)}) collective-permute-start(bf16[136,576]{1,0:T(8,128)(2,1)} %get-tuple-element.129), channel_id=1, source_target_pairs={{0,24},{8,16},{16,8},{24,0},{1,25},{9,17},{17,9},{25,1},{2,26},{10... | collective-permute-start | bytes 470024 | tf_op jit(solution)/shard_map/ppermute | solution.py:389
  233.7 36.0 %collective-permute-start.40 = (bf16[128,768]{1,0:T(8,128)(2,1)}, bf16[128,768]{1,0:T(8,128)(2,1)}, u32[]{:S(2)}, u32[]{:S(2)}) collective-permute-start(bf16[128,768]{1,0:T(8,128)(2,1)} %slice.92), channel_id=1, source_target_pairs={{0,2},{2,0},{1,3},{3,1},{4,6},{6,4},{5,7},{7,5},{8,10},{10,8},{9,1... | collective-permute-start | bytes 589832 | tf_op jit(solution)/shard_map/ppermute | solution.py:389
  (84 other events, 776.7 us)
Sparse Core Ops, SparseCore 0:
  50.6 50.8 all-gather.2

commit v3 on v2

--- a/solution.py
+++ b/solution.py
@@ -798,11 +798,10 @@
 
 
 def expert_kernel(
-    step,
-    place_ref,
     xa_ref,
     xb_ref,
-    g_all_ref,
+    ga_ref,
+    gb_ref,
     w1a_ref,
     w1b_ref,
     w2a_ref,
@@ -814,7 +813,6 @@
     send_ref,
     x_ref,
     g_ref,
-    dx_ref,
     act_ref,
     pre_ref,
     sem_ref,
@@ -823,21 +821,10 @@
     half = w1a_ref.shape[1]
     tile_cols = 256
     root = math.sqrt(2.0 / math.pi)
-    own, far = g_rows(step, place_ref[0])
-    fetch = copies(
-        [
-            (g_all_ref.at[own], g_ref.at[pl.ds(0, rows)]),
-            (g_all_ref.at[far], g_ref.at[pl.ds(rows, rows)]),
-        ],
-        sem_ref,
-    )
-    for copy in fetch:
-        copy.start()
     x_ref[:rows, :] = xa_ref[...]
     x_ref[rows:, :] = xb_ref[...]
-    dx_ref[...] = jnp.zeros_like(dx_ref)
-    for copy in fetch:
-        copy.wait()
+    g_ref[:rows, :] = ga_ref[...]
+    g_ref[rows:, :] = gb_ref[...]
 
     def tile(t, carry):
         cols = pl.ds(pl.multiple_of(t * tile_cols, tile_cols), tile_cols)
@@ -855,25 +842,20 @@
             grad_act = mm_t(g_ref[:, :width], w2_ref[cols, :])
             grad_pre = (choose * grad_act * slope).astype(BF16)
             pre_ref[:, out_cols] = grad_pre
-            dx_ref[...] += mm_t(grad_pre, w1_ref[:, cols])
         return carry
 
     lax.fori_loop(0, half // tile_cols, tile, 0)
     home = copies([(act_ref, act_home), (pre_ref, pre_home)], sem_ref)
     for copy in home:
         copy.start()
-    keep_ref[...] = dx_ref[:rows, :]
-    send_ref[...] = dx_ref[rows:, :].astype(BF16)
+    grad_x = mm_t(pre_ref[:, :half], w1a_ref[...]) + mm_t(pre_ref[:, half:], w1b_ref[...])
+    keep_ref[...] = grad_x[:rows, :]
+    send_ref[...] = grad_x[rows:, :].astype(BF16)
     for copy in home:
         copy.wait()
 
 
-def g_rows(step, place):
-    own = jnp.bitwise_xor(place, 2 * step)
-    return own, jnp.bitwise_xor(own, 1)
-
-
-def expert_out_kernel(count, place_ref, w2a_ref, w2b_ref, *refs):
+def expert_out_kernel(count, w2a_ref, w2b_ref, *refs):
     acts, keep_ref, send_ref, act_ref, sem_ref = refs[:count], *refs[count:]
     rows = keep_ref.shape[1]
     half = w2a_ref.shape[0]
@@ -913,16 +895,15 @@
     lax.fori_loop(0, half // step, tile, 0)
 
 
-def out_grad_kernel(count, place_ref, g_all_ref, *refs):
-    acts = refs[:count]
-    own_ref, far_ref, g_ref, act_ref, sem_ref = refs[count:]
-    rows = g_all_ref.shape[1]
+def out_grad_kernel(count, *refs):
+    gs, acts = refs[: 2 * count], refs[2 * count : 3 * count]
+    own_ref, far_ref, g_ref, act_ref, sem_ref = refs[3 * count :]
+    rows = gs[0].shape[0]
     half, width = own_ref.shape
     step = 256
     pairs = [(a, act_ref.at[pl.ds(k * 2 * rows, 2 * rows)]) for k, a in enumerate(acts)]
-    for k in range(count):
-        for m, place in enumerate(g_rows(k, place_ref[0])):
-            pairs.append((g_all_ref.at[place], g_ref.at[pl.ds((2 * k + m) * rows, rows)]))
+    for n, g in enumerate(gs):
+        pairs.append((g, g_ref.at[pl.ds(n * rows, rows)]))
     fetch = copies(pairs, sem_ref)
     for copy in fetch:
         copy.start()
@@ -996,6 +977,18 @@
     groups = devices // parts
     across = [(i, i ^ 3) for i in range(parts)]
     to_part = [((i % groups) * parts + i // groups) for i in range(devices)]
+    expert_ids = jnp.arange(experts, dtype=jnp.int32)
+    choose = jnp.sum(
+        gate_weights[0][:, :, None] * (routes[0][:, :, None] == expert_ids).astype(F32), axis=1
+    )
+    choose_hi = choose.astype(BF16)
+    choose_lo = (choose - choose_hi.astype(F32)).astype(BF16)
+    g_ext = jnp.concatenate(
+        [g_low, choose_hi, choose_lo, jnp.zeros((rows, EXT - 2 * experts), BF16)], axis=1
+    )
+    g_own = [g_ext] + [swap(g_ext, "z", k) for k in range(1, size_z)]
+    g_far = [swap(g, "y") for g in g_own]
+
     q_send = call(
         qkv_send_kernel,
         [((devices // 2, shard, 3 * third), BF16)],
@@ -1020,9 +1013,10 @@
     ).reshape(third, width)
 
     w2_own = w_expert_out.reshape(experts * ff_own, width)
-    w2a = jnp.concatenate([w2_own, swap(w2_own, "x")], axis=0)
+    w2_x = swap(w2_own, "x")
+    w2a = jnp.concatenate([w2_own, w2_x], axis=0)
     w2b = swap(w2a, "c")
-    q_own = after(q_own, watt, x_slots, w2a)
+    q_own = after(q_own, att_z, x_slots, w2_x)
     q_far = swap(q_own, "y")
 
     in_send = call(
@@ -1037,16 +1031,6 @@
 
     w1_x = swap(w1_own, "x")
 
-    expert_ids = jnp.arange(experts, dtype=jnp.int32)
-    choose = jnp.sum(
-        gate_weights[0][:, :, None] * (routes[0][:, :, None] == expert_ids).astype(F32), axis=1
-    )
-    choose_hi = choose.astype(BF16)
-    choose_lo = (choose - choose_hi.astype(F32)).astype(BF16)
-    g_ext = jnp.concatenate(
-        [g_low, choose_hi, choose_lo, jnp.zeros((rows, EXT - 2 * experts), BF16)], axis=1
-    )
-    g_all = lax.all_gather(g_ext, ("z", "y"), axis=0)
     place_arr = lax.axis_index(("z", "y")).astype(jnp.int32).reshape(1)
 
     table = lax.dynamic_slice_in_dim(rel_table, me * heads, heads, 0).astype(F32)
@@ -1078,18 +1062,16 @@
     keep, send = call(
         project_kernel,
         [((half, width), F32), ((half, width), BF16)],
-        [me_arr, mixed, watt],
+        [me_arr, after(mixed, g_own), watt],
         scalars=1,
         us=1,
         mib=16,
     )
     inputs = x_low.astype(F32)
-    hidden_one = inputs + reduce_seq(keep, send)
+    hidden_one = after(inputs, w1_own) + reduce_seq(keep, send)
     scaled_two, factor_two = norm_stats(hidden_one)
     normed_two = (scaled_two * gain_two).astype(BF16)
 
-    w1a = jnp.concatenate([after(w1_own, normed_two), w1_x], axis=1)
-    w1b = swap(w1a, "c")
     ff_two = parts * experts * ff_own
     pick_np = np.zeros((EXT, ff_two // 2), np.float32)
     for col in range(ff_two // 2):
@@ -1098,46 +1080,63 @@
     pick = jnp.asarray(pick_np, BF16)
     pair = 2 * rows
     x_own = [normed_two] + [swap(normed_two, "z", k) for k in range(1, size_z)]
-    x_far = [swap(x, "y") for x in x_own]
-    acts, pres, keeps, gots, backs = [], [], [], [], []
-    for k in range(size_z):
-        x_here = x_own[k] if k < 2 else after(x_own[k], backs[k - 2])
+    x_far = [swap(after(x, g_far, x_own[2]) if k == 1 else x, "y") for k, x in enumerate(x_own)]
+    w1a = jnp.concatenate([after(w1_own, x_far[1]), after(w1_x, x_far[1])], axis=1)
+    w1b = swap(w1a, "c")
+    order = [*range(1, size_z), 0]
+    acts, pres, keeps, gots, backs, far_back = {}, {}, {}, {}, {}, {}
+    for n, k in enumerate(order):
+        earlier = [acts[order[n - 1]]] if n else []
+        if n >= 2:
+            earlier.append(backs[order[n - 2]])
+        if n >= 3:
+            earlier.append(far_back[order[n - 3]])
+        x_here = after(x_own[k], *earlier)
         act, pre, dx_keep, dx_send = call(
-            functools.partial(expert_kernel, k),
+            expert_kernel,
             [
                 ((pair, ff_two), BF16),
                 ((pair, ff_two), BF16),
                 ((rows, width), F32),
                 ((rows, width), BF16),
             ],
-            [place_arr, x_here, x_far[k], g_all, w1a, w1b, w2a, w2b, pick],
+            [x_here, x_far[k], g_own[k], g_far[k], w1a, w1b, w2a, w2b, pick],
             scratch=[
                 pltpu.VMEM((pair, width), BF16),
                 pltpu.VMEM((pair, width + EXT), BF16),
-                pltpu.VMEM((pair, width), F32),
                 pltpu.VMEM((pair, ff_two), BF16),
                 pltpu.VMEM((pair, ff_two), BF16),
                 pltpu.SemaphoreType.DMA((2,)),
             ],
-            far=(3,),
             home=(0, 1),
             mib=20,
-            scalars=1,
         us=5.5,
         )
-        acts.append(act)
-        pres.append(pre)
-        keeps.append(dx_keep)
-        gots.append(swap(dx_send, "y"))
-        if k + 1 < size_z:
-            backs.append(dx_keep + gots[k].astype(F32))
+        acts[k], pres[k], keeps[k] = act, pre, dx_keep
+        gots[k] = swap(dx_send, "y")
+        backs[k] = dx_keep + gots[k].astype(F32)
+        if k:
+            far_back[k] = swap(backs[k].astype(BF16), "z", k)
+    acts, pres = [acts[k] for k in range(size_z)], [pres[k] for k in range(size_z)]
+    ready = [keeps[order[-1]], backs[order[-2]], far_back[order[-3]]]
 
     ff_half = ff_two // 2
-    backs.append(keeps[-1] + gots[-1].astype(F32))
+    out_keep, out_send = call(
+        functools.partial(expert_out_kernel, size_z),
+        [((size_z, rows, width), F32), ((size_z, rows, width), BF16)],
+        [w2a, w2b, after(acts[0], *ready), *acts[1:]],
+        scratch=[
+            pltpu.VMEM((size_z, pair, ff_two), BF16),
+            pltpu.SemaphoreType.DMA((size_z,)),
+        ],
+        far=range(2, 2 + size_z),
+        us=4.4,
+        mib=24,
+    )
     in_own, in_far = call(
         functools.partial(in_grad_kernel, size_z),
         [((width, ff_half), F32), ((width, ff_half), BF16)],
-        [*[x for both in zip(x_own, x_far) for x in both], *pres[:-1], after(pres[-1], *backs)],
+        [*[x for both in zip(x_own, x_far) for x in both], *pres[:-1], after(pres[-1], out_send)],
         scratch=[
             pltpu.VMEM((width, size_z * pair), BF16),
             pltpu.VMEM((size_z * pair, ff_two), BF16),
@@ -1147,22 +1146,9 @@
         us=6,
         mib=24,
     )
-    out_keep, out_send = call(
-        functools.partial(expert_out_kernel, size_z),
-        [((size_z, rows, width), F32), ((size_z, rows, width), BF16)],
-        [place_arr, w2a, w2b, after(acts[0], in_far), *acts[1:]],
-        scratch=[
-            pltpu.VMEM((size_z, pair, ff_two), BF16),
-            pltpu.SemaphoreType.DMA((size_z,)),
-        ],
-        scalars=1,
-        far=range(3, 3 + size_z),
-        us=4.4,
-        mib=24,
-    )
-    grad_normed_two = after(backs[0], out_send)
+    grad_normed_two = after(backs[0], in_far)
     for k in range(1, size_z):
-        grad_normed_two = grad_normed_two + swap(backs[k].astype(BF16), "z", k).astype(F32)
+        grad_normed_two = grad_normed_two + far_back[k].astype(F32)
 
     grad_hidden_norm, gain_two_part = norm_back(grad_normed_two, scaled_two, factor_two, gain_two)
     grad_hidden = g_low.astype(F32) + grad_hidden_norm
@@ -1170,8 +1156,8 @@
     branch = gather_seq(branch_low)
 
     quarter = ff_half // 2
-    in_c = after(in_own, out_send) + swap(in_far, "c").astype(F32)
-    in_x_got = swap(in_c[:, quarter:].astype(BF16), "x")
+    in_c = after(in_own, branch_low) + swap(in_far, "c").astype(F32)
+    in_x_got = swap(after(in_c[:, quarter:].astype(BF16), branch[1]), "x")
     out_y = out_keep + swap(out_send, "y").astype(F32)
     extra = 8
     wide = 3 * third
@@ -1211,44 +1197,45 @@
         us=10,
         mib=60,
     )
-    in_x = after(in_c[:, :quarter], gno_send) + in_x_got.astype(F32)
+    out_z = [swap(out_y[k].astype(BF16), "z", k) for k in range(1, size_z)]
+    w_send = after(w_send, in_x_got, out_z)
+    in_x = after(in_c[:, :quarter], w_send) + in_x_got.astype(F32)
     in_x_low = in_x.astype(BF16).reshape(devices, shard, quarter)
     in_got = lax.all_to_all(in_x_low, AXES, 0, 0, tiled=True)
-    combined = after(out_y[0], gno_send)
-    for k in range(1, size_z):
-        combined = combined + swap(out_y[k].astype(BF16), "z", k).astype(F32)
+    combined = after(out_y[0], w_send)
+    for got in out_z:
+        combined = combined + got.astype(F32)
     output = (hidden_one + combined).astype(BF16)
-    first_act = after(acts[0], gno_send)
+    first_act = after(acts[0], w_send)
     out_own, out_far = call(
         functools.partial(out_grad_kernel, size_z),
         [((ff_half, width), F32), ((ff_half, width), BF16)],
-        [place_arr, g_all, first_act, *acts[1:]],
+        [*[g for both in zip(g_own, g_far) for g in both], first_act, *acts[1:]],
         scratch=[
             pltpu.VMEM((size_z * pair, width + EXT), BF16),
             pltpu.VMEM((size_z * pair, ff_two), BF16),
             pltpu.SemaphoreType.DMA((3 * size_z,)),
         ],
-        far=range(1, 2 + size_z),
-        scalars=1,
+        far=range(3 * size_z),
         us=6.5,
         mib=24,
     )
     z_keep, *z_sends = call(
         fold_y_kernel,
         [((rows_y + extra, wide), F32)] + [((rows_y + extra, wide), BF16)] * (size_z - 1),
-        [place_arr, after(w_keep, out_far), swap(after(w_send, in_x_low, combined), "y")],
+        [place_arr, after(w_keep, out_far), swap(w_send, "y")],
         scratch=[pltpu.VMEM((size_z, rows_y, wide), F32)],
         scalars=1,
         mib=12,
         us=1,
     )
-    out_c = after(out_own, z_keep) + swap(out_far, "c").astype(F32)
+    out_c = out_own + swap(out_far, "c").astype(F32)
     out_x_got = swap(out_c[quarter:].astype(BF16), "x")
     att_share, s_keep, *s_sends = call(
         fold_z_kernel,
         [((shard, width), BF16), ((shard + extra, wide), F32)]
         + [((shard + extra, wide), BF16)] * (parts - 1),
-        [me_arr, after(z_keep, in_got), *[swap(piece, "z", k + 1) for k, piece in enumerate(z_sends)]],
+        [me_arr, after(z_keep, out_x_got), *[swap(piece, "z", k + 1) for k, piece in enumerate(z_sends)]],
         scratch=[pltpu.VMEM((parts, shard, wide), F32)],
         scalars=1,
         mib=12,

time: 290 us -> 260 us (0.90)
  waiting for transfers between devices: 88.8 us -> 58.3 us
  starting transfers between devices: 73.8 us -> 102 us
  between operations: 14.9 us -> 1.62 us
  Pallas kernels: 72.6 us -> 59.6 us
    ppermute x47 -> x54, waiting for transfers between devices: 82.6 us -> 51.8 us  [swap(): return lax.ppermute(value, axis, [(i, i ^ step) for i in range(size)])]
    ppermute x47 -> x54, starting transfers between devices: 61.1 us -> 85.9 us  [swap(): return lax.ppermute(value, axis, [(i, i ^ step) for i in range(size)])]
    pallas_call x16, Pallas kernels: 72.6 us -> 59.6 us  [call(): pl.pallas_call(kernel, out_shape=[jax.ShapeDtypeStruct(shape, dtype) for...]
    unnamed x107 -> x123, local copies, waits for them, and re-layouts: 13.8 us -> 10.3 us
  transfers between devices with their start and end apart: 54 -> 60, of which waited for: 17 -> 17; matrix products, arithmetic and copies ran while one was open for 7% -> 9% of each run, Pallas kernels for 25% -> 23%
where the time goes in v3:
time: 260 us; the launch traced here: 257 us
  starting transfers between devices  102 us (39%)
  Pallas kernels  59.6 us (23%)
  waiting for transfers between devices  58.3 us (22%)
  local copies, waits for them, and re-layouts  17.8 us (7%)
  other arithmetic  17.4 us (7%)
    ppermute x54, starting transfers between devices, swap(): return lax.ppermute(value, axis, [(i, i ^ step) for i in range(size)])  85.9 us
    pallas_call x16, Pallas kernels, call(): pl.pallas_call(kernel, out_shape=[jax.ShapeDtypeStruct(shape, dtype) for...  59.6 us
    ppermute x54, waiting for transfers between devices, swap(): return lax.ppermute(value, axis, [(i, i ^ step) for i in range(size)])  51.8 us
    unnamed x123, local copies, waits for them, and re-layouts  10.3 us
    all_to_all x1, starting transfers between devices, head_body(): lax.all_to_all(in_send, AXES, 0, 0, tiled=True)  5.61 us
    all_to_all x1, waiting for transfers between devices, head_body(): in_got = lax.all_to_all(in_x_low, AXES, 0, 0, tiled=True)  5.45 us
  transfers between devices with their start and end apart: 60, of which 17 were waited for; matrix products, arithmetic and copies ran while one was open for 9% of the time, Pallas kernels for 23%

profile of v3, /device:TPU:0, one launch (start us, length us, event | category | flops | bytes accessed | tf_op | source)
XLA Modules:
  0.0 256.7 jit_solution(2146564380000901304)
XLA Ops:
  7.3 5.1 %all-to-all-start = ((bf16[16,24,576]{2,1,0:T(8,128)(2,1)}), bf16[16,24,576]{2,1,0:T(8,128)(2,1)S(1)}, u32[]{:S(2)}, u32[]{:S(2)}) async-start(bf16[16,24,576]{2,1,0:T(8,128)(2,1)} %shard_map.206), calls=%async_computation | async-start | bytes 983040 | tf_op jit(solution)/shard_map/all_to_all | solution.py:999
  13.1 4.7 %collective-permute-start.7 = (bf16[384,768]{1,0:T(8,128)(2,1)S(1)}, bf16[384,768]{1,0:T(8,128)(2,1)S(1)}, u32[]{:S(2)}, u32[]{:S(2)}) collective-permute-start(bf16[384,768]{1,0:T(8,128)(2,1)S(1)} %bitcast.54), channel_id=1, source_target_pairs={{0,2},{2,0},{1,3},{3,1},{4,6},{6,4},{5,7},{7,5},{8,10},{10,8},{9,1... | collective-permute-start | bytes 1769480 | tf_op jit(solution)/shard_map/ppermute | solution.py:389
  19.4 6.3 %collective-permute-start.1 = (bf16[24,768]{1,0:T(8,128)(2,1)S(1)}, bf16[24,768]{1,0:T(8,128)(2,1)S(1)}, u32[]{:S(2)}, u32[]{:S(2)}) collective-permute-start(bf16[24,768]{1,0:T(8,128)(2,1)S(1)} %collective-permute-done), channel_id=1, source_target_pairs={{0,8},{8,0},{16,24},{24,16},{1,9},{9,1},{17,25},{25,17},{2,10},{10... | collective-permute-start | bytes 110600 | tf_op jit(solution)/shard_map/ppermute | solution.py:389
  37.8 5.6 %all-to-all-start.1 = ((bf16[32,24,384]{2,1,0:T(8,128)(2,1)}), bf16[32,24,384]{2,1,0:T(8,128)(2,1)}, u32[]{:S(2)}, u32[]{:S(2)}) async-start(bf16[32,24,384]{2,1,0:T(8,128)(2,1)} %shard_map.205), calls=%async_computation.1 | async-start | bytes 1179648 | tf_op jit(solution)/shard_map/all_to_all | solution.py:1030
  51.6 4.7 %collective-permute-done.8.refs_1_ = bf16[16,24,576]{2,1,0:T(8,128)(2,1)S(1)} collective-permute-done((bf16[16,24,576]{2,1,0:T(8,128)(2,1)S(1)}, bf16[16,24,576]{2,1,0:T(8,128)(2,1)S(1)}, u32[]{:S(2)}, u32[]{:S(2)}) %collective-permute-start.8) | collective-permute-done | bytes 442400 | tf_op jit(solution)/shard_map/ppermute | solution.py:389
  57.1 9.4 %shard_map.207 = (bf16[512,192]{1,0:T(8,128)(2,1)}, bf16[512,896]{1,0:T(8,128)(2,1)}, bf16[512,768]{1,0:T(8,128)(2,1)}, bf16[768,576]{1,0:T(8,128)(2,1)}, bf16[512,576]{1,0:T(8,128)(2,1)}, /*index=5*/f32[512,128]{1,0:T(8,128)}) custom-call(s32[1]{0:T(128)} %bitcast.9.me_ref, s32[1]{0:T(128)} %bitcast.10.place_ref, f32[3,32]{1,0:T(4,128)} %fusion.5.tab_ref, ...), custom_call_target="tpu_custom_call" | custom-call | bytes 29520000 | tf_op jit(solution)/shard_map/pallas_call | solution.py:927
  66.5 8.4 %collective-permute-done.10.ga_ref.refs_4_ = bf16[128,896]{1,0:T(8,128)(2,1)S(1)} collective-permute-done((bf16[128,896]{1,0:T(8,128)(2,1)S(1)}, bf16[128,896]{1,0:T(8,128)(2,1)S(1)}, u32[]{:S(2)}, u32[]{:S(2)}) %collective-permute-start.10) | collective-permute-done | bytes 229408 | tf_op jit(solution)/shard_map/ppermute | solution.py:389
  87.1 5.1 %collective-permute-start.17 = (bf16[128,768]{1,0:T(8,128)(2,1)S(1)}, bf16[128,768]{1,0:T(8,128)(2,1)S(1)}, u32[]{:S(2)}, u32[]{:S(2)}) collective-permute-start(bf16[128,768]{1,0:T(8,128)(2,1)S(1)} %multiply_convert_fusion.xa_ref.refs_0_), channel_id=1, source_target_pairs={{0,16},{8,24},{16,0},{24,8},{1,17},{9,25},{17,1},{25,9},{2,18},{10... | collective-permute-start | bytes 589832 | tf_op jit(solution)/shard_map/ppermute | solution.py:389
  94.8 4.4 %collective-permute-done.22.gb_ref.refs_7_ = bf16[128,896]{1,0:T(8,128)(2,1)S(1)} collective-permute-done((bf16[128,896]{1,0:T(8,128)(2,1)S(1)}, bf16[128,896]{1,0:T(8,128)(2,1)S(1)}, u32[]{:S(2)}, u32[]{:S(2)}) %collective-permute-start.22) | collective-permute-done | bytes 229408 | tf_op jit(solution)/shard_map/ppermute | solution.py:389
  102.8 4.0 %collective-permute-done.23.xb_ref.refs_3_ = bf16[128,768]{1,0:T(8,128)(2,1)S(1)} collective-permute-done((bf16[128,768]{1,0:T(8,128)(2,1)S(1)}, bf16[128,768]{1,0:T(8,128)(2,1)S(1)}, u32[]{:S(2)}, u32[]{:S(2)}) %collective-permute-start.23) | collective-permute-done | bytes 196640 | tf_op jit(solution)/shard_map/ppermute | solution.py:389
  112.1 3.5 %shard_map.209 = (bf16[256,1536]{1,0:T(8,128)(2,1)S(1)}, bf16[256,1536]{1,0:T(8,128)(2,1)S(1)}, f32[128,768]{1,0:T(8,128)S(1)}, bf16[128,768]{1,0:T(8,128)(2,1)S(1)}) custom-call(bf16[128,768]{1,0:T(8,128)(2,1)S(1)} %collective-permute-done.18.xa_ref.refs_2_, bf16[128,768]{1,0:T(8,128)(2,1)S(1)} %collective-permute-done.23.xb_ref.refs_3_, ...), custom_call_target="tpu_custom_call" | custom-call | bytes 20295000 | tf_op jit(solution)/shard_map/pallas_call | solution.py:927
  123.4 4.3 %collective-permute-start.30 = (bf16[128,768]{1,0:T(8,128)(2,1)S(1)}, bf16[128,768]{1,0:T(8,128)(2,1)S(1)}, u32[]{:S(2)}, u32[]{:S(2)}) collective-permute-start(bf16[128,768]{1,0:T(8,128)(2,1)S(1)} %convert_add_fusion.9), channel_id=1, source_target_pairs={{0,8},{8,0},{16,24},{24,16},{1,9},{9,1},{17,25},{25,17},{2,10},{10... | collective-permute-start | bytes 589832 | tf_op jit(solution)/shard_map/ppermute | solution.py:389
  127.7 4.1 %collective-permute-done.28.xb_ref.refs_7_ = bf16[128,768]{1,0:T(8,128)(2,1)S(1)} collective-permute-done((bf16[128,768]{1,0:T(8,128)(2,1)S(1)}, bf16[128,768]{1,0:T(8,128)(2,1)S(1)}, u32[]{:S(2)}, u32[]{:S(2)}) %collective-permute-start.28) | collective-permute-done | bytes 196640 | tf_op jit(solution)/shard_map/ppermute | solution.py:389
  131.8 3.4 %shard_map.211 = (bf16[256,1536]{1,0:T(8,128)(2,1)S(1)}, bf16[256,1536]{1,0:T(8,128)(2,1)S(1)}, f32[128,768]{1,0:T(8,128)S(1)}, bf16[128,768]{1,0:T(8,128)(2,1)S(1)}) custom-call(bf16[128,768]{1,0:T(8,128)(2,1)S(1)} %collective-permute-done.16.xa_ref.refs_6_, bf16[128,768]{1,0:T(8,128)(2,1)S(1)} %collective-permute-done.28.xb_ref.refs_7_, ...), custom_call_target="tpu_custom_call" | custom-call | bytes 20295000 | tf_op jit(solution)/shard_map/pallas_call | solution.py:927
  135.7 4.0 %collective-permute-start.33 = (bf16[128,768]{1,0:T(8,128)(2,1)S(1)}, bf16[128,768]{1,0:T(8,128)(2,1)S(1)}, u32[]{:S(2)}, u32[]{:S(2)}) collective-permute-start(bf16[128,768]{1,0:T(8,128)(2,1)S(1)} %convert_add_fusion.8), channel_id=1, source_target_pairs={{0,16},{8,24},{16,0},{24,8},{1,17},{9,25},{17,1},{25,9},{2,18},{10... | collective-permute-start | bytes 589832 | tf_op jit(solution)/shard_map/ppermute | solution.py:389
  139.7 3.6 %shard_map.212 = (bf16[256,1536]{1,0:T(8,128)(2,1)S(1)}, bf16[256,1536]{1,0:T(8,128)(2,1)S(1)}, f32[128,768]{1,0:T(8,128)S(1)}, bf16[128,768]{1,0:T(8,128)(2,1)S(1)}) custom-call(bf16[128,768]{1,0:T(8,128)(2,1)S(1)} %multiply_convert_fusion.xa_ref.refs_0_, bf16[128,768]{1,0:T(8,128)(2,1)S(1)} %collective-permute-done.31.xb_ref.refs_1_, ...), custom_call_target="tpu_custom_call" | custom-call | bytes 20295000 | tf_op jit(solution)/shard_map/pallas_call | solution.py:927
  146.5 6.3 %collective-permute-done.33 = bf16[128,768]{1,0:T(8,128)(2,1)S(1)} collective-permute-done((bf16[128,768]{1,0:T(8,128)(2,1)S(1)}, bf16[128,768]{1,0:T(8,128)(2,1)S(1)}, u32[]{:S(2)}, u32[]{:S(2)}) %collective-permute-start.33) | collective-permute-done | bytes 196640 | tf_op jit(solution)/shard_map/ppermute | solution.py:389
  152.7 4.2 %shard_map.213 = (f32[4,128,768]{2,1,0:T(8,128)S(1)}, bf16[4,128,768]{2,1,0:T(8,128)(2,1)S(1)}) custom-call(bf16[768,768]{1,0:T(8,128)(2,1)S(1)} %pad_maximum_fusion.w2a_ref, bf16[768,768]{1,0:T(8,128)(2,1)S(1)} %collective-permute-done.15.w2b_ref, bf16[256,1536]{1,0:T(8,128)(2,1)S(1)} %get-tuple-element.129.refs_0_.refs_8_, ...), custom_call_target="tpu_custom_call" | custom-call | bytes 16236000 | tf_op jit(solution)/shard_map/pallas_call | solution.py:927
  158.5 3.7 %shard_map.214 = (f32[768,768]{1,0:T(8,128)S(1)}, bf16[768,768]{1,0:T(8,128)(2,1)S(1)}) custom-call(bf16[128,768]{1,0:T(8,128)(2,1)S(1)} %multiply_convert_fusion.xa_ref.refs_0_, bf16[128,768]{1,0:T(8,128)(2,1)S(1)} %collective-permute-done.31.xb_ref.refs_1_, bf16[128,768]{1,0:T(8,128)(2,1)S(1)} %collective-permute-done.18.xa_ref.refs_2_, ...), custom_call_target="tpu_custom_call" | custom-call | bytes 22140000 | tf_op jit(solution)/shard_map/pallas_call | solution.py:927
  165.0 5.3 %collective-permute-done.37.b1_ref = bf16[128,768]{1,0:T(8,128)(2,1)S(1)} collective-permute-done((bf16[128,768]{1,0:T(8,128)(2,1)S(1)}, bf16[128,768]{1,0:T(8,128)(2,1)S(1)}, u32[]{:S(2)}, u32[]{:S(2)}) %collective-permute-start.37) | collective-permute-done | bytes 196640 | tf_op jit(solution)/shard_map/ppermute | solution.py:389
  181.3 14.0 %shard_map.215 = (f32[520,576]{1,0:T(8,128)}, bf16[520,576]{1,0:T(8,128)(2,1)}, f32[256,768]{1,0:T(8,128)}, bf16[256,768]{1,0:T(8,128)(2,1)}) custom-call(s32[1]{0:T(128)} %bitcast.9.me_ref, s32[1]{0:T(128)} %bitcast.10.place_ref, f32[3,32]{1,0:T(4,128)} %fusion.5.tab_ref, bf16[128,768]{1,0:T(8,128)(2,1)} %copy-done.37, bf16[128,768]{1,0:T(8,128)(2,1)} %copy-done.46, ...), custom_call_target="tpu_custom_call" | custom-call | bytes 36900000 | tf_op jit(solution)/shard_map/pallas_call | solution.py:927
  199.7 6.5 %shard_map.216 = (f32[768,768]{1,0:T(8,128)S(1)}, bf16[768,768]{1,0:T(8,128)(2,1)}) custom-call(bf16[128,896]{1,0:T(8,128)(2,1)S(1)} %maximum_maximum_fusion.ga_ref.refs_0_, bf16[128,896]{1,0:T(8,128)(2,1)S(1)} %copy-done.10, bf16[128,896]{1,0:T(8,128)(2,1)S(1)} %collective-permute-done.9.ga_ref.refs_2_, bf16[128,896]{1,0:T(8,128)(2,1)S(1)} %copy-done.12, ...), custom_call_target="tpu_custom_call" | custom-call | bytes 23985000 | tf_op jit(solution)/shard_map/pallas_call | solution.py:927
  223.4 5.5 %all-to-all-done.2.got_ref = bf16[32,24,384]{2,1,0:T(8,128)(2,1)S(1)} async-done(((bf16[32,24,384]{2,1,0:T(8,128)(2,1)}), bf16[32,24,384]{2,1,0:T(8,128)(2,1)S(1)}, u32[]{:S(2)}, u32[]{:S(2)}) %all-to-all-start.2) | async-done | bytes 589856 | tf_op jit(solution)/shard_map/all_to_all | solution.py:1204
  237.0 10.1 %collective-permute-done.49 = bf16[384,768]{1,0:T(8,128)(2,1)S(1)} collective-permute-done((bf16[384,768]{1,0:T(8,128)(2,1)S(1)}, bf16[384,768]{1,0:T(8,128)(2,1)S(1)}, u32[]{:S(2)}, u32[]{:S(2)}) %collective-permute-start.49) | collective-permute-done | bytes 589856 | tf_op jit(solution)/shard_map/ppermute | solution.py:389
  (292 shorter events, 118.9 us)
Async XLA Ops:
  2.5 29.9 %collective-permute-start.4 = (bf16[128,896]{1,0:T(8,128)(2,1)S(1)}, bf16[128,896]{1,0:T(8,128)(2,1)S(1)}, u32[]{:S(2)}, u32[]{:S(2)}) collective-permute-start(bf16[128,896]{1,0:T(8,128)(2,1)S(1)} %fusion.3.x0_ref), channel_id=1, source_target_pairs={{0,2},{2,0},{1,3},{3,1},{4,6},{6,4},{5,7},{7,5},{8,10},{10,8},{9,1... | collective-permute-start | bytes 688136 | tf_op jit(solution)/shard_map/ppermute | solution.py:389
  5.5 31.1 %collective-permute-start.5 = (bf16[128,896]{1,0:T(8,128)(2,1)S(1)}, bf16[128,896]{1,0:T(8,128)(2,1)S(1)}, u32[]{:S(2)}, u32[]{:S(2)}) collective-permute-start(bf16[128,896]{1,0:T(8,128)(2,1)S(1)} %fusion.3.x0_ref), channel_id=1, source_target_pairs={{0,1},{1,0},{2,3},{3,2},{4,5},{5,4},{6,7},{7,6},{8,9},{9,8},{10,11... | collective-permute-start | bytes 688136 | tf_op jit(solution)/shard_map/ppermute | solution.py:389
  7.3 30.1 %all-to-all-start = ((bf16[16,24,576]{2,1,0:T(8,128)(2,1)}), bf16[16,24,576]{2,1,0:T(8,128)(2,1)S(1)}, u32[]{:S(2)}, u32[]{:S(2)}) async-start(bf16[16,24,576]{2,1,0:T(8,128)(2,1)} %shard_map.206), calls=%async_computation | async-start | bytes 983040 | tf_op jit(solution)/shard_map/all_to_all | solution.py:999
  13.1 23.6 %collective-permute-start.7 = (bf16[384,768]{1,0:T(8,128)(2,1)S(1)}, bf16[384,768]{1,0:T(8,128)(2,1)S(1)}, u32[]{:S(2)}, u32[]{:S(2)}) collective-permute-start(bf16[384,768]{1,0:T(8,128)(2,1)S(1)} %bitcast.54), channel_id=1, source_target_pairs={{0,2},{2,0},{1,3},{3,1},{4,6},{6,4},{5,7},{7,5},{8,10},{10,8},{9,1... | collective-permute-start | bytes 1769480 | tf_op jit(solution)/shard_map/ppermute | solution.py:389
  37.4 18.9 %collective-permute-start.8 = (bf16[16,24,576]{2,1,0:T(8,128)(2,1)S(1)}, bf16[16,24,576]{2,1,0:T(8,128)(2,1)S(1)}, u32[]{:S(2)}, u32[]{:S(2)}) collective-permute-start(bf16[16,24,576]{2,1,0:T(8,128)(2,1)S(1)} %all-to-all-done.refs_0_), channel_id=1, source_target_pairs={{0,4},{4,0},{1,5},{5,1},{2,6},{6,2},{3,7},{7,3},{8,12},{12,8},{9,1... | collective-permute-start | bytes 1327112 | tf_op jit(solution)/shard_map/ppermute | solution.py:389
  37.8 45.6 %all-to-all-start.1 = ((bf16[32,24,384]{2,1,0:T(8,128)(2,1)}), bf16[32,24,384]{2,1,0:T(8,128)(2,1)}, u32[]{:S(2)}, u32[]{:S(2)}) async-start(bf16[32,24,384]{2,1,0:T(8,128)(2,1)} %shard_map.205), calls=%async_computation.1 | async-start | bytes 1179648 | tf_op jit(solution)/shard_map/all_to_all | solution.py:1030
  43.6 22.9 %collective-permute-start.9 = (bf16[128,896]{1,0:T(8,128)(2,1)S(1)}, bf16[128,896]{1,0:T(8,128)(2,1)S(1)}, u32[]{:S(2)}, u32[]{:S(2)}) collective-permute-start(bf16[128,896]{1,0:T(8,128)(2,1)S(1)} %maximum_maximum_fusion.ga_ref.refs_0_), channel_id=1, source_target_pairs={{0,8},{8,0},{16,24},{24,16},{1,9},{9,1},{17,25},{25,17},{2,10},{10... | collective-permute-start | bytes 688136 | tf_op jit(solution)/shard_map/ppermute | solution.py:389
  45.3 29.6 %collective-permute-start.10 = (bf16[128,896]{1,0:T(8,128)(2,1)S(1)}, bf16[128,896]{1,0:T(8,128)(2,1)S(1)}, u32[]{:S(2)}, u32[]{:S(2)}) collective-permute-start(bf16[128,896]{1,0:T(8,128)(2,1)S(1)} %maximum_maximum_fusion.ga_ref.refs_0_), channel_id=1, source_target_pairs={{0,16},{8,24},{16,0},{24,8},{1,17},{9,25},{17,1},{25,9},{2,18},{10... | collective-permute-start | bytes 688136 | tf_op jit(solution)/shard_map/ppermute | solution.py:389
  47.7 27.2 %collective-permute-start.11 = (bf16[128,896]{1,0:T(8,128)(2,1)S(1)}, bf16[128,896]{1,0:T(8,128)(2,1)S(1)}, u32[]{:S(2)}, u32[]{:S(2)}) collective-permute-start(bf16[128,896]{1,0:T(8,128)(2,1)S(1)} %maximum_maximum_fusion.ga_ref.refs_0_), channel_id=1, source_target_pairs={{0,24},{8,16},{16,8},{24,0},{1,25},{9,17},{17,9},{25,1},{2,26},{10... | collective-permute-start | bytes 688136 | tf_op jit(solution)/shard_map/ppermute | solution.py:389
  81.9 17.3 %collective-permute-start.22 = (bf16[128,896]{1,0:T(8,128)(2,1)S(1)}, bf16[128,896]{1,0:T(8,128)(2,1)S(1)}, u32[]{:S(2)}, u32[]{:S(2)}) collective-permute-start(bf16[128,896]{1,0:T(8,128)(2,1)S(1)} %collective-permute-done.11.ga_ref.refs_6_), channel_id=1, source_target_pairs={{0,4},{4,0},{1,5},{5,1},{2,6},{6,2},{3,7},{7,3},{8,12},{12,8},{9,1... | collective-permute-start | bytes 688136 | tf_op jit(solution)/shard_map/ppermute | solution.py:389
  85.3 22.7 %collective-permute-start.24 = (bf16[768,384]{1,0:T(8,128)(2,1)}, bf16[768,384]{1,0:T(8,128)(2,1)S(1)}, u32[]{:S(2)}, u32[]{:S(2)}) collective-permute-start(bf16[768,384]{1,0:T(8,128)(2,1)} %bitcast.8), channel_id=1, source_target_pairs={{0,2},{2,0},{1,3},{3,1},{4,6},{6,4},{5,7},{7,5},{8,10},{10,8},{9,1... | collective-permute-start | bytes 1769480 | tf_op jit(solution)/shard_map/ppermute | solution.py:389
  116.0 23.7 %collective-permute-start.31 = (bf16[128,768]{1,0:T(8,128)(2,1)S(1)}, bf16[128,768]{1,0:T(8,128)(2,1)S(1)}, u32[]{:S(2)}, u32[]{:S(2)}) collective-permute-start(bf16[128,768]{1,0:T(8,128)(2,1)S(1)} %multiply_convert_fusion.xa_ref.refs_0_), channel_id=1, source_target_pairs={{0,4},{4,0},{1,5},{5,1},{2,6},{6,2},{3,7},{7,3},{8,12},{12,8},{9,1... | collective-permute-start | bytes 589832 | tf_op jit(solution)/shard_map/ppermute | solution.py:389
  135.7 17.0 %collective-permute-start.33 = (bf16[128,768]{1,0:T(8,128)(2,1)S(1)}, bf16[128,768]{1,0:T(8,128)(2,1)S(1)}, u32[]{:S(2)}, u32[]{:S(2)}) collective-permute-start(bf16[128,768]{1,0:T(8,128)(2,1)S(1)} %convert_add_fusion.8), channel_id=1, source_target_pairs={{0,16},{8,24},{16,0},{24,8},{1,17},{9,25},{17,1},{25,9},{2,18},{10... | collective-permute-start | bytes 589832 | tf_op jit(solution)/shard_map/ppermute | solution.py:389
  143.4 19.0 %collective-permute-start.35 = (bf16[128,768]{1,0:T(8,128)(2,1)S(1)}, bf16[128,768]{1,0:T(8,128)(2,1)S(1)}, u32[]{:S(2)}, u32[]{:S(2)}) collective-permute-start(bf16[128,768]{1,0:T(8,128)(2,1)S(1)} %get-tuple-element.107), channel_id=1, source_target_pairs={{0,4},{4,0},{1,5},{5,1},{2,6},{6,2},{3,7},{7,3},{8,12},{12,8},{9,1... | collective-permute-start | bytes 589832 | tf_op jit(solution)/shard_map/ppermute | solution.py:389
  144.3 18.1 %collective-permute-start.36 = (bf16[128,768]{1,0:T(8,128)(2,1)S(1)}, bf16[128,768]{1,0:T(8,128)(2,1)S(1)}, u32[]{:S(2)}, u32[]{:S(2)}) collective-permute-start(bf16[128,768]{1,0:T(8,128)(2,1)S(1)} %convert_add_fusion.7), channel_id=1, source_target_pairs={{0,24},{8,16},{16,8},{24,0},{1,25},{9,17},{17,9},{25,1},{2,26},{10... | collective-permute-start | bytes 589832 | tf_op jit(solution)/shard_map/ppermute | solution.py:389
  171.9 23.5 %collective-permute-start.41 = (bf16[768,384]{1,0:T(8,128)(2,1)}, bf16[768,384]{1,0:T(8,128)(2,1)}, u32[]{:S(2)}, u32[]{:S(2)}) collective-permute-start(bf16[768,384]{1,0:T(8,128)(2,1)} %slice.91), channel_id=1, source_target_pairs={{0,2},{2,0},{1,3},{3,1},{4,6},{6,4},{5,7},{7,5},{8,10},{10,8},{9,1... | collective-permute-start | bytes 1769480 | tf_op jit(solution)/shard_map/ppermute | solution.py:389
  175.7 19.7 %collective-permute-start.42 = (bf16[128,768]{1,0:T(8,128)(2,1)}, bf16[128,768]{1,0:T(8,128)(2,1)}, u32[]{:S(2)}, u32[]{:S(2)}) collective-permute-start(bf16[128,768]{1,0:T(8,128)(2,1)} %get-tuple-element.160), channel_id=1, source_target_pairs={{0,8},{8,0},{16,24},{24,16},{1,9},{9,1},{17,25},{25,17},{2,10},{10... | collective-permute-start | bytes 589832 | tf_op jit(solution)/shard_map/ppermute | solution.py:389
  175.7 19.7 %collective-permute-start.43 = (bf16[128,768]{1,0:T(8,128)(2,1)}, bf16[128,768]{1,0:T(8,128)(2,1)}, u32[]{:S(2)}, u32[]{:S(2)}) collective-permute-start(bf16[128,768]{1,0:T(8,128)(2,1)} %get-tuple-element.162), channel_id=1, source_target_pairs={{0,16},{8,24},{16,0},{24,8},{1,17},{9,25},{17,1},{25,9},{2,18},{10... | collective-permute-start | bytes 589832 | tf_op jit(solution)/shard_map/ppermute | solution.py:389
  178.0 17.4 %collective-permute-start.44 = (bf16[128,768]{1,0:T(8,128)(2,1)}, bf16[128,768]{1,0:T(8,128)(2,1)}, u32[]{:S(2)}, u32[]{:S(2)}) collective-permute-start(bf16[128,768]{1,0:T(8,128)(2,1)} %get-tuple-element.161), channel_id=1, source_target_pairs={{0,24},{8,16},{16,8},{24,0},{1,25},{9,17},{17,9},{25,1},{2,26},{10... | collective-permute-start | bytes 589832 | tf_op jit(solution)/shard_map/ppermute | solution.py:389
  206.2 24.0 %collective-permute-start.48 = (bf16[768,768]{1,0:T(8,128)(2,1)}, bf16[768,768]{1,0:T(8,128)(2,1)}, u32[]{:S(2)}, u32[]{:S(2)}) collective-permute-start(bf16[768,768]{1,0:T(8,128)(2,1)} %get-tuple-element.130), channel_id=1, source_target_pairs={{0,1},{1,0},{2,3},{3,2},{4,5},{5,4},{6,7},{7,6},{8,9},{9,8},{10,11... | collective-permute-start | bytes 3538952 | tf_op jit(solution)/shard_map/ppermute | solution.py:389
  208.8 20.1 %all-to-all-start.2 = ((bf16[32,24,384]{2,1,0:T(8,128)(2,1)}), bf16[32,24,384]{2,1,0:T(8,128)(2,1)S(1)}, u32[]{:S(2)}, u32[]{:S(2)}) async-start(bf16[32,24,384]{2,1,0:T(8,128)(2,1)} %bitcast.23), calls=%async_computation.2 | async-start | bytes 1179648 | tf_op jit(solution)/shard_map/all_to_all | solution.py:1204
  216.3 30.8 %collective-permute-start.50 = (bf16[136,576]{1,0:T(8,128)(2,1)}, bf16[136,576]{1,0:T(8,128)(2,1)S(1)}, u32[]{:S(2)}, u32[]{:S(2)}) collective-permute-start(bf16[136,576]{1,0:T(8,128)(2,1)} %get-tuple-element.138), channel_id=1, source_target_pairs={{0,8},{8,0},{16,24},{24,16},{1,9},{9,1},{17,25},{25,17},{2,10},{10... | collective-permute-start | bytes 470024 | tf_op jit(solution)/shard_map/ppermute | solution.py:389
  218.0 29.1 %collective-permute-start.51 = (bf16[136,576]{1,0:T(8,128)(2,1)}, bf16[136,576]{1,0:T(8,128)(2,1)}, u32[]{:S(2)}, u32[]{:S(2)}) collective-permute-start(bf16[136,576]{1,0:T(8,128)(2,1)} %get-tuple-element.139), channel_id=1, source_target_pairs={{0,16},{8,24},{16,0},{24,8},{1,17},{9,25},{17,1},{25,9},{2,18},{10... | collective-permute-start | bytes 470024 | tf_op jit(solution)/shard_map/ppermute | solution.py:389
  220.4 26.7 %collective-permute-start.52 = (bf16[136,576]{1,0:T(8,128)(2,1)}, bf16[136,576]{1,0:T(8,128)(2,1)}, u32[]{:S(2)}, u32[]{:S(2)}) collective-permute-start(bf16[136,576]{1,0:T(8,128)(2,1)} %get-tuple-element.140), channel_id=1, source_target_pairs={{0,24},{8,16},{16,8},{24,0},{1,25},{9,17},{17,9},{25,1},{2,26},{10... | collective-permute-start | bytes 470024 | tf_op jit(solution)/shard_map/ppermute | solution.py:389
  (98 other events, 997.1 us)

commit v4 on v3

--- a/solution.py
+++ b/solution.py
@@ -1118,7 +1118,7 @@
         if k:
             far_back[k] = swap(backs[k].astype(BF16), "z", k)
     acts, pres = [acts[k] for k in range(size_z)], [pres[k] for k in range(size_z)]
-    ready = [keeps[order[-1]], backs[order[-2]], far_back[order[-3]]]
+    ready = [keeps[order[-1]], backs[order[-2]]]
 
     ff_half = ff_two // 2
     out_keep, out_send = call(
@@ -1271,7 +1271,7 @@
     grad_inputs = grad_hidden + grad_input_norm
 
     grad_w_in = call(
-        in_last_kernel, [((experts, shard, ff), F32)], [in_got], us=1.3, mib=16
+        in_last_kernel, [((experts, shard, ff), F32)], [after(in_got, out_c)], us=1.3, mib=16
     )[0]
     grad_w_out = (out_c[:quarter] + out_x_got.astype(F32)).reshape(experts, ff_own, width)
 

time: 260 us -> 249 us (0.958)
  waiting for transfers between devices: 58.3 us -> 49 us
  starting transfers between devices: 102 us -> 97.9 us
    ppermute x54, waiting for transfers between devices: 51.8 us -> 46.7 us  [swap(): return lax.ppermute(value, axis, [(i, i ^ step) for i in range(size)])]
    ppermute x54, starting transfers between devices: 85.9 us -> 82.2 us  [swap(): return lax.ppermute(value, axis, [(i, i ^ step) for i in range(size)])]
    all_to_all x1, waiting for transfers between devices: 5.45 us -> 2.35 us  [head_body(): in_got = lax.all_to_all(in_x_low, AXES, 0, 0, tiled=True)]
  transfers between devices with their start and end apart: 60 -> 60, of which waited for: 17 -> 14; matrix products, arithmetic and copies ran while one was open for 9% -> 10% of each run, Pallas kernels for 23% -> 24%
where the time goes in v4:
time: 249 us; the launch traced here: 245 us
  starting transfers between devices  97.9 us (39%)
  Pallas kernels  58 us (23%)
  waiting for transfers between devices  49 us (20%)
  local copies, waits for them, and re-layouts  19.7 us (8%)
  other arithmetic  18.9 us (8%)
    ppermute x54, starting transfers between devices, swap(): return lax.ppermute(value, axis, [(i, i ^ step) for i in range(size)])  82.2 us
    pallas_call x16, Pallas kernels, call(): pl.pallas_call(kernel, out_shape=[jax.ShapeDtypeStruct(shape, dtype) for...  58 us
    ppermute x54, waiting for transfers between devices, swap(): return lax.ppermute(value, axis, [(i, i ^ step) for i in range(size)])  46.7 us
    unnamed x123, local copies, waits for them, and re-layouts  10.6 us
    all_to_all x1, starting transfers between devices, head_body(): lax.all_to_all(in_send, AXES, 0, 0, tiled=True)  5.13 us
    all_to_all x1, starting transfers between devices, head_body(): q_own = lax.all_to_all(q_send, ('z', 'x', 'c'), 0, 0, tiled=True)  5.09 us
  transfers between devices with their start and end apart: 60, of which 14 were waited for; matrix products, arithmetic and copies ran while one was open for 10% of the time, Pallas kernels for 24%

profile of v4, /device:TPU:0, one launch (start us, length us, event | category | flops | bytes accessed | tf_op | source)
XLA Modules:
  0.0 245.1 jit_solution(3396704310628085066)
XLA Ops:
  7.3 5.1 %all-to-all-start = ((bf16[16,24,576]{2,1,0:T(8,128)(2,1)}), bf16[16,24,576]{2,1,0:T(8,128)(2,1)S(1)}, u32[]{:S(2)}, u32[]{:S(2)}) async-start(bf16[16,24,576]{2,1,0:T(8,128)(2,1)} %shard_map.206), calls=%async_computation | async-start | bytes 983040 | tf_op jit(solution)/shard_map/all_to_all | solution.py:999
  13.1 4.7 %collective-permute-start.7 = (bf16[384,768]{1,0:T(8,128)(2,1)S(1)}, bf16[384,768]{1,0:T(8,128)(2,1)S(1)}, u32[]{:S(2)}, u32[]{:S(2)}) collective-permute-start(bf16[384,768]{1,0:T(8,128)(2,1)S(1)} %bitcast.56), channel_id=1, source_target_pairs={{0,2},{2,0},{1,3},{3,1},{4,6},{6,4},{5,7},{7,5},{8,10},{10,8},{9,1... | collective-permute-start | bytes 1769480 | tf_op jit(solution)/shard_map/ppermute | solution.py:389
  19.4 6.3 %collective-permute-start.1 = (bf16[24,768]{1,0:T(8,128)(2,1)S(1)}, bf16[24,768]{1,0:T(8,128)(2,1)S(1)}, u32[]{:S(2)}, u32[]{:S(2)}) collective-permute-start(bf16[24,768]{1,0:T(8,128)(2,1)S(1)} %collective-permute-done), channel_id=1, source_target_pairs={{0,8},{8,0},{16,24},{24,16},{1,9},{9,1},{17,25},{25,17},{2,10},{10... | collective-permute-start | bytes 110600 | tf_op jit(solution)/shard_map/ppermute | solution.py:389
  29.1 3.4 %collective-permute-start.3 = (bf16[24,768]{1,0:T(8,128)(2,1)S(1)}, bf16[24,768]{1,0:T(8,128)(2,1)S(1)}, u32[]{:S(2)}, u32[]{:S(2)}) collective-permute-start(bf16[24,768]{1,0:T(8,128)(2,1)S(1)} %collective-permute-done), channel_id=1, source_target_pairs={{0,24},{8,16},{16,8},{24,0},{1,25},{9,17},{17,9},{25,1},{2,26},{10... | collective-permute-start | bytes 110600 | tf_op jit(solution)/shard_map/ppermute | solution.py:389
  37.6 5.1 %all-to-all-start.1 = ((bf16[32,24,384]{2,1,0:T(8,128)(2,1)}), bf16[32,24,384]{2,1,0:T(8,128)(2,1)S(1)}, u32[]{:S(2)}, u32[]{:S(2)}) async-start(bf16[32,24,384]{2,1,0:T(8,128)(2,1)} %shard_map.205), calls=%async_computation.1 | async-start | bytes 1179648 | tf_op jit(solution)/shard_map/all_to_all | solution.py:1030
  50.2 6.3 %collective-permute-done.8.refs_1_ = bf16[16,24,576]{2,1,0:T(8,128)(2,1)S(1)} collective-permute-done((bf16[16,24,576]{2,1,0:T(8,128)(2,1)S(1)}, bf16[16,24,576]{2,1,0:T(8,128)(2,1)S(1)}, u32[]{:S(2)}, u32[]{:S(2)}) %collective-permute-start.8) | collective-permute-done | bytes 442400 | tf_op jit(solution)/shard_map/ppermute | solution.py:389
  57.3 9.4 %shard_map.207 = (bf16[512,192]{1,0:T(8,128)(2,1)}, bf16[512,896]{1,0:T(8,128)(2,1)}, bf16[512,768]{1,0:T(8,128)(2,1)}, bf16[768,576]{1,0:T(8,128)(2,1)}, bf16[512,576]{1,0:T(8,128)(2,1)}, /*index=5*/f32[512,128]{1,0:T(8,128)}) custom-call(s32[1]{0:T(128)} %bitcast.9.me_ref, s32[1]{0:T(128)} %bitcast.10.place_ref, f32[3,32]{1,0:T(4,128)} %fusion.5.tab_ref, ...), custom_call_target="tpu_custom_call" | custom-call | bytes 29520000 | tf_op jit(solution)/shard_map/pallas_call | solution.py:927
  66.7 7.6 %collective-permute-done.10.ga_ref.refs_4_ = bf16[128,896]{1,0:T(8,128)(2,1)S(1)} collective-permute-done((bf16[128,896]{1,0:T(8,128)(2,1)S(1)}, bf16[128,896]{1,0:T(8,128)(2,1)S(1)}, u32[]{:S(2)}, u32[]{:S(2)}) %collective-permute-start.10) | collective-permute-done | bytes 229408 | tf_op jit(solution)/shard_map/ppermute | solution.py:389
  88.2 5.1 %collective-permute-start.17 = (bf16[128,768]{1,0:T(8,128)(2,1)S(1)}, bf16[128,768]{1,0:T(8,128)(2,1)S(1)}, u32[]{:S(2)}, u32[]{:S(2)}) collective-permute-start(bf16[128,768]{1,0:T(8,128)(2,1)S(1)} %multiply_convert_fusion.xa_ref.refs_0_), channel_id=1, source_target_pairs={{0,16},{8,24},{16,0},{24,8},{1,17},{9,25},{17,1},{25,9},{2,18},{10... | collective-permute-start | bytes 589832 | tf_op jit(solution)/shard_map/ppermute | solution.py:389
  94.2 4.4 %collective-permute-done.22.gb_ref.refs_7_ = bf16[128,896]{1,0:T(8,128)(2,1)S(1)} collective-permute-done((bf16[128,896]{1,0:T(8,128)(2,1)S(1)}, bf16[128,896]{1,0:T(8,128)(2,1)S(1)}, u32[]{:S(2)}, u32[]{:S(2)}) %collective-permute-start.22) | collective-permute-done | bytes 229408 | tf_op jit(solution)/shard_map/ppermute | solution.py:389
  103.3 4.0 %collective-permute-done.23.xb_ref.refs_3_ = bf16[128,768]{1,0:T(8,128)(2,1)S(1)} collective-permute-done((bf16[128,768]{1,0:T(8,128)(2,1)S(1)}, bf16[128,768]{1,0:T(8,128)(2,1)S(1)}, u32[]{:S(2)}, u32[]{:S(2)}) %collective-permute-start.23) | collective-permute-done | bytes 196640 | tf_op jit(solution)/shard_map/ppermute | solution.py:389
  111.7 3.5 %shard_map.209 = (bf16[256,1536]{1,0:T(8,128)(2,1)S(1)}, bf16[256,1536]{1,0:T(8,128)(2,1)S(1)}, f32[128,768]{1,0:T(8,128)S(1)}, bf16[128,768]{1,0:T(8,128)(2,1)S(1)}) custom-call(bf16[128,768]{1,0:T(8,128)(2,1)S(1)} %collective-permute-done.18.xa_ref.refs_2_, bf16[128,768]{1,0:T(8,128)(2,1)S(1)} %collective-permute-done.23.xb_ref.refs_3_, ...), custom_call_target="tpu_custom_call" | custom-call | bytes 20295000 | tf_op jit(solution)/shard_map/pallas_call | solution.py:927
  118.3 3.4 %shard_map.210 = (bf16[256,1536]{1,0:T(8,128)(2,1)S(1)}, bf16[256,1536]{1,0:T(8,128)(2,1)S(1)}, f32[128,768]{1,0:T(8,128)S(1)}, bf16[128,768]{1,0:T(8,128)(2,1)S(1)}) custom-call(bf16[128,768]{1,0:T(8,128)(2,1)S(1)} %collective-permute-done.17.xa_ref.refs_4_, bf16[128,768]{1,0:T(8,128)(2,1)S(1)} %collective-permute-done.26.xb_ref.refs_5_, ...), custom_call_target="tpu_custom_call" | custom-call | bytes 20295000 | tf_op jit(solution)/shard_map/pallas_call | solution.py:927
  123.1 4.0 %collective-permute-start.30 = (bf16[128,768]{1,0:T(8,128)(2,1)S(1)}, bf16[128,768]{1,0:T(8,128)(2,1)S(1)}, u32[]{:S(2)}, u32[]{:S(2)}) collective-permute-start(bf16[128,768]{1,0:T(8,128)(2,1)S(1)} %convert_add_fusion.9), channel_id=1, source_target_pairs={{0,8},{8,0},{16,24},{24,16},{1,9},{9,1},{17,25},{25,17},{2,10},{10... | collective-permute-start | bytes 589832 | tf_op jit(solution)/shard_map/ppermute | solution.py:389
  127.1 4.4 %collective-permute-done.28.xb_ref.refs_7_ = bf16[128,768]{1,0:T(8,128)(2,1)S(1)} collective-permute-done((bf16[128,768]{1,0:T(8,128)(2,1)S(1)}, bf16[128,768]{1,0:T(8,128)(2,1)S(1)}, u32[]{:S(2)}, u32[]{:S(2)}) %collective-permute-start.28) | collective-permute-done | bytes 196640 | tf_op jit(solution)/shard_map/ppermute | solution.py:389
  131.5 3.4 %shard_map.211 = (bf16[256,1536]{1,0:T(8,128)(2,1)S(1)}, bf16[256,1536]{1,0:T(8,128)(2,1)S(1)}, f32[128,768]{1,0:T(8,128)S(1)}, bf16[128,768]{1,0:T(8,128)(2,1)S(1)}) custom-call(bf16[128,768]{1,0:T(8,128)(2,1)S(1)} %collective-permute-done.16.xa_ref.refs_6_, bf16[128,768]{1,0:T(8,128)(2,1)S(1)} %collective-permute-done.28.xb_ref.refs_7_, ...), custom_call_target="tpu_custom_call" | custom-call | bytes 20295000 | tf_op jit(solution)/shard_map/pallas_call | solution.py:927
  138.1 3.6 %shard_map.212 = (bf16[256,1536]{1,0:T(8,128)(2,1)S(1)}, bf16[256,1536]{1,0:T(8,128)(2,1)S(1)}, f32[128,768]{1,0:T(8,128)S(1)}, bf16[128,768]{1,0:T(8,128)(2,1)S(1)}) custom-call(bf16[128,768]{1,0:T(8,128)(2,1)S(1)} %multiply_convert_fusion.xa_ref.refs_0_, bf16[128,768]{1,0:T(8,128)(2,1)S(1)} %collective-permute-done.31.xb_ref.refs_1_, ...), custom_call_target="tpu_custom_call" | custom-call | bytes 20295000 | tf_op jit(solution)/shard_map/pallas_call | solution.py:927
  144.8 4.2 %shard_map.213 = (f32[4,128,768]{2,1,0:T(8,128)S(1)}, bf16[4,128,768]{2,1,0:T(8,128)(2,1)S(1)}) custom-call(bf16[768,768]{1,0:T(8,128)(2,1)S(1)} %pad_maximum_fusion.w2a_ref, bf16[768,768]{1,0:T(8,128)(2,1)S(1)} %collective-permute-done.15.w2b_ref, bf16[256,1536]{1,0:T(8,128)(2,1)S(1)} %get-tuple-element.130.refs_0_.refs_8_, ...), custom_call_target="tpu_custom_call" | custom-call | bytes 16236000 | tf_op jit(solution)/shard_map/pallas_call | solution.py:927
  150.5 3.7 %shard_map.214 = (f32[768,768]{1,0:T(8,128)S(1)}, bf16[768,768]{1,0:T(8,128)(2,1)S(1)}) custom-call(bf16[128,768]{1,0:T(8,128)(2,1)S(1)} %multiply_convert_fusion.xa_ref.refs_0_, bf16[128,768]{1,0:T(8,128)(2,1)S(1)} %collective-permute-done.31.xb_ref.refs_1_, bf16[128,768]{1,0:T(8,128)(2,1)S(1)} %collective-permute-done.18.xa_ref.refs_2_, ...), custom_call_target="tpu_custom_call" | custom-call | bytes 22140000 | tf_op jit(solution)/shard_map/pallas_call | solution.py:927
  156.9 5.3 %collective-permute-done.37.b1_ref = bf16[128,768]{1,0:T(8,128)(2,1)S(1)} collective-permute-done((bf16[128,768]{1,0:T(8,128)(2,1)S(1)}, bf16[128,768]{1,0:T(8,128)(2,1)S(1)}, u32[]{:S(2)}, u32[]{:S(2)}) %collective-permute-start.37) | collective-permute-done | bytes 196640 | tf_op jit(solution)/shard_map/ppermute | solution.py:389
  174.1 14.0 %shard_map.215 = (f32[520,576]{1,0:T(8,128)}, bf16[520,576]{1,0:T(8,128)(2,1)}, f32[256,768]{1,0:T(8,128)}, bf16[256,768]{1,0:T(8,128)(2,1)}) custom-call(s32[1]{0:T(128)} %bitcast.9.me_ref, s32[1]{0:T(128)} %bitcast.10.place_ref, f32[3,32]{1,0:T(4,128)} %fusion.5.tab_ref, bf16[128,768]{1,0:T(8,128)(2,1)} %copy-done.38, bf16[128,768]{1,0:T(8,128)(2,1)} %copy-done.47, ...), custom_call_target="tpu_custom_call" | custom-call | bytes 36900000 | tf_op jit(solution)/shard_map/pallas_call | solution.py:927
  193.1 6.5 %shard_map.216 = (f32[768,768]{1,0:T(8,128)S(1)}, bf16[768,768]{1,0:T(8,128)(2,1)}) custom-call(bf16[128,896]{1,0:T(8,128)(2,1)S(1)} %maximum_maximum_fusion.ga_ref.refs_0_, bf16[128,896]{1,0:T(8,128)(2,1)S(1)} %copy-done.10, bf16[128,896]{1,0:T(8,128)(2,1)S(1)} %collective-permute-done.9.ga_ref.refs_2_, bf16[128,896]{1,0:T(8,128)(2,1)S(1)} %copy-done.12, ...), custom_call_target="tpu_custom_call" | custom-call | bytes 23985000 | tf_op jit(solution)/shard_map/pallas_call | solution.py:927
  203.8 3.4 %all-to-all-start.2 = ((bf16[32,24,384]{2,1,0:T(8,128)(2,1)}), bf16[32,24,384]{2,1,0:T(8,128)(2,1)S(1)}, u32[]{:S(2)}, u32[]{:S(2)}) async-start(bf16[32,24,384]{2,1,0:T(8,128)(2,1)} %bitcast.23), calls=%async_computation.2 | async-start | bytes 1179648 | tf_op jit(solution)/shard_map/all_to_all | solution.py:1204
  227.8 8.7 %collective-permute-done.49 = bf16[384,768]{1,0:T(8,128)(2,1)} collective-permute-done((bf16[384,768]{1,0:T(8,128)(2,1)}, bf16[384,768]{1,0:T(8,128)(2,1)}, u32[]{:S(2)}, u32[]{:S(2)}) %collective-permute-start.49) | collective-permute-done | bytes 589856 | tf_op jit(solution)/shard_map/ppermute | solution.py:389
  (292 shorter events, 114.0 us)
Async XLA Ops:
  2.5 29.9 %collective-permute-start.4 = (bf16[128,896]{1,0:T(8,128)(2,1)S(1)}, bf16[128,896]{1,0:T(8,128)(2,1)S(1)}, u32[]{:S(2)}, u32[]{:S(2)}) collective-permute-start(bf16[128,896]{1,0:T(8,128)(2,1)S(1)} %fusion.3.x0_ref), channel_id=1, source_target_pairs={{0,2},{2,0},{1,3},{3,1},{4,6},{6,4},{5,7},{7,5},{8,10},{10,8},{9,1... | collective-permute-start | bytes 688136 | tf_op jit(solution)/shard_map/ppermute | solution.py:389
  5.5 31.1 %collective-permute-start.5 = (bf16[128,896]{1,0:T(8,128)(2,1)S(1)}, bf16[128,896]{1,0:T(8,128)(2,1)S(1)}, u32[]{:S(2)}, u32[]{:S(2)}) collective-permute-start(bf16[128,896]{1,0:T(8,128)(2,1)S(1)} %fusion.3.x0_ref), channel_id=1, source_target_pairs={{0,1},{1,0},{2,3},{3,2},{4,5},{5,4},{6,7},{7,6},{8,9},{9,8},{10,11... | collective-permute-start | bytes 688136 | tf_op jit(solution)/shard_map/ppermute | solution.py:389
  7.3 29.4 %all-to-all-start = ((bf16[16,24,576]{2,1,0:T(8,128)(2,1)}), bf16[16,24,576]{2,1,0:T(8,128)(2,1)S(1)}, u32[]{:S(2)}, u32[]{:S(2)}) async-start(bf16[16,24,576]{2,1,0:T(8,128)(2,1)} %shard_map.206), calls=%async_computation | async-start | bytes 983040 | tf_op jit(solution)/shard_map/all_to_all | solution.py:999
  13.1 23.6 %collective-permute-start.7 = (bf16[384,768]{1,0:T(8,128)(2,1)S(1)}, bf16[384,768]{1,0:T(8,128)(2,1)S(1)}, u32[]{:S(2)}, u32[]{:S(2)}) collective-permute-start(bf16[384,768]{1,0:T(8,128)(2,1)S(1)} %bitcast.56), channel_id=1, source_target_pairs={{0,2},{2,0},{1,3},{3,1},{4,6},{6,4},{5,7},{7,5},{8,10},{10,8},{9,1... | collective-permute-start | bytes 1769480 | tf_op jit(solution)/shard_map/ppermute | solution.py:389
  36.7 19.8 %collective-permute-start.8 = (bf16[16,24,576]{2,1,0:T(8,128)(2,1)S(1)}, bf16[16,24,576]{2,1,0:T(8,128)(2,1)S(1)}, u32[]{:S(2)}, u32[]{:S(2)}) collective-permute-start(bf16[16,24,576]{2,1,0:T(8,128)(2,1)S(1)} %all-to-all-done.refs_0_), channel_id=1, source_target_pairs={{0,4},{4,0},{1,5},{5,1},{2,6},{6,2},{3,7},{7,3},{8,12},{12,8},{9,1... | collective-permute-start | bytes 1327112 | tf_op jit(solution)/shard_map/ppermute | solution.py:389
  37.6 46.5 %all-to-all-start.1 = ((bf16[32,24,384]{2,1,0:T(8,128)(2,1)}), bf16[32,24,384]{2,1,0:T(8,128)(2,1)S(1)}, u32[]{:S(2)}, u32[]{:S(2)}) async-start(bf16[32,24,384]{2,1,0:T(8,128)(2,1)} %shard_map.205), calls=%async_computation.1 | async-start | bytes 1179648 | tf_op jit(solution)/shard_map/all_to_all | solution.py:1030
  42.8 23.9 %collective-permute-start.9 = (bf16[128,896]{1,0:T(8,128)(2,1)S(1)}, bf16[128,896]{1,0:T(8,128)(2,1)S(1)}, u32[]{:S(2)}, u32[]{:S(2)}) collective-permute-start(bf16[128,896]{1,0:T(8,128)(2,1)S(1)} %maximum_maximum_fusion.ga_ref.refs_0_), channel_id=1, source_target_pairs={{0,8},{8,0},{16,24},{24,16},{1,9},{9,1},{17,25},{25,17},{2,10},{10... | collective-permute-start | bytes 688136 | tf_op jit(solution)/shard_map/ppermute | solution.py:389
  44.6 29.7 %collective-permute-start.10 = (bf16[128,896]{1,0:T(8,128)(2,1)S(1)}, bf16[128,896]{1,0:T(8,128)(2,1)S(1)}, u32[]{:S(2)}, u32[]{:S(2)}) collective-permute-start(bf16[128,896]{1,0:T(8,128)(2,1)S(1)} %maximum_maximum_fusion.ga_ref.refs_0_), channel_id=1, source_target_pairs={{0,16},{8,24},{16,0},{24,8},{1,17},{9,25},{17,1},{25,9},{2,18},{10... | collective-permute-start | bytes 688136 | tf_op jit(solution)/shard_map/ppermute | solution.py:389
  47.1 27.3 %collective-permute-start.11 = (bf16[128,896]{1,0:T(8,128)(2,1)S(1)}, bf16[128,896]{1,0:T(8,128)(2,1)S(1)}, u32[]{:S(2)}, u32[]{:S(2)}) collective-permute-start(bf16[128,896]{1,0:T(8,128)(2,1)S(1)} %maximum_maximum_fusion.ga_ref.refs_0_), channel_id=1, source_target_pairs={{0,24},{8,16},{16,8},{24,0},{1,25},{9,17},{17,9},{25,1},{2,26},{10... | collective-permute-start | bytes 688136 | tf_op jit(solution)/shard_map/ppermute | solution.py:389
  82.6 16.0 %collective-permute-start.22 = (bf16[128,896]{1,0:T(8,128)(2,1)S(1)}, bf16[128,896]{1,0:T(8,128)(2,1)S(1)}, u32[]{:S(2)}, u32[]{:S(2)}) collective-permute-start(bf16[128,896]{1,0:T(8,128)(2,1)S(1)} %collective-permute-done.11.ga_ref.refs_6_), channel_id=1, source_target_pairs={{0,4},{4,0},{1,5},{5,1},{2,6},{6,2},{3,7},{7,3},{8,12},{12,8},{9,1... | collective-permute-start | bytes 688136 | tf_op jit(solution)/shard_map/ppermute | solution.py:389
  85.5 21.9 %collective-permute-start.24 = (bf16[768,384]{1,0:T(8,128)(2,1)S(1)}, bf16[768,384]{1,0:T(8,128)(2,1)S(1)}, u32[]{:S(2)}, u32[]{:S(2)}) collective-permute-start(bf16[768,384]{1,0:T(8,128)(2,1)S(1)} %bitcast.51), channel_id=1, source_target_pairs={{0,2},{2,0},{1,3},{3,1},{4,6},{6,4},{5,7},{7,5},{8,10},{10,8},{9,1... | collective-permute-start | bytes 1769480 | tf_op jit(solution)/shard_map/ppermute | solution.py:389
  115.8 22.2 %collective-permute-start.31 = (bf16[128,768]{1,0:T(8,128)(2,1)S(1)}, bf16[128,768]{1,0:T(8,128)(2,1)S(1)}, u32[]{:S(2)}, u32[]{:S(2)}) collective-permute-start(bf16[128,768]{1,0:T(8,128)(2,1)S(1)} %multiply_convert_fusion.xa_ref.refs_0_), channel_id=1, source_target_pairs={{0,4},{4,0},{1,5},{5,1},{2,6},{6,2},{3,7},{7,3},{8,12},{12,8},{9,1... | collective-permute-start | bytes 589832 | tf_op jit(solution)/shard_map/ppermute | solution.py:389
  135.6 18.8 %collective-permute-start.35 = (bf16[128,768]{1,0:T(8,128)(2,1)S(1)}, bf16[128,768]{1,0:T(8,128)(2,1)S(1)}, u32[]{:S(2)}, u32[]{:S(2)}) collective-permute-start(bf16[128,768]{1,0:T(8,128)(2,1)S(1)} %convert_add_fusion.8), channel_id=1, source_target_pairs={{0,16},{8,24},{16,0},{24,8},{1,17},{9,25},{17,1},{25,9},{2,18},{10... | collective-permute-start | bytes 589832 | tf_op jit(solution)/shard_map/ppermute | solution.py:389
  148.9 17.3 %collective-permute-start.33 = (bf16[4,128,768]{2,1,0:T(8,128)(2,1)S(1)}, bf16[4,128,768]{2,1,0:T(8,128)(2,1)S(1)}, u32[]{:S(2)}, u32[]{:S(2)}) collective-permute-start(bf16[4,128,768]{2,1,0:T(8,128)(2,1)S(1)} %get-tuple-element.107), channel_id=1, source_target_pairs={{0,4},{4,0},{1,5},{5,1},{2,6},{6,2},{3,7},{7,3},{8,12},{12,8},{9,1... | collective-permute-start | bytes 2359304 | tf_op jit(solution)/shard_map/ppermute | solution.py:389
  163.9 24.3 %collective-permute-start.41 = (bf16[768,384]{1,0:T(8,128)(2,1)}, bf16[768,384]{1,0:T(8,128)(2,1)}, u32[]{:S(2)}, u32[]{:S(2)}) collective-permute-start(bf16[768,384]{1,0:T(8,128)(2,1)} %slice.91), channel_id=1, source_target_pairs={{0,2},{2,0},{1,3},{3,1},{4,6},{6,4},{5,7},{7,5},{8,10},{10,8},{9,1... | collective-permute-start | bytes 1769480 | tf_op jit(solution)/shard_map/ppermute | solution.py:389
  168.5 19.7 %collective-permute-start.42 = (bf16[128,768]{1,0:T(8,128)(2,1)}, bf16[128,768]{1,0:T(8,128)(2,1)}, u32[]{:S(2)}, u32[]{:S(2)}) collective-permute-start(bf16[128,768]{1,0:T(8,128)(2,1)} %get-tuple-element.162), channel_id=1, source_target_pairs={{0,8},{8,0},{16,24},{24,16},{1,9},{9,1},{17,25},{25,17},{2,10},{10... | collective-permute-start | bytes 589832 | tf_op jit(solution)/shard_map/ppermute | solution.py:389
  168.5 19.7 %collective-permute-start.43 = (bf16[128,768]{1,0:T(8,128)(2,1)}, bf16[128,768]{1,0:T(8,128)(2,1)}, u32[]{:S(2)}, u32[]{:S(2)}) collective-permute-start(bf16[128,768]{1,0:T(8,128)(2,1)} %get-tuple-element.164), channel_id=1, source_target_pairs={{0,16},{8,24},{16,0},{24,8},{1,17},{9,25},{17,1},{25,9},{2,18},{10... | collective-permute-start | bytes 589832 | tf_op jit(solution)/shard_map/ppermute | solution.py:389
  170.5 17.7 %collective-permute-start.44 = (bf16[128,768]{1,0:T(8,128)(2,1)}, bf16[128,768]{1,0:T(8,128)(2,1)}, u32[]{:S(2)}, u32[]{:S(2)}) collective-permute-start(bf16[128,768]{1,0:T(8,128)(2,1)} %get-tuple-element.163), channel_id=1, source_target_pairs={{0,24},{8,16},{16,8},{24,0},{1,25},{9,17},{17,9},{25,1},{2,26},{10... | collective-permute-start | bytes 589832 | tf_op jit(solution)/shard_map/ppermute | solution.py:389
  188.2 19.1 %collective-permute-start.45 = (bf16[520,576]{1,0:T(8,128)(2,1)}, bf16[520,576]{1,0:T(8,128)(2,1)}, u32[]{:S(2)}, u32[]{:S(2)}) collective-permute-start(bf16[520,576]{1,0:T(8,128)(2,1)} %get-tuple-element.126), channel_id=1, source_target_pairs={{0,4},{4,0},{1,5},{5,1},{2,6},{6,2},{3,7},{7,3},{8,12},{12,8},{9,1... | collective-permute-start | bytes 1797128 | tf_op jit(solution)/shard_map/ppermute | solution.py:389
  199.6 17.9 %collective-permute-start.48 = (bf16[768,768]{1,0:T(8,128)(2,1)}, bf16[768,768]{1,0:T(8,128)(2,1)}, u32[]{:S(2)}, u32[]{:S(2)}) collective-permute-start(bf16[768,768]{1,0:T(8,128)(2,1)} %get-tuple-element.131), channel_id=1, source_target_pairs={{0,1},{1,0},{2,3},{3,2},{4,5},{5,4},{6,7},{7,6},{8,9},{9,8},{10,11... | collective-permute-start | bytes 3538952 | tf_op jit(solution)/shard_map/ppermute | solution.py:389
  203.8 20.0 %all-to-all-start.2 = ((bf16[32,24,384]{2,1,0:T(8,128)(2,1)}), bf16[32,24,384]{2,1,0:T(8,128)(2,1)S(1)}, u32[]{:S(2)}, u32[]{:S(2)}) async-start(bf16[32,24,384]{2,1,0:T(8,128)(2,1)} %bitcast.23), calls=%async_computation.2 | async-start | bytes 1179648 | tf_op jit(solution)/shard_map/all_to_all | solution.py:1204
  210.6 25.8 %collective-permute-start.50 = (bf16[136,576]{1,0:T(8,128)(2,1)S(1)}, bf16[136,576]{1,0:T(8,128)(2,1)S(1)}, u32[]{:S(2)}, u32[]{:S(2)}) collective-permute-start(bf16[136,576]{1,0:T(8,128)(2,1)S(1)} %get-tuple-element.139), channel_id=1, source_target_pairs={{0,8},{8,0},{16,24},{24,16},{1,9},{9,1},{17,25},{25,17},{2,10},{10... | collective-permute-start | bytes 470024 | tf_op jit(solution)/shard_map/ppermute | solution.py:389
  212.3 24.2 %collective-permute-start.51 = (bf16[136,576]{1,0:T(8,128)(2,1)S(1)}, bf16[136,576]{1,0:T(8,128)(2,1)S(1)}, u32[]{:S(2)}, u32[]{:S(2)}) collective-permute-start(bf16[136,576]{1,0:T(8,128)(2,1)S(1)} %get-tuple-element.140), channel_id=1, source_target_pairs={{0,16},{8,24},{16,0},{24,8},{1,17},{9,25},{17,1},{25,9},{2,18},{10... | collective-permute-start | bytes 470024 | tf_op jit(solution)/shard_map/ppermute | solution.py:389
  214.7 21.7 %collective-permute-start.52 = (bf16[136,576]{1,0:T(8,128)(2,1)S(1)}, bf16[136,576]{1,0:T(8,128)(2,1)S(1)}, u32[]{:S(2)}, u32[]{:S(2)}) collective-permute-start(bf16[136,576]{1,0:T(8,128)(2,1)S(1)} %get-tuple-element.141), channel_id=1, source_target_pairs={{0,24},{8,16},{16,8},{24,0},{1,25},{9,17},{17,9},{25,1},{2,26},{10... | collective-permute-start | bytes 470024 | tf_op jit(solution)/shard_map/ppermute | solution.py:389
  (98 other events, 991.7 us)
